TPU v7x, 32 devices: a whole 2x2x4 slice. The times are simulated.
32 devices in a mesh: group: 2 (over y), dev: 16 (over z, x, core).
Axes of the slice: x: 2, y: 2, z: 4, core: 2. Of those that a mesh axis runs over, the one named last changes fastest.
Arguments:
- mantissa: bfloat16 [64, 32, 896], P(None, ('group', 'dev')), may hold values from 0.5 to 1
- exponent: int32 [64, 32, 7], P(None, ('group', 'dev')), may hold values from 1 to 4
- poly_square: float32 [896], replicated, may hold values from 0.02 to 0.2
- poly_cube: float32 [896], replicated, may hold values from 0.005 to 0.05
- col_map: bfloat16 [896, 896], replicated, may hold values from -0.1875 to 0.1875
- rebin_offset: int32 [32, 7], P('group'), may hold values from -8 to 7
- rebin_weight: float32 [32, 7], P('group'), may hold values from 0 to 1
- kern_first: bfloat16 [32, 3, 3], replicated, may hold values from -2 to 2
- kern_second: bfloat16 [32, 32, 3, 3], replicated, may hold values from -0.375 to 0.375
- kern_last: bfloat16 [32], replicated, may hold values from -1 to 1
Outputs:
- dual: bfloat16 [64, 32, 896], P('dev', 'group')
Inputs may be any that keep to these rules, and one draw needn't show every extreme that they name: `rebin_offset`: interpolation sources of rebinned view v lie in views v - 8 to v + 8.
All inputs are finite; a program needn't handle non-finite values.
Results may differ from a plain program's by a relative error of at most 0.0065.
Values may be sent and summed in bfloat16 or wider, within the bound.
No kernel may reach another device: no remote copies, remote signals or barrier semaphores. Data moves between devices by JAX's collectives and lax.ppermute only.
A program may use at most 64 MiB of HBM per device.

v0:
```python
import jax
import jax.numpy as jnp
from jax import lax
from jax.sharding import PartitionSpec as P

REACH = 8


def padded_2(block, sides, width):
    for axis, dim in sides:
        count = lax.axis_size(axis)
        forward = [(i, i + 1) for i in range(count - 1)]
        backward = [(target, source) for source, target in forward]
        low = lax.ppermute(
            lax.slice_in_dim(block, block.shape[dim] - width, None, axis=dim), axis, forward
        )
        high = lax.ppermute(lax.slice_in_dim(block, 0, width, axis=dim), axis, backward)
        block = jnp.concatenate([low, block, high], axis=dim)
    return block


def prepare(mantissa, exponent, poly_square, poly_cube):
    lead_rows, lead_views, width_all = mantissa.shape
    block_count = exponent.shape[2]
    counts = mantissa.astype(jnp.float32).reshape(
        lead_rows, lead_views, block_count, width_all // block_count
    )
    counts = counts * jnp.exp2(-exponent.astype(jnp.float32))[..., None]
    line_int = -jnp.log(counts).reshape(lead_rows, lead_views, width_all)
    hardened = (
        line_int + poly_square * line_int * line_int + poly_cube * line_int * line_int * line_int
    )
    return hardened.astype(jnp.bfloat16)


def resample(hardened, col_map):
    shape_in = hardened.shape
    flat = hardened.reshape(-1, shape_in[2])
    product = jnp.dot(flat, col_map, preferred_element_type=jnp.float32)
    return product.astype(jnp.bfloat16).reshape(shape_in)


def first_layer(
    piece, kern_first, view_count, col_count, view_start, col_start, total_views, width_all
):
    weights = kern_first.astype(jnp.float32)
    summed = jnp.zeros((piece.shape[0], weights.shape[0], view_count, col_count), jnp.float32)
    for offset_view in range(3):
        for offset_col in range(3):
            window = piece[
                :, offset_view : offset_view + view_count, offset_col : offset_col + col_count
            ].astype(jnp.float32)
            summed = (
                summed + weights[:, offset_view, offset_col][None, :, None, None] * window[:, None]
            )
    view_pos = view_start + jnp.arange(view_count, dtype=jnp.int32)
    col_pos = col_start + jnp.arange(col_count, dtype=jnp.int32)
    valid = ((view_pos >= 0) & (view_pos < total_views))[:, None] & (
        (col_pos >= 0) & (col_pos < width_all)
    )[None, :]
    return jnp.where(valid[None, None], jnp.maximum(summed, 0.0), 0.0).astype(jnp.bfloat16)


def second_layer(hidden, signal, kern_second, kern_last):
    view_count, col_count = (signal.shape[1], signal.shape[2])
    summed = jnp.zeros((signal.shape[0], kern_second.shape[0], view_count, col_count), jnp.float32)
    for offset_view in range(3):
        for offset_col in range(3):
            window = hidden[
                :, :, offset_view : offset_view + view_count, offset_col : offset_col + col_count
            ]
            summed = summed + jnp.einsum(
                "oi,rivc->rovc",
                kern_second[:, :, offset_view, offset_col],
                window,
                preferred_element_type=jnp.float32,
            )
    second = jnp.maximum(summed, 0.0).astype(jnp.bfloat16)
    mixed = signal.astype(jnp.float32) + jnp.einsum(
        "i,rivc->rvc", kern_last, second, preferred_element_type=jnp.float32
    )
    return mixed.astype(jnp.bfloat16)


def local(
    mantissa,
    exponent,
    poly_square,
    poly_cube,
    col_map,
    rebin_offset,
    rebin_weight,
    kern_first,
    kern_second,
    kern_last,
):
    width_all = mantissa.shape[2]
    block_count = exponent.shape[2]
    col_block = width_all // block_count
    projected = resample(prepare(mantissa, exponent, poly_square, poly_cube), col_map)
    row_major = lax.all_to_all(projected, "dev", split_axis=0, concat_axis=1, tiled=True)
    row_count, view_count = (row_major.shape[0], row_major.shape[1])
    group_idx = lax.axis_index("group")
    total_views = view_count * lax.axis_size("group")
    extended = padded_2(row_major, (("group", 1),), REACH)
    extended = extended.reshape(row_count, view_count + 2 * REACH, block_count, col_block)
    lower_idx = jnp.arange(view_count, dtype=jnp.int32)[:, None] + rebin_offset + REACH
    block_ids = jnp.arange(block_count, dtype=jnp.int32)[None, :]
    lower = extended[:, lower_idx, block_ids, :].astype(jnp.float32)
    upper = extended[:, lower_idx + 1, block_ids, :].astype(jnp.float32)
    frac = rebin_weight[None, :, :, None]
    signal = (
        ((1.0 - frac) * lower + frac * upper)
        .astype(jnp.bfloat16)
        .reshape(row_count, view_count, width_all)
    )
    rimmed = padded_2(signal, (("group", 1),), 1)
    padded = jnp.pad(rimmed, ((0, 0), (0, 0), (2, 2)))
    head = first_layer(
        padded[:, 0:3, :],
        kern_first,
        1,
        width_all + 2,
        group_idx * view_count,
        -1,
        total_views,
        width_all,
    )
    tail = first_layer(
        padded[:, view_count - 1 : view_count + 2, :],
        kern_first,
        1,
        width_all + 2,
        group_idx * view_count + view_count - 1,
        -1,
        total_views,
        width_all,
    )
    edges = padded_2(jnp.concatenate([head, tail], axis=2), (("group", 2),), 1)
    before_row = edges[:, :, 0:1]
    after_row = edges[:, :, 3:4]

    def one_block(block_idx):
        start = block_idx * col_block
        piece = lax.dynamic_slice_in_dim(padded, start, col_block + 4, axis=2)
        own_part = first_layer(
            piece,
            kern_first,
            view_count,
            col_block + 2,
            group_idx * view_count,
            start - 1,
            total_views,
            width_all,
        )
        prior = lax.dynamic_slice_in_dim(before_row, start, col_block + 2, axis=3)
        later = lax.dynamic_slice_in_dim(after_row, start, col_block + 2, axis=3)
        hidden = jnp.concatenate([prior, own_part, later], axis=2)
        return second_layer(
            hidden, piece[:, 1 : 1 + view_count, 2 : 2 + col_block], kern_second, kern_last
        )

    blocks_out = lax.map(one_block, jnp.arange(block_count, dtype=jnp.int32))
    return jnp.transpose(blocks_out, (1, 2, 0, 3)).reshape(row_count, view_count, width_all)


def solution(mesh):
    return jax.shard_map(
        local,
        mesh=mesh,
        in_specs=(
            P(None, ("group", "dev"), None),
            P(None, ("group", "dev"), None),
            P(),
            P(),
            P(),
            P("group", None),
            P("group", None),
            P(),
            P(),
            P(),
        ),
        out_specs=P("dev", "group", None),
        check_vma=False,
    )
```

profile of v0, /device:TPU:0, one launch (start us, length us, event | category | flops | bytes accessed | tf_op | source)
XLA Modules:
  0.0 129.6 jit_solution(3739840458730424565)
XLA Ops:
  0.0 0.8 multiply_exponential_fusion
  1.4 1.3 fusion.41
  3.9 0.7 reshape.486
  4.7 7.4 %all-to-all-start = ((bf16[16,2,1792]{2,1,0:T(2,128)(2,1)}), bf16[16,2,1792]{2,1,0:T(2,128)(2,1)S(1)}, u32[]{:S(2)}, u32[]{:S(2)}) async-start(bf16[16,2,1792]{2,1,0:T(2,128)(2,1)} %reshape.486), calls=%async_computation | async-start | bytes 229376 | tf_op jit(solution)/shard_map/all_to_all | solution.py:101
  12.8 6.9 %all-to-all-done = bf16[16,2,1792]{2,1,0:T(2,128)(2,1)S(1)} async-done(((bf16[16,2,1792]{2,1,0:T(2,128)(2,1)}), bf16[16,2,1792]{2,1,0:T(2,128)(2,1)S(1)}, u32[]{:S(2)}, u32[]{:S(2)}) %all-to-all-start) | async-done | bytes 114720 | tf_op jit(solution)/shard_map/all_to_all | solution.py:101
  20.5 3.4 %collective-permute-start = (bf16[4,8,896]{2,0,1:T(4,128)(2,1)S(1)}, bf16[4,8,896]{2,0,1:T(4,128)(2,1)S(1)}, u32[]{:S(2)}, u32[]{:S(2)}) collective-permute-start(bf16[4,8,896]{2,0,1:T(4,128)(2,1)S(1)} %get-tuple-element.193), channel_id=1, source_target_pairs={{0,16},{1,17},{2,18},{3,19},{4,20},{5,21},{6,22},{7,23},{8,24},{9,... | collective-permute-start | bytes 172040 | tf_op jit(solution)/shard_map/ppermute | solution.py:14
  24.0 1.3 collective-permute-start.1
  25.8 4.2 %collective-permute-done.1 = bf16[4,8,896]{2,0,1:T(4,128)(2,1)S(1)} collective-permute-done((bf16[4,8,896]{2,0,1:T(4,128)(2,1)S(1)}, bf16[4,8,896]{2,0,1:T(4,128)(2,1)S(1)}, u32[]{:S(2)}, u32[]{:S(2)}) %collective-permute-start.1) | collective-permute-done | bytes 57376 | tf_op jit(solution)/shard_map/ppermute | solution.py:17
  30.3 1.2 gather_fusion
  31.6 1.2 gather_fusion.1
  33.0 1.6 %collective-permute-start.2 = (bf16[4,1,896]{2,1,0:T(2,128)(2,1)S(1)}, bf16[4,1,896]{2,1,0:T(2,128)(2,1)S(1)}, u32[]{:S(2)}, u32[]{:S(2)}) collective-permute-start(bf16[4,1,896]{2,1,0:T(2,128)(2,1)S(1)} %get-tuple-element.191), channel_id=1, source_target_pairs={{0,16},{1,17},{2,18},{3,19},{4,20},{5,21},{6,22},{7,23},{8,24},{9,... | collective-permute-start | bytes 21512 | tf_op jit(solution)/shard_map/ppermute | solution.py:14
  34.6 1.3 collective-permute-start.3
  36.0 4.2 %collective-permute-done.3 = bf16[4,1,896]{2,1,0:T(2,128)(2,1)S(1)} collective-permute-done((bf16[4,1,896]{2,1,0:T(2,128)(2,1)S(1)}, bf16[4,1,896]{2,1,0:T(2,128)(2,1)S(1)}, u32[]{:S(2)}, u32[]{:S(2)}) %collective-permute-start.3) | collective-permute-done | bytes 7200 | tf_op jit(solution)/shard_map/ppermute | solution.py:17
  41.2 1.3 collective-permute-start.5
  43.1 5.9 %collective-permute-start.4 = (bf16[4,32,1,898]{3,1,2,0:T(8,128)(2,1)S(1)}, bf16[4,32,1,898]{3,1,2,0:T(8,128)(2,1)}, u32[]{:S(2)}, u32[]{:S(2)}) collective-permute-start(bf16[4,32,1,898]{3,1,2,0:T(8,128)(2,1)S(1)} %select_convert_fusion.2), channel_id=1, source_target_pairs={{0,16},{1,17},{2,18},{3,19},{4,20},{5,21},{6,22},{7,23},{8,24},{9,... | collective-permute-start | bytes 689672 | tf_op jit(solution)/shard_map/ppermute | solution.py:14
  49.6 2.6 %collective-permute-done.4 = bf16[4,32,1,898]{3,1,2,0:T(8,128)(2,1)} collective-permute-done((bf16[4,32,1,898]{3,1,2,0:T(8,128)(2,1)S(1)}, bf16[4,32,1,898]{3,1,2,0:T(8,128)(2,1)}, u32[]{:S(2)}, u32[]{:S(2)}) %collective-permute-start.4) | collective-permute-done | bytes 229920 | tf_op jit(solution)/shard_map/ppermute | solution.py:14
  52.2 75.8 %while.12 = (s32[]{:T(128)}, bf16[7,4,16,128]{3,2,1,0:T(8,128)(2,1)}, s32[7]{0:T(128)S(1)}, bf16[4,18,900]{2,1,0:T(8,128)(2,1)S(1)}, bf16[4,32,1,898]{3,1,2,0:T(...) while((s32[]{:T(128)}, ...), condition=%wide.region_1.2_spmd, body=%wide.region_0.1_spmd.sunk | while | flops 165859344 | bytes 26632192 | solution.py:163
  53.9 1.9 %select_convert_fusion.4 = bf16[4,32,16,130]{3,1,2,0:T(8,128)(2,1)S(1)} fusion(f32[4,16,130]{2,1,0:T(8,128)S(1)} %get-tuple-element.289, f32[32]{0:T(128)S(1)} %get-tuple-element.290, f32[4,16,130]{2,1,0:T(8,128)S(1)} %get-tuple-element.291, f32[32]{0:T(128)S(1)} %get-tuple-element.292, f32[4,16,130]{2,1,0:T(8,128)S(1)} %get-tuple-element.293, ...), kind=kLoop, calls=%fused_computation.2.clone.1 | loop fusion | flops 5324800 | bytes 835232 | tf_op jit(solution)/shard_map/while/body/eval_jaxpr/convert_element_type | solution.py:61
  55.8 1.1 constant_dynamic-slice_fusion.3
  59.3 1.4 %convolution_add_fusion.21 = f32[4,16,128,32]{2,3,1,0:T(8,128)} fusion(f32[4,16,128,32]{2,3,1,0:T(8,128)S(1)} %convolution_add_fusion.20, bf16[4,32,16,130]{3,1,2,0:T(8,128)(2,1)S(1)} %select_convert_fusion.4, bf16[4,32,1,130]{3,1,2,0:T(8,128)(2,1)S(1)} %get-tuple-element.308, bf16[32,32,3,3]{1,0,3,2:T(8,128)(2,1)S(1)} %get-tuple-element.352), kind=kOutput, calls=%fused_computation.9.clone.1 | convolution fusion | flops 18087936 | bytes 3219456 | tf_op jit(solution)/shard_map/while/body/eval_jaxpr/oi,rivc->rovc/dot_general | solution.py:72
  60.6 1.7 %fusion.108 = f32[1,4,16,128]{3,0,2,1:T(1,128)S(1)} fusion(f32[4,16,128,32]{2,3,1,0:T(8,128)} %convolution_add_fusion.21, bf16[4,32,1,130]{3,1,2,0:T(8,128)(2,1)S(1)} %get-tuple-element.308, bf16[4,32,16,130]{3,1,2,0:T(8,128)(2,1)S(1)} %select_convert_fusion.4, bf16[32,32,3,3]{1,0,3,2:T(8,128)(2,1)S(1)} %get-tuple-element.352, ...), kind=kOutput, calls=%fused_computation.18.clone.1 | convolution fusion | flops 19136512 | bytes 2204160 | tf_op jit(solution)/shard_map/while/body/eval_jaxpr/i,rivc->rvc/dot_general | solution.py:79
  64.8 1.9 %select_convert_fusion.4 = bf16[4,32,16,130]{3,1,2,0:T(8,128)(2,1)S(1)} fusion(f32[4,16,130]{2,1,0:T(8,128)S(1)} %get-tuple-element.289, f32[32]{0:T(128)S(1)} %get-tuple-element.290, f32[4,16,130]{2,1,0:T(8,128)S(1)} %get-tuple-element.291, f32[32]{0:T(128)S(1)} %get-tuple-element.292, f32[4,16,130]{2,1,0:T(8,128)S(1)} %get-tuple-element.293, ...), kind=kLoop, calls=%fused_computation.2.clone.1 | loop fusion | flops 5324800 | bytes 835232 | tf_op jit(solution)/shard_map/while/body/eval_jaxpr/convert_element_type | solution.py:61
  66.7 1.1 constant_dynamic-slice_fusion.3
  70.1 1.4 %convolution_add_fusion.21 = f32[4,16,128,32]{2,3,1,0:T(8,128)} fusion(f32[4,16,128,32]{2,3,1,0:T(8,128)S(1)} %convolution_add_fusion.20, bf16[4,32,16,130]{3,1,2,0:T(8,128)(2,1)S(1)} %select_convert_fusion.4, bf16[4,32,1,130]{3,1,2,0:T(8,128)(2,1)S(1)} %get-tuple-element.308, bf16[32,32,3,3]{1,0,3,2:T(8,128)(2,1)S(1)} %get-tuple-element.352), kind=kOutput, calls=%fused_computation.9.clone.1 | convolution fusion | flops 18087936 | bytes 3219456 | tf_op jit(solution)/shard_map/while/body/eval_jaxpr/oi,rivc->rovc/dot_general | solution.py:72
  71.5 1.7 %fusion.108 = f32[1,4,16,128]{3,0,2,1:T(1,128)S(1)} fusion(f32[4,16,128,32]{2,3,1,0:T(8,128)} %convolution_add_fusion.21, bf16[4,32,1,130]{3,1,2,0:T(8,128)(2,1)S(1)} %get-tuple-element.308, bf16[4,32,16,130]{3,1,2,0:T(8,128)(2,1)S(1)} %select_convert_fusion.4, bf16[32,32,3,3]{1,0,3,2:T(8,128)(2,1)S(1)} %get-tuple-element.352, ...), kind=kOutput, calls=%fused_computation.18.clone.1 | convolution fusion | flops 19136512 | bytes 2204160 | tf_op jit(solution)/shard_map/while/body/eval_jaxpr/i,rivc->rvc/dot_general | solution.py:79
  75.6 1.9 %select_convert_fusion.4 = bf16[4,32,16,130]{3,1,2,0:T(8,128)(2,1)S(1)} fusion(f32[4,16,130]{2,1,0:T(8,128)S(1)} %get-tuple-element.289, f32[32]{0:T(128)S(1)} %get-tuple-element.290, f32[4,16,130]{2,1,0:T(8,128)S(1)} %get-tuple-element.291, f32[32]{0:T(128)S(1)} %get-tuple-element.292, f32[4,16,130]{2,1,0:T(8,128)S(1)} %get-tuple-element.293, ...), kind=kLoop, calls=%fused_computation.2.clone.1 | loop fusion | flops 5324800 | bytes 835232 | tf_op jit(solution)/shard_map/while/body/eval_jaxpr/convert_element_type | solution.py:61
  77.5 1.1 constant_dynamic-slice_fusion.3
  80.9 1.4 %convolution_add_fusion.21 = f32[4,16,128,32]{2,3,1,0:T(8,128)} fusion(f32[4,16,128,32]{2,3,1,0:T(8,128)S(1)} %convolution_add_fusion.20, bf16[4,32,16,130]{3,1,2,0:T(8,128)(2,1)S(1)} %select_convert_fusion.4, bf16[4,32,1,130]{3,1,2,0:T(8,128)(2,1)S(1)} %get-tuple-element.308, bf16[32,32,3,3]{1,0,3,2:T(8,128)(2,1)S(1)} %get-tuple-element.352), kind=kOutput, calls=%fused_computation.9.clone.1 | convolution fusion | flops 18087936 | bytes 3219456 | tf_op jit(solution)/shard_map/while/body/eval_jaxpr/oi,rivc->rovc/dot_general | solution.py:72
  82.3 1.7 %fusion.108 = f32[1,4,16,128]{3,0,2,1:T(1,128)S(1)} fusion(f32[4,16,128,32]{2,3,1,0:T(8,128)} %convolution_add_fusion.21, bf16[4,32,1,130]{3,1,2,0:T(8,128)(2,1)S(1)} %get-tuple-element.308, bf16[4,32,16,130]{3,1,2,0:T(8,128)(2,1)S(1)} %select_convert_fusion.4, bf16[32,32,3,3]{1,0,3,2:T(8,128)(2,1)S(1)} %get-tuple-element.352, ...), kind=kOutput, calls=%fused_computation.18.clone.1 | convolution fusion | flops 19136512 | bytes 2204160 | tf_op jit(solution)/shard_map/while/body/eval_jaxpr/i,rivc->rvc/dot_general | solution.py:79
  86.5 1.9 %select_convert_fusion.4 = bf16[4,32,16,130]{3,1,2,0:T(8,128)(2,1)S(1)} fusion(f32[4,16,130]{2,1,0:T(8,128)S(1)} %get-tuple-element.289, f32[32]{0:T(128)S(1)} %get-tuple-element.290, f32[4,16,130]{2,1,0:T(8,128)S(1)} %get-tuple-element.291, f32[32]{0:T(128)S(1)} %get-tuple-element.292, f32[4,16,130]{2,1,0:T(8,128)S(1)} %get-tuple-element.293, ...), kind=kLoop, calls=%fused_computation.2.clone.1 | loop fusion | flops 5324800 | bytes 835232 | tf_op jit(solution)/shard_map/while/body/eval_jaxpr/convert_element_type | solution.py:61
  88.3 1.1 constant_dynamic-slice_fusion.3
  91.8 1.4 %convolution_add_fusion.21 = f32[4,16,128,32]{2,3,1,0:T(8,128)} fusion(f32[4,16,128,32]{2,3,1,0:T(8,128)S(1)} %convolution_add_fusion.20, bf16[4,32,16,130]{3,1,2,0:T(8,128)(2,1)S(1)} %select_convert_fusion.4, bf16[4,32,1,130]{3,1,2,0:T(8,128)(2,1)S(1)} %get-tuple-element.308, bf16[32,32,3,3]{1,0,3,2:T(8,128)(2,1)S(1)} %get-tuple-element.352), kind=kOutput, calls=%fused_computation.9.clone.1 | convolution fusion | flops 18087936 | bytes 3219456 | tf_op jit(solution)/shard_map/while/body/eval_jaxpr/oi,rivc->rovc/dot_general | solution.py:72
  93.1 1.7 %fusion.108 = f32[1,4,16,128]{3,0,2,1:T(1,128)S(1)} fusion(f32[4,16,128,32]{2,3,1,0:T(8,128)} %convolution_add_fusion.21, bf16[4,32,1,130]{3,1,2,0:T(8,128)(2,1)S(1)} %get-tuple-element.308, bf16[4,32,16,130]{3,1,2,0:T(8,128)(2,1)S(1)} %select_convert_fusion.4, bf16[32,32,3,3]{1,0,3,2:T(8,128)(2,1)S(1)} %get-tuple-element.352, ...), kind=kOutput, calls=%fused_computation.18.clone.1 | convolution fusion | flops 19136512 | bytes 2204160 | tf_op jit(solution)/shard_map/while/body/eval_jaxpr/i,rivc->rvc/dot_general | solution.py:79
  97.3 1.9 %select_convert_fusion.4 = bf16[4,32,16,130]{3,1,2,0:T(8,128)(2,1)S(1)} fusion(f32[4,16,130]{2,1,0:T(8,128)S(1)} %get-tuple-element.289, f32[32]{0:T(128)S(1)} %get-tuple-element.290, f32[4,16,130]{2,1,0:T(8,128)S(1)} %get-tuple-element.291, f32[32]{0:T(128)S(1)} %get-tuple-element.292, f32[4,16,130]{2,1,0:T(8,128)S(1)} %get-tuple-element.293, ...), kind=kLoop, calls=%fused_computation.2.clone.1 | loop fusion | flops 5324800 | bytes 835232 | tf_op jit(solution)/shard_map/while/body/eval_jaxpr/convert_element_type | solution.py:61
  99.2 1.1 constant_dynamic-slice_fusion.3
  102.6 1.4 %convolution_add_fusion.21 = f32[4,16,128,32]{2,3,1,0:T(8,128)} fusion(f32[4,16,128,32]{2,3,1,0:T(8,128)S(1)} %convolution_add_fusion.20, bf16[4,32,16,130]{3,1,2,0:T(8,128)(2,1)S(1)} %select_convert_fusion.4, bf16[4,32,1,130]{3,1,2,0:T(8,128)(2,1)S(1)} %get-tuple-element.308, bf16[32,32,3,3]{1,0,3,2:T(8,128)(2,1)S(1)} %get-tuple-element.352), kind=kOutput, calls=%fused_computation.9.clone.1 | convolution fusion | flops 18087936 | bytes 3219456 | tf_op jit(solution)/shard_map/while/body/eval_jaxpr/oi,rivc->rovc/dot_general | solution.py:72
  104.0 1.7 %fusion.108 = f32[1,4,16,128]{3,0,2,1:T(1,128)S(1)} fusion(f32[4,16,128,32]{2,3,1,0:T(8,128)} %convolution_add_fusion.21, bf16[4,32,1,130]{3,1,2,0:T(8,128)(2,1)S(1)} %get-tuple-element.308, bf16[4,32,16,130]{3,1,2,0:T(8,128)(2,1)S(1)} %select_convert_fusion.4, bf16[32,32,3,3]{1,0,3,2:T(8,128)(2,1)S(1)} %get-tuple-element.352, ...), kind=kOutput, calls=%fused_computation.18.clone.1 | convolution fusion | flops 19136512 | bytes 2204160 | tf_op jit(solution)/shard_map/while/body/eval_jaxpr/i,rivc->rvc/dot_general | solution.py:79
  105.7 0.7 fusion.109
  108.1 1.9 %select_convert_fusion.4 = bf16[4,32,16,130]{3,1,2,0:T(8,128)(2,1)S(1)} fusion(f32[4,16,130]{2,1,0:T(8,128)S(1)} %get-tuple-element.289, f32[32]{0:T(128)S(1)} %get-tuple-element.290, f32[4,16,130]{2,1,0:T(8,128)S(1)} %get-tuple-element.291, f32[32]{0:T(128)S(1)} %get-tuple-element.292, f32[4,16,130]{2,1,0:T(8,128)S(1)} %get-tuple-element.293, ...), kind=kLoop, calls=%fused_computation.2.clone.1 | loop fusion | flops 5324800 | bytes 835232 | tf_op jit(solution)/shard_map/while/body/eval_jaxpr/convert_element_type | solution.py:61
  110.0 1.1 constant_dynamic-slice_fusion.3
  113.4 1.4 %convolution_add_fusion.21 = f32[4,16,128,32]{2,3,1,0:T(8,128)} fusion(f32[4,16,128,32]{2,3,1,0:T(8,128)S(1)} %convolution_add_fusion.20, bf16[4,32,16,130]{3,1,2,0:T(8,128)(2,1)S(1)} %select_convert_fusion.4, bf16[4,32,1,130]{3,1,2,0:T(8,128)(2,1)S(1)} %get-tuple-element.308, bf16[32,32,3,3]{1,0,3,2:T(8,128)(2,1)S(1)} %get-tuple-element.352), kind=kOutput, calls=%fused_computation.9.clone.1 | convolution fusion | flops 18087936 | bytes 3219456 | tf_op jit(solution)/shard_map/while/body/eval_jaxpr/oi,rivc->rovc/dot_general | solution.py:72
  114.8 1.7 %fusion.108 = f32[1,4,16,128]{3,0,2,1:T(1,128)S(1)} fusion(f32[4,16,128,32]{2,3,1,0:T(8,128)} %convolution_add_fusion.21, bf16[4,32,1,130]{3,1,2,0:T(8,128)(2,1)S(1)} %get-tuple-element.308, bf16[4,32,16,130]{3,1,2,0:T(8,128)(2,1)S(1)} %select_convert_fusion.4, bf16[32,32,3,3]{1,0,3,2:T(8,128)(2,1)S(1)} %get-tuple-element.352, ...), kind=kOutput, calls=%fused_computation.18.clone.1 | convolution fusion | flops 19136512 | bytes 2204160 | tf_op jit(solution)/shard_map/while/body/eval_jaxpr/i,rivc->rvc/dot_general | solution.py:79
  119.0 1.9 %select_convert_fusion.4 = bf16[4,32,16,130]{3,1,2,0:T(8,128)(2,1)S(1)} fusion(f32[4,16,130]{2,1,0:T(8,128)S(1)} %get-tuple-element.289, f32[32]{0:T(128)S(1)} %get-tuple-element.290, f32[4,16,130]{2,1,0:T(8,128)S(1)} %get-tuple-element.291, f32[32]{0:T(128)S(1)} %get-tuple-element.292, f32[4,16,130]{2,1,0:T(8,128)S(1)} %get-tuple-element.293, ...), kind=kLoop, calls=%fused_computation.2.clone.1 | loop fusion | flops 5324800 | bytes 835232 | tf_op jit(solution)/shard_map/while/body/eval_jaxpr/convert_element_type | solution.py:61
  120.9 1.0 constant_dynamic-slice_fusion.3
  124.2 1.4 %convolution_add_fusion.21 = f32[4,16,128,32]{2,3,1,0:T(8,128)} fusion(f32[4,16,128,32]{2,3,1,0:T(8,128)S(1)} %convolution_add_fusion.20, bf16[4,32,16,130]{3,1,2,0:T(8,128)(2,1)S(1)} %select_convert_fusion.4, bf16[4,32,1,130]{3,1,2,0:T(8,128)(2,1)S(1)} %get-tuple-element.308, bf16[32,32,3,3]{1,0,3,2:T(8,128)(2,1)S(1)} %get-tuple-element.352), kind=kOutput, calls=%fused_computation.9.clone.1 | convolution fusion | flops 18087936 | bytes 3219456 | tf_op jit(solution)/shard_map/while/body/eval_jaxpr/oi,rivc->rovc/dot_general | solution.py:72
  125.6 1.7 %fusion.108 = f32[1,4,16,128]{3,0,2,1:T(1,128)S(1)} fusion(f32[4,16,128,32]{2,3,1,0:T(8,128)} %convolution_add_fusion.21, bf16[4,32,1,130]{3,1,2,0:T(8,128)(2,1)S(1)} %get-tuple-element.308, bf16[4,32,16,130]{3,1,2,0:T(8,128)(2,1)S(1)} %select_convert_fusion.4, bf16[32,32,3,3]{1,0,3,2:T(8,128)(2,1)S(1)} %get-tuple-element.352, ...), kind=kOutput, calls=%fused_computation.18.clone.1 | convolution fusion | flops 19136512 | bytes 2204160 | tf_op jit(solution)/shard_map/while/body/eval_jaxpr/i,rivc->rvc/dot_general | solution.py:79
  127.3 0.7 fusion.109
  128.0 1.6 %copy_bitcast_fusion = bf16[4,16,896]{2,1,0:T(8,128)(2,1)} fusion(bf16[7,4,16,128]{3,2,1,0:T(8,128)(2,1)} %get-tuple-element.132), kind=kLoop, calls=%fused_computation.99 | loop fusion | bytes 229376 | tf_op jit(solution)/shard_map/reshape | solution.py:164
  (179 shorter events, 33.1 us)
Async XLA Ops:
  0.0 1.4 %copy-start = (bf16[896,896]{1,0:T(8,128)(2,1)S(1)}, bf16[896,896]{1,0:T(8,128)(2,1)}, u32[]{:S(2)}) copy-start(bf16[896,896]{1,0:T(8,128)(2,1)} %param.16) | copy-start | bytes 4816900
  1.0 11.0 %copy-start.3 = (f32[16,7]{0,1:T(8,128)S(1)}, f32[16,7]{0,1:T(8,128)}, u32[]{:S(2)}) copy-start(f32[16,7]{0,1:T(8,128)} %param.18) | copy-start | bytes 1348
  1.1 11.1 %copy-start.5 = (s32[16,7]{0,1:T(8,128)S(1)}, s32[16,7]{0,1:T(8,128)}, u32[]{:S(2)}) copy-start(s32[16,7]{0,1:T(8,128)} %param.17) | copy-start | bytes 1348
  1.1 11.5 %copy-start.2 = (bf16[32,3,3]{0,2,1:T(4,128)(2,1)S(1)}, bf16[32,3,3]{0,2,1:T(4,128)(2,1)}, u32[]{:S(2)}) copy-start(bf16[32,3,3]{0,2,1:T(4,128)(2,1)} %param.19) | copy-start | bytes 1732
  4.7 15.0 %all-to-all-start = ((bf16[16,2,1792]{2,1,0:T(2,128)(2,1)}), bf16[16,2,1792]{2,1,0:T(2,128)(2,1)S(1)}, u32[]{:S(2)}, u32[]{:S(2)}) async-start(bf16[16,2,1792]{2,1,0:T(2,128)(2,1)} %reshape.486), calls=%async_computation | async-start | bytes 229376 | tf_op jit(solution)/shard_map/all_to_all | solution.py:101
  20.5 5.2 %collective-permute-start = (bf16[4,8,896]{2,0,1:T(4,128)(2,1)S(1)}, bf16[4,8,896]{2,0,1:T(4,128)(2,1)S(1)}, u32[]{:S(2)}, u32[]{:S(2)}) collective-permute-start(bf16[4,8,896]{2,0,1:T(4,128)(2,1)S(1)} %get-tuple-element.193), channel_id=1, source_target_pairs={{0,16},{1,17},{2,18},{3,19},{4,20},{5,21},{6,22},{7,23},{8,24},{9,... | collective-permute-start | bytes 172040 | tf_op jit(solution)/shard_map/ppermute | solution.py:14
  24.0 6.1 %collective-permute-start.1 = (bf16[4,8,896]{2,0,1:T(4,128)(2,1)S(1)}, bf16[4,8,896]{2,0,1:T(4,128)(2,1)S(1)}, u32[]{:S(2)}, u32[]{:S(2)}) collective-permute-start(bf16[4,8,896]{2,0,1:T(4,128)(2,1)S(1)} %get-tuple-element.194), channel_id=1, source_target_pairs={{16,0},{17,1},{18,2},{19,3},{20,4},{21,5},{22,6},{23,7},{24,8},{25... | collective-permute-start | bytes 172040 | tf_op jit(solution)/shard_map/ppermute | solution.py:17
  32.9 19.3 %copy-start.1 = (bf16[32,32,3,3]{1,0,3,2:T(8,128)(2,1)S(1)}, bf16[32,32,3,3]{1,0,3,2:T(8,128)(2,1)}, u32[]{:S(2)}) copy-start(bf16[32,32,3,3]{1,0,3,2:T(8,128)(2,1)} %param.20) | copy-start | bytes 55300
  32.9 19.3 %copy-start.4 = (bf16[32]{0:T(256)(128)(2,1)S(1)}, bf16[32]{0:T(256)(128)(2,1)}, u32[]{:S(2)}) copy-start(bf16[32]{0:T(256)(128)(2,1)} %param.21) | copy-start | bytes 196
  33.0 3.0 %collective-permute-start.2 = (bf16[4,1,896]{2,1,0:T(2,128)(2,1)S(1)}, bf16[4,1,896]{2,1,0:T(2,128)(2,1)S(1)}, u32[]{:S(2)}, u32[]{:S(2)}) collective-permute-start(bf16[4,1,896]{2,1,0:T(2,128)(2,1)S(1)} %get-tuple-element.191), channel_id=1, source_target_pairs={{0,16},{1,17},{2,18},{3,19},{4,20},{5,21},{6,22},{7,23},{8,24},{9,... | collective-permute-start | bytes 21512 | tf_op jit(solution)/shard_map/ppermute | solution.py:14
  34.6 5.6 %collective-permute-start.3 = (bf16[4,1,896]{2,1,0:T(2,128)(2,1)S(1)}, bf16[4,1,896]{2,1,0:T(2,128)(2,1)S(1)}, u32[]{:S(2)}, u32[]{:S(2)}) collective-permute-start(bf16[4,1,896]{2,1,0:T(2,128)(2,1)S(1)} %get-tuple-element.192), channel_id=1, source_target_pairs={{16,0},{17,1},{18,2},{19,3},{20,4},{21,5},{22,6},{23,7},{24,8},{25... | collective-permute-start | bytes 21512 | tf_op jit(solution)/shard_map/ppermute | solution.py:17
  41.2 8.4 %collective-permute-start.5 = (bf16[4,32,1,898]{3,1,2,0:T(8,128)(2,1)S(1)}, bf16[4,32,1,898]{3,1,2,0:T(8,128)(2,1)}, u32[]{:S(2)}, u32[]{:S(2)}) collective-permute-start(bf16[4,32,1,898]{3,1,2,0:T(8,128)(2,1)S(1)} %select_convert_fusion.1), channel_id=1, source_target_pairs={{16,0},{17,1},{18,2},{19,3},{20,4},{21,5},{22,6},{23,7},{24,8},{25... | collective-permute-start | bytes 689672 | tf_op jit(solution)/shard_map/ppermute | solution.py:17
  43.1 9.1 %collective-permute-start.4 = (bf16[4,32,1,898]{3,1,2,0:T(8,128)(2,1)S(1)}, bf16[4,32,1,898]{3,1,2,0:T(8,128)(2,1)}, u32[]{:S(2)}, u32[]{:S(2)}) collective-permute-start(bf16[4,32,1,898]{3,1,2,0:T(8,128)(2,1)S(1)} %select_convert_fusion.2), channel_id=1, source_target_pairs={{0,16},{1,17},{2,18},{3,19},{4,20},{5,21},{6,22},{7,23},{8,24},{9,... | collective-permute-start | bytes 689672 | tf_op jit(solution)/shard_map/ppermute | solution.py:14
where the time goes:
time: 131 us; the launch traced here: 130 us
  matrix products  39.2 us (30%)
  other arithmetic  24.1 us (18%)
  starting transfers between devices  22.2 us (17%)
  waiting for transfers between devices  19.1 us (15%)
  local copies, waits for them, and re-layouts  19 us (15%)
  loops' own time  5.54 us (4%)
    dot_general x56, matrix products, second_layer(): jnp.einsum('oi,rivc->rovc', kern_second[:, :, offset_view, offset_col], w...  25.9 us
    convert_element_type x9, other arithmetic, first_layer(): jnp.where(valid[None, None], jnp.maximum(summed, 0.0), 0.0)  14 us
    dot_general x7, matrix products, second_layer(): jnp.einsum('i,rivc->rvc', kern_last, second, preferred_element_type=jnp.f...  12.1 us
    ppermute x3, starting transfers between devices, padded_2(): lax.ppermute(lax.slice_in_dim(block, block.shape[dim] - width, None, axis...  11 us
    ppermute x3, waiting for transfers between devices, padded_2(): lax.ppermute(lax.slice_in_dim(block, 0, width, axis=dim), axis, backward)  8.99 us
    all_to_all x1, starting transfers between devices, local(): lax.all_to_all(projected, 'dev', split_axis=0, concat_axis=1, tiled=True)  7.36 us
    dynamic_slice x7, local copies, waits for them, and re-layouts, one_block(): later = lax.dynamic_slice_in_dim(after_row, start, col_block + 2, axis=3)  7.3 us
    all_to_all x1, waiting for transfers between devices, local(): lax.all_to_all(projected, 'dev', split_axis=0, concat_axis=1, tiled=True)  6.9 us
  transfers between devices with their start and end apart: 7, of which 7 were waited for; matrix products, arithmetic and copies ran while one was open for 1% of the time, Pallas kernels for 0%

commit v1 on v0

v1 whole, which is shorter than its diff:
```python
import jax
import jax.numpy as jnp
from jax import lax
from jax.sharding import PartitionSpec as P

REACH = 8
RIM = 2


def halo_exchange(block, axis, dim, width):
    count = lax.axis_size(axis)
    forward = [(i, i + 1) for i in range(count - 1)]
    backward = [(target, source) for source, target in forward]
    low = lax.ppermute(
        lax.slice_in_dim(block, block.shape[dim] - width, None, axis=dim), axis, forward
    )
    high = lax.ppermute(lax.slice_in_dim(block, 0, width, axis=dim), axis, backward)
    return low, high


def prepare(mantissa, exponent, poly_square, poly_cube):
    lead_rows, lead_views, width_all = mantissa.shape
    block_count = exponent.shape[2]
    counts = mantissa.astype(jnp.float32).reshape(
        lead_rows, lead_views, block_count, width_all // block_count
    )
    counts = counts * jnp.exp2(-exponent.astype(jnp.float32))[..., None]
    line_int = -jnp.log(counts).reshape(lead_rows, lead_views, width_all)
    hardened = (
        line_int + poly_square * line_int * line_int + poly_cube * line_int * line_int * line_int
    )
    return hardened.astype(jnp.bfloat16)


def resample(hardened, col_map):
    shape_in = hardened.shape
    flat = hardened.reshape(-1, shape_in[2])
    product = jnp.dot(flat, col_map, preferred_element_type=jnp.float32)
    return product.astype(jnp.bfloat16).reshape(shape_in)


def local(
    mantissa,
    exponent,
    poly_square,
    poly_cube,
    col_map,
    rebin_offset,
    rebin_weight,
    kern_first,
    kern_second,
    kern_last,
):
    width_all = mantissa.shape[2]
    block_count = exponent.shape[2]
    col_block = width_all // block_count
    projected = resample(prepare(mantissa, exponent, poly_square, poly_cube), col_map)
    row_major = lax.all_to_all(projected, "dev", split_axis=0, concat_axis=1, tiled=True)
    row_count, view_count = (row_major.shape[0], row_major.shape[1])
    group_idx = lax.axis_index("group")
    total_views = view_count * lax.axis_size("group")
    view_start = group_idx * view_count
    halo = REACH + RIM

    params = jnp.stack([rebin_offset.astype(jnp.float32), rebin_weight], axis=0)
    low, high = halo_exchange(row_major, "group", 1, halo)
    params_low, params_high = halo_exchange(params, "group", 1, RIM)
    extended = jnp.concatenate([low, row_major, high], axis=1)
    params_ext = jnp.concatenate([params_low, params, params_high], axis=1)

    sig_views = view_count + 2 * RIM
    offset_ext = params_ext[0].astype(jnp.int32)
    weight_ext = params_ext[1]
    extended = extended.reshape(row_count, view_count + 2 * halo, block_count, col_block)
    lower_idx = jnp.arange(sig_views, dtype=jnp.int32)[:, None] + offset_ext + REACH
    block_ids = jnp.arange(block_count, dtype=jnp.int32)[None, :]
    lower = extended[:, lower_idx, block_ids, :].astype(jnp.float32)
    upper = extended[:, lower_idx + 1, block_ids, :].astype(jnp.float32)
    frac = weight_ext[None, :, :, None]
    signal = ((1.0 - frac) * lower + frac * upper).reshape(row_count, sig_views, width_all)
    sig_pos = view_start - RIM + jnp.arange(sig_views, dtype=jnp.int32)
    sig_valid = (sig_pos >= 0) & (sig_pos < total_views)
    signal = jnp.where(sig_valid[None, :, None], signal, 0.0).astype(jnp.bfloat16)

    numbers = ("NCHW", "OIHW", "NCHW")
    first = lax.conv_general_dilated(
        signal[:, None],
        kern_first[:, None],
        (1, 1),
        ((0, 0), (1, 1)),
        dimension_numbers=numbers,
        preferred_element_type=jnp.float32,
    )
    first_pos = view_start - 1 + jnp.arange(view_count + 2, dtype=jnp.int32)
    first_valid = (first_pos >= 0) & (first_pos < total_views)
    first = jnp.where(first_valid[None, None, :, None], jnp.maximum(first, 0.0), 0.0)
    first = first.astype(jnp.bfloat16)
    second = lax.conv_general_dilated(
        first,
        kern_second,
        (1, 1),
        ((0, 0), (1, 1)),
        dimension_numbers=numbers,
        preferred_element_type=jnp.float32,
    )
    second = jnp.maximum(second, 0.0).astype(jnp.bfloat16)
    mixed = signal[:, RIM : RIM + view_count].astype(jnp.float32) + jnp.einsum(
        "i,rivc->rvc", kern_last, second, preferred_element_type=jnp.float32
    )
    return mixed.astype(jnp.bfloat16)


def solution(mesh):
    return jax.shard_map(
        local,
        mesh=mesh,
        in_specs=(
            P(None, ("group", "dev"), None),
            P(None, ("group", "dev"), None),
            P(),
            P(),
            P(),
            P("group", None),
            P("group", None),
            P(),
            P(),
            P(),
        ),
        out_specs=P("dev", "group", None),
        check_vma=False,
    )
```

time: 131 us -> 118 us (0.901)
  local copies, waits for them, and re-layouts: 19 us -> 45.2 us
  other arithmetic: 24.1 us -> 9.33 us
  waiting for transfers between devices: 19.1 us -> 6.21 us
  loops' own time: 5.54 us -> 0 us
  starting transfers between devices: 22.2 us -> 17.9 us
    dot_general x63 -> x1, matrix products: 38 us -> 0.59 us  [local(): jnp.einsum('i,rivc->rvc', kern_last, second, preferred_element_type=jnp.f...]
    conv_general_dilated x0 -> x2, matrix products: none -> 36.2 us  [the longest x1 20.2 us: local(): lax.conv_general_dilated(first, kern_second, (1, 1), ((0, 0), (1, 1)), di...]
    conv_general_dilated x0 -> x4, local copies, waits for them, and re-layouts: none -> 20.9 us  [the longest x1 19.5 us: local(): lax.conv_general_dilated(first, kern_second, (1, 1), ((0, 0), (1, 1)), di...]
    convert_element_type x4 -> x6, local copies, waits for them, and re-layouts: 0.16 us -> 16.3 us  [the longest x3 15.5 us: local(): second = jnp.maximum(second, 0.0).astype(jnp.bfloat16)]
    ppermute x6 -> x4, waiting for transfers between devices: 12.2 us -> 0.01 us  [the longest x2 0.01 us: halo_exchange(): lax.ppermute(lax.slice_in_dim(block, block.shape[dim] - width, None, axis...]
    convert_element_type x26 -> x3, other arithmetic: 15.7 us -> 3.71 us  [the longest x1 3.31 us: local(): second = jnp.maximum(second, 0.0).astype(jnp.bfloat16)]
    dynamic_slice x14 -> x0, local copies, waits for them, and re-layouts: 11.9 us -> none  [the longest x7 7.3 us: one_block(): later = lax.dynamic_slice_in_dim(after_row, start, col_block + 2, axis=3)]
    another operation x1 -> x0, loops' own time: 5.54 us -> none  [local(): blocks_out = lax.map(one_block, jnp.arange(block_count, dtype=jnp.int32))]
  transfers between devices with their start and end apart: 7 -> 5, of which waited for: 7 -> 1; matrix products, arithmetic and copies ran while one was open for 1% -> 7% of each run, Pallas kernels for 0% -> 0%
where the time goes in v1:
time: 118 us; the launch traced here: 117 us
  local copies, waits for them, and re-layouts  45.2 us (38%)
  matrix products  38.1 us (32%)
  starting transfers between devices  17.9 us (15%)
  other arithmetic  9.33 us (8%)
  waiting for transfers between devices  6.21 us (5%)
    conv_general_dilated x1, matrix products, local(): lax.conv_general_dilated(first, kern_second, (1, 1), ((0, 0), (1, 1)), di...  20.2 us
    conv_general_dilated x1, local copies, waits for them, and re-layouts, local(): lax.conv_general_dilated(first, kern_second, (1, 1), ((0, 0), (1, 1)), di...  19.5 us
    conv_general_dilated x1, matrix products, local(): lax.conv_general_dilated(signal[:, None], kern_first[:, None], (1, 1), ((...  16 us
    convert_element_type x3, local copies, waits for them, and re-layouts, local(): second = jnp.maximum(second, 0.0).astype(jnp.bfloat16)  15.5 us
    ppermute x2, starting transfers between devices, halo_exchange(): lax.ppermute(lax.slice_in_dim(block, block.shape[dim] - width, None, axis...  9.41 us
    all_to_all x1, waiting for transfers between devices, local(): lax.all_to_all(projected, 'dev', split_axis=0, concat_axis=1, tiled=True)  6.2 us
    all_to_all x1, starting transfers between devices, local(): lax.all_to_all(projected, 'dev', split_axis=0, concat_axis=1, tiled=True)  5.91 us
    convert_element_type x1, other arithmetic, local(): second = jnp.maximum(second, 0.0).astype(jnp.bfloat16)  3.31 us
  transfers between devices with their start and end apart: 5, of which 1 were waited for; matrix products, arithmetic and copies ran while one was open for 7% of the time, Pallas kernels for 0%

profile of v1, /device:TPU:0, one launch (start us, length us, event | category | flops | bytes accessed | tf_op | source)
XLA Modules:
  0.0 117.1 jit_solution(6797341398389743550)
XLA Ops:
  0.0 0.8 convert_bitcast_fusion.4
  0.8 0.8 slice_maximum_fusion
  1.6 4.9 %collective-permute-start = (f32[2,2,7]{1,2,0:T(8,128)S(1)}, f32[2,2,7]{1,2,0:T(8,128)S(1)}, u32[]{:S(2)}, u32[]{:S(2)}) collective-permute-start(f32[2,2,7]{1,2,0:T(8,128)S(1)} %get-tuple-element.11), channel_id=1, source_target_pairs={{0,16},{1,17},{2,18},{3,19},{4,20},{5,21},{6,22},{7,23},{8,24},{9,... | collective-permute-start | bytes 344 | tf_op jit(solution)/shard_map/ppermute | solution.py:14
  6.5 1.3 %collective-permute-start.1 = (f32[2,2,7]{1,2,0:T(8,128)S(1)}, f32[2,2,7]{1,2,0:T(8,128)S(1)}, u32[]{:S(2)}, u32[]{:S(2)}) collective-permute-start(f32[2,2,7]{1,2,0:T(8,128)S(1)} %get-tuple-element.12), channel_id=1, source_target_pairs={{16,0},{17,1},{18,2},{19,3},{20,4},{21,5},{22,6},{23,7},{24,8},{25... | collective-permute-start | bytes 344 | tf_op jit(solution)/shard_map/ppermute | solution.py:17
  7.8 0.7 multiply_exponential_fusion
  8.5 0.1 copy.96
  8.6 0.1 mul.107
  8.8 1.3 %fusion.18 = bf16[64,1,896]{2,0,1:T(8,128)(2,1)S(1)} fusion(bf16[896,896]{1,0:T(8,128)(2,1)S(1)} %copy-done, f32[64,1,896]{2,0,1:T(8,128)S(1)} %mul.108, bf16[64,1,896]{2,0,1:T(8,128)(2,1)} %param.10, f32[896]{0:T(1024)} %param.13, f32[896]{0:T(1024)} %param.12), kind=kOutput, calls=%fused_computation.24 | convolution fusion | flops 103448576 | bytes 2071552 | tf_op jit(solution)/shard_map/dot_general | solution.py:38
  10.1 0.5 broadcast.220
  10.6 0.7 reduce.1
  11.3 0.7 reshape.212
  12.0 5.9 %all-to-all-start = ((bf16[16,2,1792]{2,1,0:T(2,128)(2,1)}), bf16[16,2,1792]{2,1,0:T(2,128)(2,1)S(1)}, u32[]{:S(2)}, u32[]{:S(2)}) async-start(bf16[16,2,1792]{2,1,0:T(2,128)(2,1)} %reshape.212), calls=%async_computation | async-start | bytes 229376 | tf_op jit(solution)/shard_map/all_to_all | solution.py:58
  18.0 0.6 slice.46
  18.6 0.8 pad_maximum_fusion.2
  19.4 6.2 %all-to-all-done = bf16[16,2,1792]{2,1,0:T(2,128)(2,1)S(1)} async-done(((bf16[16,2,1792]{2,1,0:T(2,128)(2,1)}), bf16[16,2,1792]{2,1,0:T(2,128)(2,1)S(1)}, u32[]{:S(2)}, u32[]{:S(2)}) %all-to-all-start) | async-done | bytes 114720 | tf_op jit(solution)/shard_map/all_to_all | solution.py:58
  25.6 0.1 reshape.213
  25.7 0.7 reduce
  26.5 1.3 %collective-permute-start.3 = (bf16[4,10,896]{2,0,1:T(4,128)(2,1)S(1)}, bf16[4,10,896]{2,0,1:T(4,128)(2,1)S(1)}, u32[]{:S(2)}, u32[]{:S(2)}) collective-permute-start(bf16[4,10,896]{2,0,1:T(4,128)(2,1)S(1)} %get-tuple-element.8), channel_id=1, source_target_pairs={{16,0},{17,1},{18,2},{19,3},{20,4},{21,5},{22,6},{23,7},{24,8},{25... | collective-permute-start | bytes 215048 | tf_op jit(solution)/shard_map/ppermute | solution.py:17
  27.8 4.5 %collective-permute-start.2 = (bf16[4,10,896]{2,0,1:T(4,128)(2,1)S(1)}, bf16[4,10,896]{2,0,1:T(4,128)(2,1)S(1)}, u32[]{:S(2)}, u32[]{:S(2)}) collective-permute-start(bf16[4,10,896]{2,0,1:T(4,128)(2,1)S(1)} %get-tuple-element.7), channel_id=1, source_target_pairs={{0,16},{1,17},{2,18},{3,19},{4,20},{5,21},{6,22},{7,23},{8,24},{9,... | collective-permute-start | bytes 215048 | tf_op jit(solution)/shard_map/ppermute | solution.py:14
  32.3 0.1 copy.85
  32.4 0.1 reshape.194
  32.5 0.1 copy.87
  32.6 0.1 reshape.200
  32.7 0.1 copy.78
  32.8 0.1 mul.103
  32.9 0.1 copy.86
  33.0 0.1 mul.118
  33.2 0.6 slice.42
  33.8 0.6 slice.44
  34.4 0.2 pad_maximum_fusion
  34.6 1.8 %gather_fusion = bf16[140,4,128]{2,1,0:T(4,128)(2,1)S(1)} fusion(bf16[4,36,7,128]{3,0,2,1:T(4,128)(2,1)S(1)} %pad_maximum_fusion, s32[140]{0:T(256)S(1)} %reshape.194), kind=kCustom, calls=%fused_computation | custom fusion | bytes 287840 | tf_op jit(solution)/shard_map/gather | solution.py:77
  36.4 1.8 %gather_fusion.1 = bf16[140,4,128]{2,1,0:T(4,128)(2,1)S(1)} fusion(bf16[4,36,7,128]{3,0,2,1:T(4,128)(2,1)S(1)} %pad_maximum_fusion, s32[140]{0:T(256)S(1)} %reshape.200), kind=kCustom, calls=%fused_computation.1 | custom fusion | bytes 287840 | tf_op jit(solution)/shard_map/gather | solution.py:78
  38.2 0.2 fusion.33
  38.4 0.9 convert_bitcast_fusion
  39.3 0.2 pad
  39.4 0.2 reshape.179
  39.7 0.1 fusion.32
  39.9 1.1 copy.88
  41.0 16.0 %fusion.14 = bf16[18,4,8,113,32]{4,2,1,3,0:T(8,128)(2,1)S(1)} fusion(pred[18]{0:T(512)(128)(4,1)S(1)} %compare_and_fusion, pred[32,113]{0,1:T(8,128)(4,1)} %constant.51, bf16[1,20,32,115]{2,0,3,1:T(2,128)(2,1)S(1)} %copy.88, bf16[32,1,3,3]{0,3,2,1:T(4,128)(2,1)} %bitcast.117), kind=kOutput, calls=%fused_computation.17 | convolution fusion | flops 47904768 | bytes 4317042 | tf_op jit(solution)/shard_map/conv_general_dilated | solution.py:86
  57.1 20.2 %fusion.4 = bf16[16,32,113,32]{3,1,2,0:T(8,128)(2,1)} fusion(bf16[32,32,3,3]{1,0,3,2:T(8,128)(2,1)S(1)} %copy-done.6, bf16[18,4,7,1,32]{4,2,1,3,0:T(8,128)(2,1)S(1)} %get-tuple-element.6, bf16[18,4,7,1,32]{4,2,1,3,0:T(8,128)(2,1)S(1)} %get-tuple-element.5, bf16[18,4,8,113,32]{4,2,1,3,0:T(8,128)(2,1)S(1)} %fusion.14), kind=kOutput, calls=%fused_computation.9 | convolution fusion | flops 1087598592 | bytes 7951360 | tf_op jit(solution)/shard_map/conv_general_dilated | solution.py:98
  77.2 19.5 %copy.90 = bf16[16,32,113,32]{2,3,1,0:T(8,128)(2,1)} copy(bf16[16,32,113,32]{3,1,2,0:T(8,128)(2,1)} %fusion.4) | data formatting | bytes 7405568 | tf_op jit(solution)/shard_map/conv_general_dilated | solution.py:98
  96.7 3.3 %maximum_convert_fusion = bf16[16,32,113,32]{2,3,1,0:T(8,128)(2,1)S(1)} fusion(bf16[16,32,113,32]{2,3,1,0:T(8,128)(2,1)} %copy.90), kind=kLoop, calls=%fused_computation.19 | loop fusion | flops 5554176 | bytes 7405568 | tf_op jit(solution)/shard_map/convert_element_type | solution.py:106
  100.1 3.7 %copy.91 = bf16[16,32,113,32]{2,1,3,0:T(8,128)(2,1)} copy(bf16[16,32,113,32]{2,3,1,0:T(8,128)(2,1)S(1)} %maximum_convert_fusion) | data formatting | bytes 7405568 | tf_op jit(solution)/shard_map/convert_element_type | solution.py:106
  103.7 8.4 %reshape.186 = bf16[16,4,904,32]{2,1,3,0:T(4,128)(2,1)} reshape(bf16[16,32,113,32]{2,1,3,0:T(8,128)(2,1)} %copy.91) | data formatting | bytes 7405568 | tf_op jit(solution)/shard_map/convert_element_type | solution.py:106
  112.2 3.4 %slice_bitcast_fusion = bf16[4,32,16,896]{3,0,1,2:T(4,128)(2,1)S(1)} fusion(bf16[16,4,904,32]{2,1,3,0:T(4,128)(2,1)} %reshape.186), kind=kLoop, calls=%fused_computation.20 | loop fusion | bytes 7340032 | tf_op jit(solution)/shard_map/convert_element_type | solution.py:106
  115.6 0.6 fusion.16
  116.2 0.2 fusion.30
  116.4 0.7 copy.92
  (34 shorter events, 0.4 us)
Async XLA Ops:
  0.0 8.8 %copy-start = (bf16[896,896]{1,0:T(8,128)(2,1)S(1)}, bf16[896,896]{1,0:T(8,128)(2,1)}, u32[]{:S(2)}) copy-start(bf16[896,896]{1,0:T(8,128)(2,1)} %param.14) | copy-start | bytes 4816900
  1.6 17.0 %collective-permute-start = (f32[2,2,7]{1,2,0:T(8,128)S(1)}, f32[2,2,7]{1,2,0:T(8,128)S(1)}, u32[]{:S(2)}, u32[]{:S(2)}) collective-permute-start(f32[2,2,7]{1,2,0:T(8,128)S(1)} %get-tuple-element.11), channel_id=1, source_target_pairs={{0,16},{1,17},{2,18},{3,19},{4,20},{5,21},{6,22},{7,23},{8,24},{9,... | collective-permute-start | bytes 344 | tf_op jit(solution)/shard_map/ppermute | solution.py:14
  6.5 12.1 %collective-permute-start.1 = (f32[2,2,7]{1,2,0:T(8,128)S(1)}, f32[2,2,7]{1,2,0:T(8,128)S(1)}, u32[]{:S(2)}, u32[]{:S(2)}) collective-permute-start(f32[2,2,7]{1,2,0:T(8,128)S(1)} %get-tuple-element.12), channel_id=1, source_target_pairs={{16,0},{17,1},{18,2},{19,3},{20,4},{21,5},{22,6},{23,7},{24,8},{25... | collective-permute-start | bytes 344 | tf_op jit(solution)/shard_map/ppermute | solution.py:17
  12.0 13.6 %all-to-all-start = ((bf16[16,2,1792]{2,1,0:T(2,128)(2,1)}), bf16[16,2,1792]{2,1,0:T(2,128)(2,1)S(1)}, u32[]{:S(2)}, u32[]{:S(2)}) async-start(bf16[16,2,1792]{2,1,0:T(2,128)(2,1)} %reshape.212), calls=%async_computation | async-start | bytes 229376 | tf_op jit(solution)/shard_map/all_to_all | solution.py:58
  26.5 8.0 %collective-permute-start.3 = (bf16[4,10,896]{2,0,1:T(4,128)(2,1)S(1)}, bf16[4,10,896]{2,0,1:T(4,128)(2,1)S(1)}, u32[]{:S(2)}, u32[]{:S(2)}) collective-permute-start(bf16[4,10,896]{2,0,1:T(4,128)(2,1)S(1)} %get-tuple-element.8), channel_id=1, source_target_pairs={{16,0},{17,1},{18,2},{19,3},{20,4},{21,5},{22,6},{23,7},{24,8},{25... | collective-permute-start | bytes 215048 | tf_op jit(solution)/shard_map/ppermute | solution.py:17
  27.8 6.7 %collective-permute-start.2 = (bf16[4,10,896]{2,0,1:T(4,128)(2,1)S(1)}, bf16[4,10,896]{2,0,1:T(4,128)(2,1)S(1)}, u32[]{:S(2)}, u32[]{:S(2)}) collective-permute-start(bf16[4,10,896]{2,0,1:T(4,128)(2,1)S(1)} %get-tuple-element.7), channel_id=1, source_target_pairs={{0,16},{1,17},{2,18},{3,19},{4,20},{5,21},{6,22},{7,23},{8,24},{9,... | collective-permute-start | bytes 215048 | tf_op jit(solution)/shard_map/ppermute | solution.py:14
  41.0 16.1 %copy-start.6 = (bf16[32,32,3,3]{1,0,3,2:T(8,128)(2,1)S(1)}, bf16[32,32,3,3]{1,0,3,2:T(8,128)(2,1)}, u32[]{:S(2)}) copy-start(bf16[32,32,3,3]{1,0,3,2:T(8,128)(2,1)} %param.18) | copy-start | bytes 55300
  96.7 18.9 %copy-start.7 = (bf16[32]{0:T(256)(128)(2,1)S(1)}, bf16[32]{0:T(256)(128)(2,1)}, u32[]{:S(2)}) copy-start(bf16[32]{0:T(256)(128)(2,1)} %param.19) | copy-start | bytes 196
  100.0 16.1 %copy-start.1 = (f32[4,20,896]{2,0,1:T(4,128)S(1)}, f32[4,20,896]{2,0,1:T(4,128)}, u32[]{:S(2)}) copy-start(f32[4,20,896]{2,0,1:T(4,128)} %get-tuple-element.13) | copy-start | bytes 860164
  100.0 16.1 %copy-start.2 = (f32[4,20,896]{2,0,1:T(4,128)S(1)}, f32[4,20,896]{2,0,1:T(4,128)}, u32[]{:S(2)}) copy-start(f32[4,20,896]{2,0,1:T(4,128)} %get-tuple-element.14) | copy-start | bytes 860164
  100.0 16.1 %copy-start.3 = (f32[16,896]{1,0:T(8,128)S(1)}, f32[16,896]{1,0:T(8,128)}, u32[]{:S(2)}) copy-start(f32[16,896]{1,0:T(8,128)} %slice.42) | copy-start | bytes 172036
  100.0 16.1 %copy-start.4 = (f32[16,896]{1,0:T(8,128)S(1)}, f32[16,896]{1,0:T(8,128)}, u32[]{:S(2)}) copy-start(f32[16,896]{1,0:T(8,128)} %slice.44) | copy-start | bytes 172036
  100.1 16.1 %copy-start.5 = (pred[16]{0:T(512)(128)(4,1)S(1)}, pred[16]{0:T(512)(128)(4,1)}, u32[]{:S(2)}) copy-start(pred[16]{0:T(512)(128)(4,1)} %slice.46) | copy-start | bytes 52

commit v2 on v1

--- a/solution.py
+++ b/solution.py
@@ -1,6 +1,10 @@
+import functools
+
 import jax
 import jax.numpy as jnp
 from jax import lax
+from jax.experimental import pallas as pl
+from jax.experimental.pallas import tpu as pltpu
 from jax.sharding import PartitionSpec as P
 
 REACH = 8
@@ -16,6 +20,72 @@
     )
     high = lax.ppermute(lax.slice_in_dim(block, 0, width, axis=dim), axis, backward)
     return low, high
+
+
+def conv_kernel(bounds_ref, sig_ref, w1_ref, w2_ref, kl_ref, out_ref, feat_ref, dual_ref, *, first_views, out_views, width, channels):
+    view_start = bounds_ref[0]
+    total_views = bounds_ref[1]
+    col = lax.broadcasted_iota(jnp.int32, (channels, width), 1)
+    keep_left = col >= 1
+    keep_right = col < width - 1
+    w1 = w1_ref[...]
+    for u in range(first_views):
+        taps = sig_ref[0, 3 * u : 3 * u + 16, :].astype(jnp.bfloat16)
+        hidden = jnp.dot(w1, taps, preferred_element_type=jnp.float32)
+        pos = view_start - 1 + u
+        scale = ((pos >= 0) & (pos < total_views)).astype(jnp.float32)
+        hidden = jnp.maximum(hidden, 0.0) * scale
+        base = 3 * u * channels
+        feat_ref[base : base + channels, :] = jnp.where(keep_left, pltpu.roll(hidden, 1, 1), 0.0).astype(jnp.bfloat16)
+        feat_ref[base + channels : base + 2 * channels, :] = hidden.astype(jnp.bfloat16)
+        feat_ref[base + 2 * channels : base + 3 * channels, :] = jnp.where(
+            keep_right, pltpu.roll(hidden, width - 1, 1), 0.0
+        ).astype(jnp.bfloat16)
+    w2 = w2_ref[...]
+    kl = kl_ref[...]
+    for v in range(out_views):
+        window = feat_ref[3 * v * channels : 3 * (v + 3) * channels, :]
+        second = jnp.dot(w2, window, preferred_element_type=jnp.float32)
+        second = jnp.maximum(second, 0.0).astype(jnp.bfloat16).astype(jnp.float32)
+        mix = jnp.sum(kl * second, axis=0, keepdims=True)
+        centre = sig_ref[0, 3 * (v + 2) + 1 : 3 * (v + 2) + 2, :]
+        dual_ref[v : v + 1, :] = centre + mix
+    out_ref[0] = dual_ref[...].astype(out_ref.dtype)
+
+
+def dual_conv(signal, bounds, kern_first, kern_second, kern_last):
+    rows, sig_views, width = signal.shape
+    channels = kern_first.shape[0]
+    first_views = sig_views - 2
+    out_views = sig_views - 4
+    zero = jnp.zeros_like(signal[..., :1])
+    left = jnp.concatenate([zero, signal[..., :-1]], axis=-1)
+    right = jnp.concatenate([signal[..., 1:], zero], axis=-1)
+    stacked = jnp.stack([left, signal, right], axis=2).astype(jnp.float32)
+    stacked = stacked.reshape(rows, sig_views * 3, width)
+    pad_rows = -(-(3 * first_views + 13) // 8) * 8
+    stacked = jnp.pad(stacked, ((0, 0), (0, pad_rows - sig_views * 3), (0, 0)))
+    w1 = jnp.pad(kern_first.reshape(channels, 9), ((0, 0), (0, 7)))
+    w2 = jnp.transpose(kern_second, (0, 2, 3, 1)).reshape(channels, 9 * channels)
+    kl = kern_last.astype(jnp.float32).reshape(channels, 1)
+    kernel = functools.partial(conv_kernel, first_views=first_views, out_views=out_views, width=width, channels=channels)
+    return pl.pallas_call(
+        kernel,
+        out_shape=jax.ShapeDtypeStruct((rows, out_views, width), jnp.bfloat16),
+        grid=(rows,),
+        in_specs=[
+            pl.BlockSpec(memory_space=pltpu.SMEM),
+            pl.BlockSpec((1, pad_rows, width), lambda r: (r, 0, 0)),
+            pl.BlockSpec((channels, 16), lambda r: (0, 0)),
+            pl.BlockSpec((channels, 9 * channels), lambda r: (0, 0)),
+            pl.BlockSpec((channels, 1), lambda r: (0, 0)),
+        ],
+        out_specs=pl.BlockSpec((1, out_views, width), lambda r: (r, 0, 0)),
+        scratch_shapes=[
+            pltpu.VMEM((first_views * 3 * channels, width), jnp.bfloat16),
+            pltpu.VMEM((out_views, width), jnp.float32),
+        ],
+    )(bounds, stacked, w1.astype(jnp.bfloat16), w2.astype(jnp.bfloat16), kl)
 
 
 def prepare(mantissa, exponent, poly_square, poly_cube):
@@ -82,32 +152,8 @@
     sig_valid = (sig_pos >= 0) & (sig_pos < total_views)
     signal = jnp.where(sig_valid[None, :, None], signal, 0.0).astype(jnp.bfloat16)
 
-    numbers = ("NCHW", "OIHW", "NCHW")
-    first = lax.conv_general_dilated(
-        signal[:, None],
-        kern_first[:, None],
-        (1, 1),
-        ((0, 0), (1, 1)),
-        dimension_numbers=numbers,
-        preferred_element_type=jnp.float32,
-    )
-    first_pos = view_start - 1 + jnp.arange(view_count + 2, dtype=jnp.int32)
-    first_valid = (first_pos >= 0) & (first_pos < total_views)
-    first = jnp.where(first_valid[None, None, :, None], jnp.maximum(first, 0.0), 0.0)
-    first = first.astype(jnp.bfloat16)
-    second = lax.conv_general_dilated(
-        first,
-        kern_second,
-        (1, 1),
-        ((0, 0), (1, 1)),
-        dimension_numbers=numbers,
-        preferred_element_type=jnp.float32,
-    )
-    second = jnp.maximum(second, 0.0).astype(jnp.bfloat16)
-    mixed = signal[:, RIM : RIM + view_count].astype(jnp.float32) + jnp.einsum(
-        "i,rivc->rvc", kern_last, second, preferred_element_type=jnp.float32
-    )
-    return mixed.astype(jnp.bfloat16)
+    bounds = jnp.stack([view_start, total_views]).astype(jnp.int32)
+    return dual_conv(signal, bounds, kern_first, kern_second, kern_last)
 
 
 def solution(mesh):

time: 118 us -> 50.4 us (0.43)
  matrix products: 38.1 us -> 1.31 us
  local copies, waits for them, and re-layouts: 45.2 us -> 8.77 us
  Pallas kernels: 0 us -> 9.54 us
  other arithmetic: 9.33 us -> 6.29 us
    conv_general_dilated x2 -> x0, matrix products: 36.2 us -> none  [the longest x1 20.2 us: local(): lax.conv_general_dilated(first, kern_second, (1, 1), ((0, 0), (1, 1)), di...]
    conv_general_dilated x4 -> x0, local copies, waits for them, and re-layouts: 20.9 us -> none  [the longest x1 19.5 us: local(): lax.conv_general_dilated(first, kern_second, (1, 1), ((0, 0), (1, 1)), di...]
    convert_element_type x6 -> x1, local copies, waits for them, and re-layouts: 16.3 us -> 0.05 us  [dual_conv(): stacked = jnp.stack([left, signal, right], axis=2).astype(jnp.float32)]
    pallas_call x0 -> x1, Pallas kernels: none -> 9.54 us  [dual_conv(): pl.pallas_call(kernel, out_shape=jax.ShapeDtypeStruct((rows, out_views, w...]
    convert_element_type x3 -> x0, other arithmetic: 4.37 us -> none  [the longest x1 3.31 us: local(): second = jnp.maximum(second, 0.0).astype(jnp.bfloat16)]
    slice x3 -> x1, local copies, waits for them, and re-layouts: 1.89 us -> 0.15 us  [dual_conv(): left = jnp.concatenate([zero, signal[..., :-1]], axis=-1)]
    reshape x0 -> x4, local copies, waits for them, and re-layouts: none -> 1.52 us  [the longest x1 0.71 us: dual_conv(): jnp.transpose(kern_second, (0, 2, 3, 1)).reshape(channels, 9 * channels)]
    all_to_all x1, waiting for transfers between devices: 6.2 us -> 4.76 us  [local(): lax.all_to_all(projected, 'dev', split_axis=0, concat_axis=1, tiled=True)]
  transfers between devices with their start and end apart: 5 -> 5, of which waited for: 1 -> 2; matrix products, arithmetic and copies ran while one was open for 7% -> 16% of each run, Pallas kernels for 0% -> 0%
where the time goes in v2:
time: 50.4 us; the launch traced here: 50 us
  starting transfers between devices  17.9 us (36%)
  Pallas kernels  9.54 us (19%)
  local copies, waits for them, and re-layouts  8.77 us (17%)
  other arithmetic  6.29 us (12%)
  waiting for transfers between devices  5.86 us (12%)
  matrix products  1.31 us (3%)
    pallas_call x1, Pallas kernels, dual_conv(): pl.pallas_call(kernel, out_shape=jax.ShapeDtypeStruct((rows, out_views, w...  9.54 us
    ppermute x2, starting transfers between devices, halo_exchange(): lax.ppermute(lax.slice_in_dim(block, block.shape[dim] - width, None, axis...  9.41 us
    all_to_all x1, starting transfers between devices, local(): lax.all_to_all(projected, 'dev', split_axis=0, concat_axis=1, tiled=True)  5.91 us
    all_to_all x1, waiting for transfers between devices, local(): lax.all_to_all(projected, 'dev', split_axis=0, concat_axis=1, tiled=True)  4.76 us
    ppermute x2, starting transfers between devices, halo_exchange(): lax.ppermute(lax.slice_in_dim(block, 0, width, axis=dim), axis, backward)  2.58 us
    gather x1, local copies, waits for them, and re-layouts, local(): upper = extended[:, lower_idx + 1, block_ids, :].astype(jnp.float32)  1.8 us
    gather x1, local copies, waits for them, and re-layouts, local(): lower = extended[:, lower_idx, block_ids, :].astype(jnp.float32)  1.8 us
    another operation x2, other arithmetic, local(): params = jnp.stack([rebin_offset.astype(jnp.float32), rebin_weight], axis=0)  1.64 us
  transfers between devices with their start and end apart: 5, of which 2 were waited for; matrix products, arithmetic and copies ran while one was open for 16% of the time, Pallas kernels for 0%

profile of v2, /device:TPU:0, one launch (start us, length us, event | category | flops | bytes accessed | tf_op | source)
XLA Modules:
  0.0 50.0 jit_solution(7980715976141623964)
XLA Ops:
  0.0 0.8 %convert_bitcast_fusion.4 = f32[1,16,7]{1,2,0:T(8,128)S(1)} fusion(s32[16,7]{0,1:T(8,128)} %param.15), kind=kLoop, calls=%fused_computation.45 | loop fusion | flops 112 | bytes 896 | tf_op jit(solution)/shard_map/stack | solution.py:135
  0.8 0.8 %slice_maximum_fusion = (f32[2,2,7]{1,2,0:T(8,128)S(1)}, f32[2,2,7]{1,2,0:T(8,128)S(1)}) fusion(f32[1,16,7]{1,2,0:T(8,128)} %bitcast.110, f32[1,16,7]{1,2,0:T(8,128)S(1)} %convert_bitcast_fusion.4), kind=kLoop, calls=%fused_computation.32 | loop fusion | flops 56 | bytes 1120 | tf_op jit(solution)/shard_map/stack | solution.py:135
  1.6 4.9 %collective-permute-start = (f32[2,2,7]{1,2,0:T(8,128)S(1)}, f32[2,2,7]{1,2,0:T(8,128)S(1)}, u32[]{:S(2)}, u32[]{:S(2)}) collective-permute-start(f32[2,2,7]{1,2,0:T(8,128)S(1)} %get-tuple-element.11), channel_id=1, source_target_pairs={{0,16},{1,17},{2,18},{3,19},{4,20},{5,21},{6,22},{7,23},{8,24},{9,... | collective-permute-start | bytes 344 | tf_op jit(solution)/shard_map/ppermute | solution.py:18
  6.5 1.3 %collective-permute-start.1 = (f32[2,2,7]{1,2,0:T(8,128)S(1)}, f32[2,2,7]{1,2,0:T(8,128)S(1)}, u32[]{:S(2)}, u32[]{:S(2)}) collective-permute-start(f32[2,2,7]{1,2,0:T(8,128)S(1)} %get-tuple-element.12), channel_id=1, source_target_pairs={{16,0},{17,1},{18,2},{19,3},{20,4},{21,5},{22,6},{23,7},{24,8},{25... | collective-permute-start | bytes 344 | tf_op jit(solution)/shard_map/ppermute | solution.py:21
  7.8 0.7 %multiply_exponential_fusion = f32[64,1,7]{0,1,2:T(1,128)S(1)} fusion(s32[64,1,7]{0,1,2:T(1,128)} %param.11), kind=kLoop, calls=%fused_computation.46 | loop fusion | flops 1344 | bytes 3584 | tf_op jit(solution)/shard_map/exp2 | solution.py:97
  8.5 0.1 copy.62
  8.6 0.1 mul.107
  8.7 0.0 copy-start.1
  8.8 0.0 copy-start.3
  8.8 0.0 copy-start.4
  8.9 1.3 %fusion = bf16[64,1,896]{2,0,1:T(8,128)(2,1)S(1)} fusion(bf16[896,896]{1,0:T(8,128)(2,1)S(1)} %copy-done, f32[64,1,896]{2,0,1:T(8,128)S(1)} %mul.108, bf16[64,1,896]{2,0,1:T(8,128)(2,1)} %param.10, f32[896]{0:T(1024)} %param.13, f32[896]{0:T(1024)} %param.12), kind=kOutput, calls=%fused_computation.3 | convolution fusion | flops 103448576 | bytes 2071552 | tf_op jit(solution)/shard_map/dot_general | solution.py:108
  10.2 0.5 %broadcast.174 = bf16[]{:T(256)} broadcast(bf16[]{:T(256)} %constant.79), dimensions={} | broadcast | bytes 4 | tf_op jit(solution)/shard_map/reshape | solution.py:109
  10.7 0.7 %reduce.1 = bf16[64,896]{1,0:T(8,128)(2,1)S(1)} reduce(bf16[64,1,896]{2,0,1:T(8,128)(2,1)S(1)} %fusion, bf16[]{:T(256)} %broadcast.174), dimensions={1}, to_apply=%copy.49.reduce_sub_computation | reduce | bytes 229378 | tf_op jit(solution)/shard_map/reshape | solution.py:109
  11.4 0.7 %reshape.211 = bf16[16,2,1792]{2,1,0:T(2,128)(2,1)} reshape(bf16[64,896]{1,0:T(8,128)(2,1)S(1)} %reduce.1) | data formatting | bytes 229376
  12.1 5.9 %all-to-all-start = ((bf16[16,2,1792]{2,1,0:T(2,128)(2,1)}), bf16[16,2,1792]{2,1,0:T(2,128)(2,1)S(1)}, u32[]{:S(2)}, u32[]{:S(2)}) async-start(bf16[16,2,1792]{2,1,0:T(2,128)(2,1)} %reshape.211), calls=%async_computation | async-start | bytes 229376 | tf_op jit(solution)/shard_map/all_to_all | solution.py:128
  18.0 0.1 copy.60
  18.1 0.7 %reshape.186.w2_ref = bf16[32,288]{1,0:T(8,128)(2,1)} reshape(bf16[32,3,3,32]{3,2,1,0:T(4,128)(2,1)S(1)} %copy.60) | data formatting | bytes 36864 | tf_op jit(solution)/shard_map/reshape | solution.py:69
  18.8 0.1 copy.59
  18.9 0.7 %copy.61.kl_ref = f32[32,1]{1,0:T(8,128)} copy(f32[32,1]{0,1:T(1,128)S(1)} %bitcast_convert_fusion) | data formatting | bytes 256 | tf_op jit(solution)/shard_map/reshape | solution.py:70
  19.6 0.6 %pad_add_fusion.bounds_ref = s32[2]{0:T(128)} fusion(s32[1]{0:T(128)} %constant.10.clone.1, s32[1]{0:T(128)} %bitcast), kind=kLoop, calls=%fused_computation.49 | loop fusion | flops 2 | bytes 16 | tf_op jit(solution)/shard_map/stack | solution.py:155
  20.2 0.6 %pad.14.w1_ref = bf16[32,16]{1,0:T(8,128)(2,1)} pad(bf16[32,9]{1,0:T(8,128)(2,1)S(1)} %copy.59, bf16[]{:T(256)} %constant.42.clone.1), padding=0_0x0_7 | pad | bytes 1602 | tf_op jit(solution)/shard_map/jit(_pad)/pad | solution.py:68
  20.8 0.1 pad_maximum_fusion.3
  20.9 4.8 %all-to-all-done = bf16[16,2,1792]{2,1,0:T(2,128)(2,1)S(1)} async-done(((bf16[16,2,1792]{2,1,0:T(2,128)(2,1)}), bf16[16,2,1792]{2,1,0:T(2,128)(2,1)S(1)}, u32[]{:S(2)}, u32[]{:S(2)}) %all-to-all-start) | async-done | bytes 114720 | tf_op jit(solution)/shard_map/all_to_all | solution.py:128
  25.7 0.1 reshape.212
  25.8 0.7 %reduce = bf16[64,896]{1,0:T(8,128)(2,1)S(1)} reduce(bf16[64,1,896]{2,1,0:T(2,128)(2,1)S(1)} %reshape.212, bf16[]{:T(256)} %constant.79), dimensions={1}, to_apply=%all_to_all.13.reduce_sub_computation | reduce | bytes 229378 | tf_op jit(solution)/shard_map/all_to_all | solution.py:128
  26.5 1.3 %collective-permute-start.3 = (bf16[4,10,896]{2,0,1:T(4,128)(2,1)S(1)}, bf16[4,10,896]{2,0,1:T(4,128)(2,1)S(1)}, u32[]{:S(2)}, u32[]{:S(2)}) collective-permute-start(bf16[4,10,896]{2,0,1:T(4,128)(2,1)S(1)} %get-tuple-element.8), channel_id=1, source_target_pairs={{16,0},{17,1},{18,2},{19,3},{20,4},{21,5},{22,6},{23,7},{24,8},{25... | collective-permute-start | bytes 215048 | tf_op jit(solution)/shard_map/ppermute | solution.py:21
  27.8 4.5 %collective-permute-start.2 = (bf16[4,10,896]{2,0,1:T(4,128)(2,1)S(1)}, bf16[4,10,896]{2,0,1:T(4,128)(2,1)S(1)}, u32[]{:S(2)}, u32[]{:S(2)}) collective-permute-start(bf16[4,10,896]{2,0,1:T(4,128)(2,1)S(1)} %get-tuple-element.7), channel_id=1, source_target_pairs={{0,16},{1,17},{2,18},{3,19},{4,20},{5,21},{6,22},{7,23},{8,24},{9,... | collective-permute-start | bytes 215048 | tf_op jit(solution)/shard_map/ppermute | solution.py:18
  32.4 0.1 copy.56
  32.5 0.1 reshape.201
  32.6 0.1 copy.54
  32.7 0.1 reshape.195
  32.8 0.1 copy.47
  32.9 0.1 mul.103
  33.0 0.1 copy.55
  33.1 0.1 mul.118
  33.2 1.1 %collective-permute-done.2 = bf16[4,10,896]{2,0,1:T(4,128)(2,1)S(1)} collective-permute-done((bf16[4,10,896]{2,0,1:T(4,128)(2,1)S(1)}, bf16[4,10,896]{2,0,1:T(4,128)(2,1)S(1)}, u32[]{:S(2)}, u32[]{:S(2)}) %collective-permute-start.2) | collective-permute-done | bytes 71712 | tf_op jit(solution)/shard_map/ppermute | solution.py:18
  34.3 0.2 pad_maximum_fusion.1
  34.5 1.8 %gather_fusion.1 = bf16[140,4,128]{2,1,0:T(4,128)(2,1)S(1)} fusion(bf16[4,36,7,128]{3,0,2,1:T(4,128)(2,1)S(1)} %pad_maximum_fusion.1, s32[140]{0:T(256)S(1)} %reshape.201), kind=kCustom, calls=%fused_computation.1 | custom fusion | bytes 287840 | tf_op jit(solution)/shard_map/gather | solution.py:148
  36.3 1.8 %gather_fusion = bf16[140,4,128]{2,1,0:T(4,128)(2,1)S(1)} fusion(bf16[4,36,7,128]{3,0,2,1:T(4,128)(2,1)S(1)} %pad_maximum_fusion.1, s32[140]{0:T(256)S(1)} %reshape.195), kind=kCustom, calls=%fused_computation | custom fusion | bytes 287840 | tf_op jit(solution)/shard_map/gather | solution.py:147
  38.1 0.2 fusion.8
  38.3 0.2 fusion.4
  38.5 0.1 fusion.24
  38.7 0.2 pad_bitcast_fusion
  38.8 0.4 pad_maximum_fusion
  39.2 0.1 copy.57
  39.4 0.1 copy.58
  39.4 1.0 %pad_convert_fusion.sig_ref = f32[4,72,896]{2,1,0:T(8,128)} fusion(bf16[4,60,896]{2,1,0:T(8,128)(2,1)S(1)} %copy.58), kind=kLoop, calls=%fused_computation.4 | loop fusion | flops 258048 | bytes 1462272 | tf_op jit(solution)/shard_map/jit(_pad)/pad | solution.py:67
  40.4 9.5 %shard_map.100 = bf16[4,16,896]{2,1,0:T(8,128)(2,1)} custom-call(s32[2]{0:T(128)} %pad_add_fusion.bounds_ref, f32[4,72,896]{2,1,0:T(8,128)} %pad_convert_fusion.sig_ref, bf16[32,16]{1,0:T(8,128)(2,1)} %pad.14.w1_ref, bf16[32,288]{1,0:T(8,128)(2,1)} %reshape.186.w2_ref, f32[32,1]{1,0:T(8,128)} %copy.61.kl_ref), custom_call_target="tpu_custom_call" | custom-call | tf_op jit(solution)/shard_map/pallas_call | solution.py:72
  (23 shorter events, 0.3 us)
Async XLA Ops:
  0.0 8.8 %copy-start = (bf16[896,896]{1,0:T(8,128)(2,1)S(1)}, bf16[896,896]{1,0:T(8,128)(2,1)}, u32[]{:S(2)}) copy-start(bf16[896,896]{1,0:T(8,128)(2,1)} %param.14) | copy-start | bytes 4816900
  1.6 19.2 %collective-permute-start = (f32[2,2,7]{1,2,0:T(8,128)S(1)}, f32[2,2,7]{1,2,0:T(8,128)S(1)}, u32[]{:S(2)}, u32[]{:S(2)}) collective-permute-start(f32[2,2,7]{1,2,0:T(8,128)S(1)} %get-tuple-element.11), channel_id=1, source_target_pairs={{0,16},{1,17},{2,18},{3,19},{4,20},{5,21},{6,22},{7,23},{8,24},{9,... | collective-permute-start | bytes 344 | tf_op jit(solution)/shard_map/ppermute | solution.py:18
  6.5 14.3 %collective-permute-start.1 = (f32[2,2,7]{1,2,0:T(8,128)S(1)}, f32[2,2,7]{1,2,0:T(8,128)S(1)}, u32[]{:S(2)}, u32[]{:S(2)}) collective-permute-start(f32[2,2,7]{1,2,0:T(8,128)S(1)} %get-tuple-element.12), channel_id=1, source_target_pairs={{16,0},{17,1},{18,2},{19,3},{20,4},{21,5},{22,6},{23,7},{24,8},{25... | collective-permute-start | bytes 344 | tf_op jit(solution)/shard_map/ppermute | solution.py:21
  8.7 9.3 %copy-start.1 = (bf16[32,32,3,3]{1,0,3,2:T(8,128)(2,1)S(1)}, bf16[32,32,3,3]{1,0,3,2:T(8,128)(2,1)}, u32[]{:S(2)}) copy-start(bf16[32,32,3,3]{1,0,3,2:T(8,128)(2,1)} %param.18) | copy-start | bytes 55300
  8.8 10.0 %copy-start.3 = (bf16[32,3,3]{0,2,1:T(4,128)(2,1)S(1)}, bf16[32,3,3]{0,2,1:T(4,128)(2,1)}, u32[]{:S(2)}) copy-start(bf16[32,3,3]{0,2,1:T(4,128)(2,1)} %param.17) | copy-start | bytes 1732
  8.8 10.1 %copy-start.4 = (bf16[32]{0:T(256)(128)(2,1)S(1)}, bf16[32]{0:T(256)(128)(2,1)}, u32[]{:S(2)}) copy-start(bf16[32]{0:T(256)(128)(2,1)} %param.19) | copy-start | bytes 196
  8.8 12.0 %copy-start.2 = (f32[16,7]{0,1:T(8,128)S(1)}, f32[16,7]{0,1:T(8,128)}, u32[]{:S(2)}) copy-start(f32[16,7]{0,1:T(8,128)} %param.16) | copy-start | bytes 1348
  12.1 13.6 %all-to-all-start = ((bf16[16,2,1792]{2,1,0:T(2,128)(2,1)}), bf16[16,2,1792]{2,1,0:T(2,128)(2,1)S(1)}, u32[]{:S(2)}, u32[]{:S(2)}) async-start(bf16[16,2,1792]{2,1,0:T(2,128)(2,1)} %reshape.211), calls=%async_computation | async-start | bytes 229376 | tf_op jit(solution)/shard_map/all_to_all | solution.py:128
  26.5 6.7 %collective-permute-start.3 = (bf16[4,10,896]{2,0,1:T(4,128)(2,1)S(1)}, bf16[4,10,896]{2,0,1:T(4,128)(2,1)S(1)}, u32[]{:S(2)}, u32[]{:S(2)}) collective-permute-start(bf16[4,10,896]{2,0,1:T(4,128)(2,1)S(1)} %get-tuple-element.8), channel_id=1, source_target_pairs={{16,0},{17,1},{18,2},{19,3},{20,4},{21,5},{22,6},{23,7},{24,8},{25... | collective-permute-start | bytes 215048 | tf_op jit(solution)/shard_map/ppermute | solution.py:21
  27.8 6.5 %collective-permute-start.2 = (bf16[4,10,896]{2,0,1:T(4,128)(2,1)S(1)}, bf16[4,10,896]{2,0,1:T(4,128)(2,1)S(1)}, u32[]{:S(2)}, u32[]{:S(2)}) collective-permute-start(bf16[4,10,896]{2,0,1:T(4,128)(2,1)S(1)} %get-tuple-element.7), channel_id=1, source_target_pairs={{0,16},{1,17},{2,18},{3,19},{4,20},{5,21},{6,22},{7,23},{8,24},{9,... | collective-permute-start | bytes 215048 | tf_op jit(solution)/shard_map/ppermute | solution.py:18

commit v3 on v2

v3 whole, which is shorter than its diff:
```python
import functools

import jax
import jax.numpy as jnp
from jax import lax
from jax.experimental import pallas as pl
from jax.experimental.pallas import tpu as pltpu
from jax.sharding import PartitionSpec as P

REACH = 8
RIM = 2


def halo_exchange(block, axis, dim, width):
    count = lax.axis_size(axis)
    forward = [(i, i + 1) for i in range(count - 1)]
    backward = [(target, source) for source, target in forward]
    low = lax.ppermute(
        lax.slice_in_dim(block, block.shape[dim] - width, None, axis=dim), axis, forward
    )
    high = lax.ppermute(lax.slice_in_dim(block, 0, width, axis=dim), axis, backward)
    return low, high


def conv_kernel(
    offset_ref,
    weight_ref,
    bounds_ref,
    ext_ref,
    w1_ref,
    w2_ref,
    kl_ref,
    out_ref,
    sig_ref,
    feat_ref,
    dual_ref,
    *,
    sig_views,
    block_count,
    col_block,
    channels,
):
    width = block_count * col_block
    first_views = sig_views - 2
    out_views = sig_views - 4
    view_start = bounds_ref[0]
    total_views = bounds_ref[1]
    lane = lax.broadcasted_iota(jnp.int32, (1, width), 1)
    sig_ref[3 * sig_views :, :] = jnp.zeros((sig_ref.shape[0] - 3 * sig_views, width), jnp.float32)
    for u in range(sig_views):
        pos = view_start - RIM + u
        keep = ((pos >= 0) & (pos < total_views)).astype(jnp.float32)
        for k in range(block_count):
            low = u + offset_ref[u * block_count + k] + REACH
            frac = weight_ref[u * block_count + k]
            cols = pl.ds(k * col_block, col_block)
            lower = ext_ref[0, low, :, cols]
            upper = ext_ref[0, low + 1, :, cols]
            value = ((1.0 - frac) * lower + frac * upper).astype(jnp.bfloat16)
            sig_ref[3 * u + 1 : 3 * u + 2, cols] = value.astype(jnp.float32) * keep
        row = sig_ref[3 * u + 1 : 3 * u + 2, :]
        sig_ref[3 * u : 3 * u + 1, :] = jnp.where(lane >= 1, pltpu.roll(row, 1, 1), 0.0)
        sig_ref[3 * u + 2 : 3 * u + 3, :] = jnp.where(
            lane < width - 1, pltpu.roll(row, width - 1, 1), 0.0
        )
    col = lax.broadcasted_iota(jnp.int32, (channels, width), 1)
    keep_left = col >= 1
    keep_right = col < width - 1
    w1 = w1_ref[...]
    for u in range(first_views):
        taps = sig_ref[3 * u : 3 * u + 16, :].astype(jnp.bfloat16)
        hidden = jnp.dot(w1, taps, preferred_element_type=jnp.float32)
        pos = view_start - 1 + u
        scale = ((pos >= 0) & (pos < total_views)).astype(jnp.float32)
        hidden = jnp.maximum(hidden, 0.0) * scale
        base = 3 * u * channels
        feat_ref[base : base + channels, :] = jnp.where(
            keep_left, pltpu.roll(hidden, 1, 1), 0.0
        ).astype(jnp.bfloat16)
        feat_ref[base + channels : base + 2 * channels, :] = hidden.astype(jnp.bfloat16)
        feat_ref[base + 2 * channels : base + 3 * channels, :] = jnp.where(
            keep_right, pltpu.roll(hidden, width - 1, 1), 0.0
        ).astype(jnp.bfloat16)
    w2 = w2_ref[...]
    kl = kl_ref[...]
    for v in range(out_views):
        window = feat_ref[3 * v * channels : 3 * (v + 3) * channels, :]
        second = jnp.dot(w2, window, preferred_element_type=jnp.float32)
        second = jnp.maximum(second, 0.0).astype(jnp.bfloat16).astype(jnp.float32)
        mix = jnp.sum(kl * second, axis=0, keepdims=True)
        centre = sig_ref[3 * (v + 2) + 1 : 3 * (v + 2) + 2, :]
        dual_ref[v : v + 1, :] = centre + mix
    out_ref[0] = dual_ref[...].astype(out_ref.dtype)


def rebin_dual(extended, offsets, weights, bounds, kern_first, kern_second, kern_last):
    rows, ext_views, width = extended.shape
    sig_views, block_count = offsets.shape
    col_block = width // block_count
    channels = kern_first.shape[0]
    first_views = sig_views - 2
    out_views = sig_views - 4
    pad_rows = -(-(3 * first_views + 13) // 8) * 8
    w1 = jnp.pad(kern_first.reshape(channels, 9), ((0, 0), (0, 7)))
    w2 = jnp.transpose(kern_second, (0, 2, 3, 1)).reshape(channels, 9 * channels)
    kl = kern_last.astype(jnp.float32).reshape(channels, 1)
    kernel = functools.partial(
        conv_kernel,
        sig_views=sig_views,
        block_count=block_count,
        col_block=col_block,
        channels=channels,
    )
    grid_spec = pltpu.PrefetchScalarGridSpec(
        num_scalar_prefetch=3,
        grid=(rows,),
        in_specs=[
            pl.BlockSpec((1, ext_views, 1, width), lambda r, *_: (r, 0, 0, 0)),
            pl.BlockSpec((channels, 16), lambda r, *_: (0, 0)),
            pl.BlockSpec((channels, 9 * channels), lambda r, *_: (0, 0)),
            pl.BlockSpec((channels, 1), lambda r, *_: (0, 0)),
        ],
        out_specs=pl.BlockSpec((1, out_views, width), lambda r, *_: (r, 0, 0)),
        scratch_shapes=[
            pltpu.VMEM((pad_rows, width), jnp.float32),
            pltpu.VMEM((first_views * 3 * channels, width), jnp.bfloat16),
            pltpu.VMEM((out_views, width), jnp.float32),
        ],
    )
    return pl.pallas_call(
        kernel,
        out_shape=jax.ShapeDtypeStruct((rows, out_views, width), jnp.bfloat16),
        grid_spec=grid_spec,
    )(
        offsets.reshape(-1),
        weights.reshape(-1),
        bounds,
        extended.astype(jnp.float32).reshape(rows, ext_views, 1, width),
        w1.astype(jnp.bfloat16),
        w2.astype(jnp.bfloat16),
        kl,
    )


def prepare(mantissa, exponent, poly_square, poly_cube):
    lead_rows, lead_views, width_all = mantissa.shape
    block_count = exponent.shape[2]
    counts = mantissa.astype(jnp.float32).reshape(
        lead_rows, lead_views, block_count, width_all // block_count
    )
    counts = counts * jnp.exp2(-exponent.astype(jnp.float32))[..., None]
    line_int = -jnp.log(counts).reshape(lead_rows, lead_views, width_all)
    hardened = (
        line_int + poly_square * line_int * line_int + poly_cube * line_int * line_int * line_int
    )
    return hardened.astype(jnp.bfloat16)


def resample(hardened, col_map):
    shape_in = hardened.shape
    flat = hardened.reshape(-1, shape_in[2])
    product = jnp.dot(flat, col_map, preferred_element_type=jnp.float32)
    return product.astype(jnp.bfloat16).reshape(shape_in)


def local(
    mantissa,
    exponent,
    poly_square,
    poly_cube,
    col_map,
    rebin_offset,
    rebin_weight,
    kern_first,
    kern_second,
    kern_last,
):
    projected = resample(prepare(mantissa, exponent, poly_square, poly_cube), col_map)
    row_major = lax.all_to_all(projected, "dev", split_axis=0, concat_axis=1, tiled=True)
    row_count, view_count = (row_major.shape[0], row_major.shape[1])
    group_idx = lax.axis_index("group")
    total_views = view_count * lax.axis_size("group")
    view_start = group_idx * view_count
    halo = REACH + RIM

    params = jnp.stack([rebin_offset.astype(jnp.float32), rebin_weight], axis=0)
    low, high = halo_exchange(row_major, "group", 1, halo)
    params_low, params_high = halo_exchange(params, "group", 1, RIM)
    extended = jnp.concatenate([low, row_major, high], axis=1)
    params_ext = jnp.concatenate([params_low, params, params_high], axis=1)

    offsets = params_ext[0].astype(jnp.int32)
    weights = params_ext[1]
    bounds = jnp.stack([view_start, total_views]).astype(jnp.int32)
    return rebin_dual(extended, offsets, weights, bounds, kern_first, kern_second, kern_last)


def solution(mesh):
    return jax.shard_map(
        local,
        mesh=mesh,
        in_specs=(
            P(None, ("group", "dev"), None),
            P(None, ("group", "dev"), None),
            P(),
            P(),
            P(),
            P("group", None),
            P("group", None),
            P(),
            P(),
            P(),
        ),
        out_specs=P("dev", "group", None),
        check_vma=False,
    )
```

time: 50.4 us -> 51.8 us (1.028)
  local copies, waits for them, and re-layouts: 8.77 us -> 5.81 us
  waiting for transfers between devices: 5.86 us -> 8.54 us
  Pallas kernels: 9.54 us -> 11.8 us
    ppermute x2, waiting for transfers between devices: 0.01 us -> 3.72 us  [halo_exchange(): lax.ppermute(lax.slice_in_dim(block, 0, width, axis=dim), axis, backward)]
    gather x2 -> x0, local copies, waits for them, and re-layouts: 3.6 us -> none  [the longest x1 1.8 us: local(): upper = extended[:, lower_idx + 1, block_ids, :].astype(jnp.float32)]
    pallas_call x1, Pallas kernels: 9.54 us -> 11.8 us  [rebin_dual(): pl.pallas_call(kernel, out_shape=jax.ShapeDtypeStruct((rows, out_views, w...]
    convert_element_type x2 -> x1, other arithmetic: 0.38 us -> 1.49 us  [rebin_dual(): extended.astype(jnp.float32).reshape(rows, ext_views, 1, width)]
    ppermute x2, waiting for transfers between devices: 1.09 us -> 0.01 us  [halo_exchange(): lax.ppermute(lax.slice_in_dim(block, block.shape[dim] - width, None, axis...]
    pad x1 -> x0, other arithmetic: 1.02 us -> none  [dual_conv(): stacked = jnp.pad(stacked, ((0, 0), (0, pad_rows - sig_views * 3), (0, 0)))]
    convert_element_type x1 -> x2, local copies, waits for them, and re-layouts: 0.05 us -> 0.77 us  [local(): offsets = params_ext[0].astype(jnp.int32)]
  transfers between devices with their start and end apart: 5 -> 5, of which waited for: 2 -> 2; matrix products, arithmetic and copies ran while one was open for 16% -> 17% of each run, Pallas kernels for 0% -> 0%
where the time goes in v3:
time: 51.8 us; the launch traced here: 51.3 us
  starting transfers between devices  17.9 us (35%)
  Pallas kernels  11.8 us (23%)
  waiting for transfers between devices  8.54 us (16%)
  local copies, waits for them, and re-layouts  5.81 us (11%)
  other arithmetic  5.79 us (11%)
  matrix products  1.31 us (3%)
    pallas_call x1, Pallas kernels, rebin_dual(): pl.pallas_call(kernel, out_shape=jax.ShapeDtypeStruct((rows, out_views, w...  11.8 us
    ppermute x2, starting transfers between devices, halo_exchange(): lax.ppermute(lax.slice_in_dim(block, block.shape[dim] - width, None, axis...  9.41 us
    all_to_all x1, starting transfers between devices, local(): lax.all_to_all(projected, 'dev', split_axis=0, concat_axis=1, tiled=True)  5.91 us
    all_to_all x1, waiting for transfers between devices, local(): lax.all_to_all(projected, 'dev', split_axis=0, concat_axis=1, tiled=True)  4.82 us
    ppermute x2, waiting for transfers between devices, halo_exchange(): lax.ppermute(lax.slice_in_dim(block, 0, width, axis=dim), axis, backward)  3.72 us
    ppermute x2, starting transfers between devices, halo_exchange(): lax.ppermute(lax.slice_in_dim(block, 0, width, axis=dim), axis, backward)  2.58 us
    another operation x2, other arithmetic, local(): params = jnp.stack([rebin_offset.astype(jnp.float32), rebin_weight], axis=0)  1.64 us
    convert_element_type x1, other arithmetic, rebin_dual(): extended.astype(jnp.float32).reshape(rows, ext_views, 1, width)  1.49 us
  transfers between devices with their start and end apart: 5, of which 2 were waited for; matrix products, arithmetic and copies ran while one was open for 17% of the time, Pallas kernels for 0%

profile of v3, /device:TPU:0, one launch (start us, length us, event | category | flops | bytes accessed | tf_op | source)
XLA Modules:
  0.0 51.3 jit_solution(6055281103246437649)
XLA Ops:
  0.0 0.0 copy-start
  0.0 0.8 %convert_bitcast_fusion = f32[1,16,7]{1,2,0:T(8,128)S(1)} fusion(s32[16,7]{0,1:T(8,128)} %param.15), kind=kLoop, calls=%fused_computation.15 | loop fusion | flops 112 | bytes 896 | tf_op jit(solution)/shard_map/stack | solution.py:186
  0.8 0.8 %slice_maximum_fusion = (f32[2,2,7]{1,2,0:T(8,128)S(1)}, f32[2,2,7]{1,2,0:T(8,128)S(1)}) fusion(f32[1,16,7]{1,2,0:T(8,128)} %bitcast.32, f32[1,16,7]{1,2,0:T(8,128)S(1)} %convert_bitcast_fusion), kind=kLoop, calls=%fused_computation.12 | loop fusion | flops 56 | bytes 1120 | tf_op jit(solution)/shard_map/stack | solution.py:186
  1.6 4.9 %collective-permute-start = (f32[2,2,7]{1,2,0:T(8,128)S(1)}, f32[2,2,7]{1,2,0:T(8,128)S(1)}, u32[]{:S(2)}, u32[]{:S(2)}) collective-permute-start(f32[2,2,7]{1,2,0:T(8,128)S(1)} %get-tuple-element.9), channel_id=1, source_target_pairs={{0,16},{1,17},{2,18},{3,19},{4,20},{5,21},{6,22},{7,23},{8,24},{9,... | collective-permute-start | bytes 344 | tf_op jit(solution)/shard_map/ppermute | solution.py:18
  6.5 1.3 %collective-permute-start.1 = (f32[2,2,7]{1,2,0:T(8,128)S(1)}, f32[2,2,7]{1,2,0:T(8,128)S(1)}, u32[]{:S(2)}, u32[]{:S(2)}) collective-permute-start(f32[2,2,7]{1,2,0:T(8,128)S(1)} %get-tuple-element.10), channel_id=1, source_target_pairs={{16,0},{17,1},{18,2},{19,3},{20,4},{21,5},{22,6},{23,7},{24,8},{25... | collective-permute-start | bytes 344 | tf_op jit(solution)/shard_map/ppermute | solution.py:21
  7.8 0.7 %multiply_exponential_fusion = f32[64,1,7]{0,1,2:T(1,128)S(1)} fusion(s32[64,1,7]{0,1,2:T(1,128)} %param.11), kind=kLoop, calls=%fused_computation.16 | loop fusion | flops 1344 | bytes 3584 | tf_op jit(solution)/shard_map/exp2 | solution.py:151
  8.5 0.1 copy.59
  8.6 0.1 mul.56
  8.7 0.0 copy-start.1
  8.8 0.0 copy-done
  8.8 0.0 copy-start.3
  8.8 0.0 copy-start.4
  8.8 0.0 copy-start.2
  8.9 1.3 %fusion = bf16[64,1,896]{2,0,1:T(8,128)(2,1)S(1)} fusion(bf16[896,896]{1,0:T(8,128)(2,1)S(1)} %copy-done, f32[64,1,896]{2,0,1:T(8,128)S(1)} %mul.57, bf16[64,1,896]{2,0,1:T(8,128)(2,1)} %param.10, f32[896]{0:T(1024)} %param.13, f32[896]{0:T(1024)} %param.12), kind=kOutput, calls=%fused_computation.1 | convolution fusion | flops 103448576 | bytes 2071552 | tf_op jit(solution)/shard_map/dot_general | solution.py:162
  10.2 0.5 %broadcast.17 = bf16[]{:T(256)} broadcast(bf16[]{:T(256)} %constant.19), dimensions={} | broadcast | bytes 4 | tf_op jit(solution)/shard_map/reshape | solution.py:163
  10.7 0.7 %reduce.1 = bf16[64,896]{1,0:T(8,128)(2,1)S(1)} reduce(bf16[64,1,896]{2,0,1:T(8,128)(2,1)S(1)} %fusion, bf16[]{:T(256)} %broadcast.17), dimensions={1}, to_apply=%copy.50.reduce_sub_computation | reduce | bytes 229378 | tf_op jit(solution)/shard_map/reshape | solution.py:163
  11.4 0.7 %reshape.108 = bf16[16,2,1792]{2,1,0:T(2,128)(2,1)} reshape(bf16[64,896]{1,0:T(8,128)(2,1)S(1)} %reduce.1) | data formatting | bytes 229376
  12.1 5.9 %all-to-all-start = ((bf16[16,2,1792]{2,1,0:T(2,128)(2,1)}), bf16[16,2,1792]{2,1,0:T(2,128)(2,1)S(1)}, u32[]{:S(2)}, u32[]{:S(2)}) async-start(bf16[16,2,1792]{2,1,0:T(2,128)(2,1)} %reshape.108), calls=%async_computation | async-start | bytes 229376 | tf_op jit(solution)/shard_map/all_to_all | solution.py:179
  18.0 0.0 copy-done.1
  18.0 0.1 copy.57
  18.1 0.7 %reshape.102.w2_ref = bf16[32,288]{1,0:T(8,128)(2,1)} reshape(bf16[32,3,3,32]{3,2,1,0:T(4,128)(2,1)S(1)} %copy.57) | data formatting | bytes 36864 | tf_op jit(solution)/shard_map/reshape | solution.py:105
  18.8 0.0 copy-done.3
  18.8 0.1 copy.56
  18.9 0.0 copy-done.4
  18.9 0.7 %copy.58.kl_ref = f32[32,1]{1,0:T(8,128)} copy(f32[32,1]{0,1:T(1,128)S(1)} %bitcast_convert_fusion) | data formatting | bytes 256 | tf_op jit(solution)/shard_map/reshape | solution.py:106
  19.6 0.6 %pad_add_fusion.bounds_ref = s32[2]{0:T(128)} fusion(s32[1]{0:T(128)} %constant.12.clone.1, s32[1]{0:T(128)} %bitcast.2), kind=kLoop, calls=%fused_computation.17 | loop fusion | flops 2 | bytes 16 | tf_op jit(solution)/shard_map/stack | solution.py:194
  20.2 0.6 %pad.4.w1_ref = bf16[32,16]{1,0:T(8,128)(2,1)} pad(bf16[32,9]{1,0:T(8,128)(2,1)S(1)} %copy.56, bf16[]{:T(256)} %constant.14.clone.1), padding=0_0x0_7 | pad | bytes 1602 | tf_op jit(solution)/shard_map/jit(_pad)/pad | solution.py:104
  20.8 0.0 collective-permute-done
  20.8 0.0 collective-permute-done.1
  20.8 0.0 copy-done.2
  20.8 0.1 pad_maximum_fusion.1
  20.9 4.8 %all-to-all-done = bf16[16,2,1792]{2,1,0:T(2,128)(2,1)S(1)} async-done(((bf16[16,2,1792]{2,1,0:T(2,128)(2,1)}), bf16[16,2,1792]{2,1,0:T(2,128)(2,1)S(1)}, u32[]{:S(2)}, u32[]{:S(2)}) %all-to-all-start) | async-done | bytes 114720 | tf_op jit(solution)/shard_map/all_to_all | solution.py:179
  25.7 0.1 reshape.109
  25.8 0.7 %reduce = bf16[64,896]{1,0:T(8,128)(2,1)S(1)} reduce(bf16[64,1,896]{2,1,0:T(2,128)(2,1)S(1)} %reshape.109, bf16[]{:T(256)} %constant.19), dimensions={1}, to_apply=%all_to_all.13.reduce_sub_computation | reduce | bytes 229378 | tf_op jit(solution)/shard_map/all_to_all | solution.py:179
  26.5 0.2 copy.68
  26.7 4.5 %collective-permute-start.2 = (bf16[4,10,896]{2,1,0:T(8,128)(2,1)S(1)}, bf16[4,10,896]{2,1,0:T(8,128)(2,1)S(1)}, u32[]{:S(2)}, u32[]{:S(2)}) collective-permute-start(bf16[4,10,896]{2,1,0:T(8,128)(2,1)S(1)} %get-tuple-element.5), channel_id=1, source_target_pairs={{0,16},{1,17},{2,18},{3,19},{4,20},{5,21},{6,22},{7,23},{8,24},{9,... | collective-permute-start | bytes 215048 | tf_op jit(solution)/shard_map/ppermute | solution.py:18
  31.3 1.3 %collective-permute-start.3 = (bf16[4,10,896]{2,1,0:T(8,128)(2,1)S(1)}, bf16[4,10,896]{2,1,0:T(8,128)(2,1)S(1)}, u32[]{:S(2)}, u32[]{:S(2)}) collective-permute-start(bf16[4,10,896]{2,1,0:T(8,128)(2,1)S(1)} %get-tuple-element.6), channel_id=1, source_target_pairs={{16,0},{17,1},{18,2},{19,3},{20,4},{21,5},{22,6},{23,7},{24,8},{25... | collective-permute-start | bytes 215048 | tf_op jit(solution)/shard_map/ppermute | solution.py:21
  32.6 0.1 copy.47
  32.7 0.7 %convert_element_type.39.offset_ref = s32[140]{0:T(256)} reshape(s32[1,20,7]{2,1,0:T(8,128)S(1)} %copy.47) | data formatting | bytes 1120 | tf_op jit(solution)/shard_map/convert_element_type | solution.py:192
  33.4 0.1 copy.48
  33.5 0.7 %reshape_squeeze.3.weight_ref = f32[140]{0:T(256)} reshape(f32[1,20,7]{2,1,0:T(8,128)S(1)} %copy.48) | data formatting | bytes 1120 | tf_op jit(solution)/shard_map/reshape;squeeze | solution.py:136
  34.1 0.0 collective-permute-done.2
  34.1 0.1 copy.54
  34.2 3.7 %collective-permute-done.3 = bf16[4,10,896]{2,1,0:T(8,128)(2,1)S(1)} collective-permute-done((bf16[4,10,896]{2,1,0:T(8,128)(2,1)S(1)}, bf16[4,10,896]{2,1,0:T(8,128)(2,1)S(1)}, u32[]{:S(2)}, u32[]{:S(2)}) %collective-permute-start.3) | collective-permute-done | bytes 71712 | tf_op jit(solution)/shard_map/ppermute | solution.py:21
  38.0 0.1 copy.55
  38.1 1.5 %maximum_convert_fusion.ext_ref = f32[4,36,1,896]{3,2,1,0:T(1,128)} fusion(bf16[4,10,1,896]{3,2,1,0:T(2,128)(2,1)S(1)} %copy.55, bf16[4,16,1,896]{3,2,1,0:T(2,128)(2,1)S(1)} %bitcast.26, bf16[4,10,1,896]{3,2,1,0:T(2,128)(2,1)S(1)} %copy.54), kind=kLoop, calls=%fused_computation.2 | loop fusion | flops 387072 | bytes 774144 | tf_op jit(solution)/shard_map/convert_element_type | solution.py:138
  39.6 11.8 %shard_map.100 = bf16[4,16,896]{2,1,0:T(8,128)(2,1)} custom-call(s32[140]{0:T(256)} %convert_element_type.39.offset_ref, f32[140]{0:T(256)} %reshape_squeeze.3.weight_ref, s32[2]{0:T(128)} %pad_add_fusion.bounds_ref, f32[4,36,1,896]{3,2,1,0:T(1,128)} %maximum_convert_fusion.ext_ref, bf16[32,16]{1,0:T(8,128)(2,1)} %pad.4.w1_ref, ...), custom_call_target="tpu_custom_call" | custom-call | tf_op jit(solution)/shard_map/pallas_call | solution.py:130
  (7 shorter events, 0.2 us)
Async XLA Ops:
  0.0 8.8 %copy-start = (bf16[896,896]{1,0:T(8,128)(2,1)S(1)}, bf16[896,896]{1,0:T(8,128)(2,1)}, u32[]{:S(2)}) copy-start(bf16[896,896]{1,0:T(8,128)(2,1)} %param.14) | copy-start | bytes 4816900
  1.6 19.1 %collective-permute-start = (f32[2,2,7]{1,2,0:T(8,128)S(1)}, f32[2,2,7]{1,2,0:T(8,128)S(1)}, u32[]{:S(2)}, u32[]{:S(2)}) collective-permute-start(f32[2,2,7]{1,2,0:T(8,128)S(1)} %get-tuple-element.9), channel_id=1, source_target_pairs={{0,16},{1,17},{2,18},{3,19},{4,20},{5,21},{6,22},{7,23},{8,24},{9,... | collective-permute-start | bytes 344 | tf_op jit(solution)/shard_map/ppermute | solution.py:18
  6.5 14.3 %collective-permute-start.1 = (f32[2,2,7]{1,2,0:T(8,128)S(1)}, f32[2,2,7]{1,2,0:T(8,128)S(1)}, u32[]{:S(2)}, u32[]{:S(2)}) collective-permute-start(f32[2,2,7]{1,2,0:T(8,128)S(1)} %get-tuple-element.10), channel_id=1, source_target_pairs={{16,0},{17,1},{18,2},{19,3},{20,4},{21,5},{22,6},{23,7},{24,8},{25... | collective-permute-start | bytes 344 | tf_op jit(solution)/shard_map/ppermute | solution.py:21
  8.7 9.3 %copy-start.1 = (bf16[32,32,3,3]{1,0,3,2:T(8,128)(2,1)S(1)}, bf16[32,32,3,3]{1,0,3,2:T(8,128)(2,1)}, u32[]{:S(2)}) copy-start(bf16[32,32,3,3]{1,0,3,2:T(8,128)(2,1)} %param.18) | copy-start | bytes 55300
  8.8 10.0 %copy-start.3 = (bf16[32,3,3]{0,2,1:T(4,128)(2,1)S(1)}, bf16[32,3,3]{0,2,1:T(4,128)(2,1)}, u32[]{:S(2)}) copy-start(bf16[32,3,3]{0,2,1:T(4,128)(2,1)} %param.17) | copy-start | bytes 1732
  8.8 10.1 %copy-start.4 = (bf16[32]{0:T(256)(128)(2,1)S(1)}, bf16[32]{0:T(256)(128)(2,1)}, u32[]{:S(2)}) copy-start(bf16[32]{0:T(256)(128)(2,1)} %param.19) | copy-start | bytes 196
  8.8 11.9 %copy-start.2 = (f32[16,7]{0,1:T(8,128)S(1)}, f32[16,7]{0,1:T(8,128)}, u32[]{:S(2)}) copy-start(f32[16,7]{0,1:T(8,128)} %param.16) | copy-start | bytes 1348
  12.1 13.6 %all-to-all-start = ((bf16[16,2,1792]{2,1,0:T(2,128)(2,1)}), bf16[16,2,1792]{2,1,0:T(2,128)(2,1)S(1)}, u32[]{:S(2)}, u32[]{:S(2)}) async-start(bf16[16,2,1792]{2,1,0:T(2,128)(2,1)} %reshape.108), calls=%async_computation | async-start | bytes 229376 | tf_op jit(solution)/shard_map/all_to_all | solution.py:179
  26.7 7.4 %collective-permute-start.2 = (bf16[4,10,896]{2,1,0:T(8,128)(2,1)S(1)}, bf16[4,10,896]{2,1,0:T(8,128)(2,1)S(1)}, u32[]{:S(2)}, u32[]{:S(2)}) collective-permute-start(bf16[4,10,896]{2,1,0:T(8,128)(2,1)S(1)} %get-tuple-element.5), channel_id=1, source_target_pairs={{0,16},{1,17},{2,18},{3,19},{4,20},{5,21},{6,22},{7,23},{8,24},{9,... | collective-permute-start | bytes 215048 | tf_op jit(solution)/shard_map/ppermute | solution.py:18
  31.3 6.7 %collective-permute-start.3 = (bf16[4,10,896]{2,1,0:T(8,128)(2,1)S(1)}, bf16[4,10,896]{2,1,0:T(8,128)(2,1)S(1)}, u32[]{:S(2)}, u32[]{:S(2)}) collective-permute-start(bf16[4,10,896]{2,1,0:T(8,128)(2,1)S(1)} %get-tuple-element.6), channel_id=1, source_target_pairs={{16,0},{17,1},{18,2},{19,3},{20,4},{21,5},{22,6},{23,7},{24,8},{25... | collective-permute-start | bytes 215048 | tf_op jit(solution)/shard_map/ppermute | solution.py:21

commit v4 on v3

--- a/solution.py
+++ b/solution.py
@@ -9,17 +9,6 @@
 
 REACH = 8
 RIM = 2
-
-
-def halo_exchange(block, axis, dim, width):
-    count = lax.axis_size(axis)
-    forward = [(i, i + 1) for i in range(count - 1)]
-    backward = [(target, source) for source, target in forward]
-    low = lax.ppermute(
-        lax.slice_in_dim(block, block.shape[dim] - width, None, axis=dim), axis, forward
-    )
-    high = lax.ppermute(lax.slice_in_dim(block, 0, width, axis=dim), axis, backward)
-    return low, high
 
 
 def conv_kernel(
@@ -176,21 +165,47 @@
     kern_last,
 ):
     projected = resample(prepare(mantissa, exponent, poly_square, poly_cube), col_map)
-    row_major = lax.all_to_all(projected, "dev", split_axis=0, concat_axis=1, tiled=True)
-    row_count, view_count = (row_major.shape[0], row_major.shape[1])
-    group_idx = lax.axis_index("group")
-    total_views = view_count * lax.axis_size("group")
-    view_start = group_idx * view_count
+    lead_rows, _, width = projected.shape
+    group_count = lax.axis_size("group")
+    dev_count = lax.axis_size("dev")
+    row_count = lead_rows // dev_count
+    block_count = rebin_offset.shape[1]
+    view_count = rebin_offset.shape[0]
+    total_views = view_count * group_count
+    view_start = lax.axis_index("group") * view_count
+
+    own = lax.axis_index("dev")
+    own_offset = lax.dynamic_slice_in_dim(rebin_offset, own, 1, axis=0).astype(jnp.float32)
+    own_weight = lax.dynamic_slice_in_dim(rebin_weight, own, 1, axis=0)
+    weight_high = lax.reduce_precision(own_weight, exponent_bits=8, mantissa_bits=7)
+    rest = own_weight - weight_high
+    weight_mid = lax.reduce_precision(rest, exponent_bits=8, mantissa_bits=7)
+    weight_low = rest - weight_mid
+    param_row = jnp.concatenate([own_offset, weight_high, weight_mid, weight_low], axis=1)
+    param_row = param_row.astype(jnp.bfloat16)
+    param_row = jnp.pad(param_row, ((0, 0), (0, width - 4 * block_count)))
+    chunk = jnp.concatenate(
+        [
+            projected.reshape(dev_count, row_count, width),
+            jnp.broadcast_to(param_row[None], (dev_count, 1, width)),
+        ],
+        axis=1,
+    )
+    chunk = jnp.broadcast_to(chunk[None], (group_count,) + chunk.shape)
+    chunk = chunk.reshape(group_count * dev_count, row_count + 1, width)
+    received = lax.all_to_all(chunk, ("group", "dev"), 0, 0, tiled=True)
+
     halo = REACH + RIM
-
-    params = jnp.stack([rebin_offset.astype(jnp.float32), rebin_weight], axis=0)
-    low, high = halo_exchange(row_major, "group", 1, halo)
-    params_low, params_high = halo_exchange(params, "group", 1, RIM)
-    extended = jnp.concatenate([low, row_major, high], axis=1)
-    params_ext = jnp.concatenate([params_low, params, params_high], axis=1)
-
-    offsets = params_ext[0].astype(jnp.int32)
-    weights = params_ext[1]
+    views = jnp.pad(received[:, :row_count], ((halo, halo), (0, 0), (0, 0)))
+    views = lax.dynamic_slice_in_dim(views, view_start, view_count + 2 * halo, axis=0)
+    extended = jnp.transpose(views, (1, 0, 2))
+    params = received[:, row_count, : 4 * block_count].astype(jnp.float32)
+    params = jnp.pad(params, ((RIM, RIM), (0, 0)))
+    params = lax.dynamic_slice_in_dim(params, view_start, view_count + 2 * RIM, axis=0)
+    offsets = params[:, :block_count].astype(jnp.int32)
+    weights = params[:, block_count : 2 * block_count] + (
+        params[:, 2 * block_count : 3 * block_count] + params[:, 3 * block_count :]
+    )
     bounds = jnp.stack([view_start, total_views]).astype(jnp.int32)
     return rebin_dual(extended, offsets, weights, bounds, kern_first, kern_second, kern_last)
 

time: 51.8 us -> 42.2 us (0.81)
  starting transfers between devices: 17.9 us -> 7.3 us
  other arithmetic: 5.79 us -> 1.8 us
  waiting for transfers between devices: 8.54 us -> 11.7 us
  local copies, waits for them, and re-layouts: 5.81 us -> 7.85 us
    ppermute x4 -> x0, starting transfers between devices: 12 us -> none  [the longest x2 9.41 us: halo_exchange(): lax.ppermute(lax.slice_in_dim(block, block.shape[dim] - width, None, axis...]
    all_to_all x1, waiting for transfers between devices: 4.82 us -> 11.7 us  [local(): received = lax.all_to_all(chunk, ('group', 'dev'), 0, 0, tiled=True)]
    ppermute x4 -> x0, waiting for transfers between devices: 3.72 us -> none  [the longest x2 3.72 us: halo_exchange(): lax.ppermute(lax.slice_in_dim(block, 0, width, axis=dim), axis, backward)]
    reshape x1 -> x3, local copies, waits for them, and re-layouts: 0.51 us -> 2.59 us  [the longest x1 1.32 us: rebin_dual(): extended.astype(jnp.float32).reshape(rows, ext_views, 1, width)]
    dynamic_slice x0 -> x2, local copies, waits for them, and re-layouts: none -> 1.64 us  [the longest x1 0.88 us: local(): own_weight = lax.dynamic_slice_in_dim(rebin_weight, own, 1, axis=0)]
    another operation x2, other arithmetic: 1.64 us -> 0.02 us  [local(): params = jnp.stack([rebin_offset.astype(jnp.float32), rebin_weight], axis=0)]
    convert_element_type x1 -> x0, other arithmetic: 1.49 us -> none  [rebin_dual(): extended.astype(jnp.float32).reshape(rows, ext_views, 1, width)]
    all_to_all x1, starting transfers between devices: 5.91 us -> 7.3 us  [local(): received = lax.all_to_all(chunk, ('group', 'dev'), 0, 0, tiled=True)]
  transfers between devices with their start and end apart: 5 -> 1, of which waited for: 2 -> 1; matrix products, arithmetic and copies ran while one was open for 17% -> 7% of each run, Pallas kernels for 0% -> 0%
where the time goes in v4:
time: 42.2 us; the launch traced here: 41.8 us
  Pallas kernels  11.8 us (28%)
  waiting for transfers between devices  11.7 us (28%)
  local copies, waits for them, and re-layouts  7.85 us (19%)
  starting transfers between devices  7.3 us (17%)
  other arithmetic  1.8 us (4%)
  matrix products  1.3 us (3%)
    pallas_call x1, Pallas kernels, rebin_dual(): pl.pallas_call(kernel, out_shape=jax.ShapeDtypeStruct((rows, out_views, w...  11.8 us
    all_to_all x1, waiting for transfers between devices, local(): received = lax.all_to_all(chunk, ('group', 'dev'), 0, 0, tiled=True)  11.7 us
    all_to_all x1, starting transfers between devices, local(): received = lax.all_to_all(chunk, ('group', 'dev'), 0, 0, tiled=True)  7.3 us
    reshape x1, local copies, waits for them, and re-layouts, rebin_dual(): extended.astype(jnp.float32).reshape(rows, ext_views, 1, width)  1.32 us
    dot_general x1, matrix products, resample(): product = jnp.dot(flat, col_map, preferred_element_type=jnp.float32)  1.3 us
    dynamic_slice x1, local copies, waits for them, and re-layouts, local(): own_weight = lax.dynamic_slice_in_dim(rebin_weight, own, 1, axis=0)  0.88 us
  transfers between devices with their start and end apart: 1, of which 1 were waited for; matrix products, arithmetic and copies ran while one was open for 7% of the time, Pallas kernels for 0%

profile of v4, /device:TPU:0, one launch (start us, length us, event | category | flops | bytes accessed | tf_op | source)
XLA Modules:
  0.0 41.8 jit_solution(7863198531319228010)
XLA Ops:
  0.0 0.0 copy-start
  0.0 0.9 %constant_dynamic-slice_fusion = f32[1,7]{0,1:T(8,128)S(1)} fusion(f32[16,7]{0,1:T(8,128)} %param.16, s32[]{:T(128)S(6)} %select_n.10), kind=kLoop, calls=%fused_computation.22 | loop fusion | bytes 60 | tf_op jit(solution)/shard_map/dynamic_slice | solution.py:179
  0.9 0.1 copy.38
  1.0 0.8 %constant_dynamic-slice_fusion.1 = s32[1,7]{0,1:T(8,128)S(1)} fusion(s32[16,7]{0,1:T(8,128)} %param.15, s32[]{:T(128)S(6)} %select_n.10), kind=kLoop, calls=%fused_computation.23 | loop fusion | bytes 60 | tf_op jit(solution)/shard_map/dynamic_slice | solution.py:178
  1.7 0.1 copy.37
  1.9 0.7 %multiply_exponential_fusion = f32[64,1,7]{0,1,2:T(1,128)S(1)} fusion(s32[64,1,7]{0,1,2:T(1,128)} %param.11), kind=kLoop, calls=%fused_computation.21 | loop fusion | flops 1344 | bytes 3584 | tf_op jit(solution)/shard_map/exp2 | solution.py:140
  2.5 0.1 copy.36
  2.6 0.1 mul.55
  2.8 0.0 copy-done
  2.8 1.3 %convolution_convert_fusion = bf16[64,896]{1,0:T(8,128)(2,1)S(1)} fusion(bf16[896,896]{1,0:T(8,128)(2,1)S(1)} %copy-done, f32[64,1,896]{2,0,1:T(8,128)S(1)} %mul.56, bf16[64,1,896]{2,0,1:T(8,128)(2,1)} %param.10, f32[896]{0:T(1024)} %param.13, f32[896]{0:T(1024)} %param.12), kind=kOutput, calls=%fused_computation | convolution fusion | flops 103448576 | bytes 2071552 | tf_op jit(solution)/shard_map/dot_general | solution.py:151
  4.1 0.0 copy-start.1
  4.2 0.0 copy-start.2
  4.2 0.0 copy-start.3
  4.2 0.1 fusion.7
  4.4 0.1 pad_maximum_fusion
  4.5 0.8 %broadcast_in_dim.8 = bf16[2,16,5,896]{3,2,1,0:T(8,128)(2,1)} broadcast(bf16[16,5,896]{2,1,0:T(8,128)(2,1)S(1)} %pad_maximum_fusion), dimensions={1,2,3} | broadcast | bytes 430080 | tf_op jit(solution)/shard_map/broadcast_in_dim | solution.py:194
  5.3 7.3 %all-to-all-start = ((bf16[32,5,896]{2,1,0:T(8,128)(2,1)}), bf16[32,5,896]{2,1,0:T(8,128)(2,1)S(1)}, u32[]{:S(2)}, u32[]{:S(2)}) async-start(bf16[32,5,896]{2,1,0:T(8,128)(2,1)} %bitcast.2), calls=%async_computation | async-start | bytes 917504 | tf_op jit(solution)/shard_map/all_to_all | solution.py:196
  12.6 0.0 copy-done.1
  12.6 0.1 copy.33
  12.7 0.7 %reshape.131.w2_ref = bf16[32,288]{1,0:T(8,128)(2,1)} reshape(bf16[32,3,3,32]{3,2,1,0:T(4,128)(2,1)S(1)} %copy.33) | data formatting | bytes 36864 | tf_op jit(solution)/shard_map/reshape | solution.py:94
  13.4 0.0 copy-done.2
  13.4 0.1 copy.32
  13.5 0.0 copy-done.3
  13.5 0.7 %copy.35.kl_ref = f32[32,1]{1,0:T(8,128)} copy(f32[32,1]{0,1:T(1,128)S(1)} %bitcast_convert_fusion) | data formatting | bytes 256 | tf_op jit(solution)/shard_map/reshape | solution.py:95
  14.2 0.6 %pad.23.w1_ref = bf16[32,16]{1,0:T(8,128)(2,1)} pad(bf16[32,9]{1,0:T(8,128)(2,1)S(1)} %copy.32, bf16[]{:T(256)} %constant.19.clone.1), padding=0_0x0_7 | pad | bytes 1602 | tf_op jit(solution)/shard_map/jit(_pad)/pad | solution.py:93
  14.8 0.6 %pad_add_fusion.bounds_ref = s32[2]{0:T(128)} fusion(s32[1]{0:T(128)} %constant.23.clone.1, s32[1]{0:T(128)} %bitcast.4), kind=kLoop, calls=%fused_computation.29 | loop fusion | flops 2 | bytes 16 | tf_op jit(solution)/shard_map/stack | solution.py:209
  15.4 11.7 %all-to-all-done = bf16[32,5,896]{2,1,0:T(8,128)(2,1)S(1)} async-done(((bf16[32,5,896]{2,1,0:T(8,128)(2,1)}), bf16[32,5,896]{2,1,0:T(8,128)(2,1)S(1)}, u32[]{:S(2)}, u32[]{:S(2)}) %all-to-all-start) | async-done | bytes 286752 | tf_op jit(solution)/shard_map/all_to_all | solution.py:196
  27.2 0.1 fusion.5
  27.2 0.6 %reshape.126.offset_ref = s32[140]{0:T(256)} reshape(s32[20,7]{1,0:T(8,128)S(1)} %get-tuple-element.6) | data formatting | bytes 1120 | tf_op jit(solution)/shard_map/reshape | solution.py:124
  27.9 0.6 %reshape.127.weight_ref = f32[140]{0:T(256)} reshape(f32[20,7]{1,0:T(8,128)S(1)} %get-tuple-element.5) | data formatting | bytes 1120 | tf_op jit(solution)/shard_map/reshape | solution.py:125
  28.5 0.1 slice.29
  28.6 0.1 convert_bitcast_fusion
  28.7 1.3 %copy.34.ext_ref = f32[4,36,1,896]{3,2,1,0:T(1,128)} copy(f32[4,36,1,896]{3,0,1,2:T(4,128)S(1)} %convert_bitcast_fusion) | data formatting | bytes 1032192 | tf_op jit(solution)/shard_map/reshape | solution.py:127
  30.1 11.8 %shard_map.100 = bf16[4,16,896]{2,1,0:T(8,128)(2,1)} custom-call(s32[140]{0:T(256)} %reshape.126.offset_ref, f32[140]{0:T(256)} %reshape.127.weight_ref, s32[2]{0:T(128)} %pad_add_fusion.bounds_ref, f32[4,36,1,896]{3,2,1,0:T(1,128)} %copy.34.ext_ref, bf16[32,16]{1,0:T(8,128)(2,1)} %pad.23.w1_ref, bf16[32,288]{1,0:T(8,128)(2,1)} %reshape.131.w2_ref, ...), custom_call_target="tpu_custom_call" | custom-call | tf_op jit(solution)/shard_map/pallas_call | solution.py:119
  (10 shorter events, 0.2 us)
Async XLA Ops:
  0.0 2.8 %copy-start = (bf16[896,896]{1,0:T(8,128)(2,1)S(1)}, bf16[896,896]{1,0:T(8,128)(2,1)}, u32[]{:S(2)}) copy-start(bf16[896,896]{1,0:T(8,128)(2,1)} %param.14) | copy-start | bytes 4816900
  4.1 8.4 %copy-start.1 = (bf16[32,32,3,3]{1,0,3,2:T(8,128)(2,1)S(1)}, bf16[32,32,3,3]{1,0,3,2:T(8,128)(2,1)}, u32[]{:S(2)}) copy-start(bf16[32,32,3,3]{1,0,3,2:T(8,128)(2,1)} %param.18) | copy-start | bytes 55300
  4.2 9.2 %copy-start.2 = (bf16[32,3,3]{0,2,1:T(4,128)(2,1)S(1)}, bf16[32,3,3]{0,2,1:T(4,128)(2,1)}, u32[]{:S(2)}) copy-start(bf16[32,3,3]{0,2,1:T(4,128)(2,1)} %param.17) | copy-start | bytes 1732
  4.2 9.3 %copy-start.3 = (bf16[32]{0:T(256)(128)(2,1)S(1)}, bf16[32]{0:T(256)(128)(2,1)}, u32[]{:S(2)}) copy-start(bf16[32]{0:T(256)(128)(2,1)} %param.19) | copy-start | bytes 196
  5.3 21.8 %all-to-all-start = ((bf16[32,5,896]{2,1,0:T(8,128)(2,1)}), bf16[32,5,896]{2,1,0:T(8,128)(2,1)S(1)}, u32[]{:S(2)}, u32[]{:S(2)}) async-start(bf16[32,5,896]{2,1,0:T(8,128)(2,1)} %bitcast.2), calls=%async_computation | async-start | bytes 917504 | tf_op jit(solution)/shard_map/all_to_all | solution.py:196

commit v5 on v4

--- a/solution.py
+++ b/solution.py
@@ -174,40 +174,51 @@
     total_views = view_count * group_count
     view_start = lax.axis_index("group") * view_count
 
-    own = lax.axis_index("dev")
-    own_offset = lax.dynamic_slice_in_dim(rebin_offset, own, 1, axis=0).astype(jnp.float32)
-    own_weight = lax.dynamic_slice_in_dim(rebin_weight, own, 1, axis=0)
-    weight_high = lax.reduce_precision(own_weight, exponent_bits=8, mantissa_bits=7)
-    rest = own_weight - weight_high
+    weight_high = lax.reduce_precision(rebin_weight, exponent_bits=8, mantissa_bits=7)
+    rest = rebin_weight - weight_high
     weight_mid = lax.reduce_precision(rest, exponent_bits=8, mantissa_bits=7)
     weight_low = rest - weight_mid
-    param_row = jnp.concatenate([own_offset, weight_high, weight_mid, weight_low], axis=1)
-    param_row = param_row.astype(jnp.bfloat16)
-    param_row = jnp.pad(param_row, ((0, 0), (0, width - 4 * block_count)))
-    chunk = jnp.concatenate(
-        [
-            projected.reshape(dev_count, row_count, width),
-            jnp.broadcast_to(param_row[None], (dev_count, 1, width)),
-        ],
-        axis=1,
-    )
-    chunk = jnp.broadcast_to(chunk[None], (group_count,) + chunk.shape)
-    chunk = chunk.reshape(group_count * dev_count, row_count + 1, width)
-    received = lax.all_to_all(chunk, ("group", "dev"), 0, 0, tiled=True)
-
+    param_block = jnp.concatenate(
+        [rebin_offset.astype(jnp.float32), weight_high, weight_mid, weight_low], axis=1
+    )
+    param_size = view_count * 4 * block_count
+    param_rows = -(-param_size // width)
+    param_block = jnp.pad(param_block.reshape(-1), (0, param_rows * width - param_size))
+    param_block = param_block.astype(jnp.bfloat16).reshape(1, param_rows, width)
+
+    pieces = 1
+    piece_rows = row_count // pieces
+    by_dest = projected.reshape(dev_count, row_count, width)
     halo = REACH + RIM
-    views = jnp.pad(received[:, :row_count], ((halo, halo), (0, 0), (0, 0)))
-    views = lax.dynamic_slice_in_dim(views, view_start, view_count + 2 * halo, axis=0)
-    extended = jnp.transpose(views, (1, 0, 2))
-    params = received[:, row_count, : 4 * block_count].astype(jnp.float32)
-    params = jnp.pad(params, ((RIM, RIM), (0, 0)))
-    params = lax.dynamic_slice_in_dim(params, view_start, view_count + 2 * RIM, axis=0)
-    offsets = params[:, :block_count].astype(jnp.int32)
-    weights = params[:, block_count : 2 * block_count] + (
-        params[:, 2 * block_count : 3 * block_count] + params[:, 3 * block_count :]
-    )
-    bounds = jnp.stack([view_start, total_views]).astype(jnp.int32)
-    return rebin_dual(extended, offsets, weights, bounds, kern_first, kern_second, kern_last)
+    outputs = []
+    params = None
+    for piece in range(pieces):
+        part = by_dest[:, piece * piece_rows : (piece + 1) * piece_rows]
+        if piece == 0:
+            part = jnp.concatenate(
+                [part, jnp.broadcast_to(param_block, (dev_count, param_rows, width))], axis=1
+            )
+        part = jnp.broadcast_to(part[None], (group_count,) + part.shape)
+        part = part.reshape((group_count * dev_count,) + part.shape[2:])
+        received = lax.all_to_all(part, ("group", "dev"), 0, 0, tiled=True)
+        if piece == 0:
+            table = received.reshape(group_count, dev_count, -1, width)[:, 0, piece_rows:]
+            table = table.reshape(group_count, -1)[:, :param_size].astype(jnp.float32)
+            table = table.reshape(total_views, 4 * block_count)
+            table = jnp.pad(table, ((RIM, RIM), (0, 0)))
+            params = lax.dynamic_slice_in_dim(table, view_start, view_count + 2 * RIM, axis=0)
+        views = jnp.pad(received[:, :piece_rows], ((halo, halo), (0, 0), (0, 0)))
+        views = lax.dynamic_slice_in_dim(views, view_start, view_count + 2 * halo, axis=0)
+        extended = jnp.transpose(views, (1, 0, 2))
+        offsets = params[:, :block_count].astype(jnp.int32)
+        weights = params[:, block_count : 2 * block_count] + (
+            params[:, 2 * block_count : 3 * block_count] + params[:, 3 * block_count :]
+        )
+        bounds = jnp.stack([view_start, total_views]).astype(jnp.int32)
+        outputs.append(
+            rebin_dual(extended, offsets, weights, bounds, kern_first, kern_second, kern_last)
+        )
+    return jnp.concatenate(outputs, axis=0) if pieces > 1 else outputs[0]
 
 
 def solution(mesh):

time: 42.2 us -> 42.2 us (level)
  local copies, waits for them, and re-layouts: 7.85 us -> 6.36 us
  other arithmetic: 1.8 us -> 3.23 us
    dynamic_slice x2 -> x0, local copies, waits for them, and re-layouts: 1.64 us -> none  [the longest x1 0.88 us: local(): own_weight = lax.dynamic_slice_in_dim(rebin_weight, own, 1, axis=0)]
    another operation x2, other arithmetic: 0.02 us -> 1.5 us
where the time goes in v5:
time: 42.2 us; the launch traced here: 41.8 us
  Pallas kernels  11.8 us (28%)
  waiting for transfers between devices  11.6 us (27%)
  starting transfers between devices  7.3 us (17%)
  local copies, waits for them, and re-layouts  6.36 us (15%)
  other arithmetic  3.23 us (8%)
  matrix products  1.3 us (3%)
    pallas_call x1, Pallas kernels, rebin_dual(): pl.pallas_call(kernel, out_shape=jax.ShapeDtypeStruct((rows, out_views, w...  11.8 us
    all_to_all x1, waiting for transfers between devices, local(): received = lax.all_to_all(part, ('group', 'dev'), 0, 0, tiled=True)  11.6 us
    all_to_all x1, starting transfers between devices, local(): received = lax.all_to_all(part, ('group', 'dev'), 0, 0, tiled=True)  7.3 us
    another operation x2, other arithmetic  1.5 us
    reshape x1, local copies, waits for them, and re-layouts, rebin_dual(): extended.astype(jnp.float32).reshape(rows, ext_views, 1, width)  1.32 us
    dot_general x1, matrix products, resample(): product = jnp.dot(flat, col_map, preferred_element_type=jnp.float32)  1.3 us
  transfers between devices with their start and end apart: 1, of which 1 were waited for; matrix products, arithmetic and copies ran while one was open for 7% of the time, Pallas kernels for 0%

profile of v5, /device:TPU:0, one launch (start us, length us, event | category | flops | bytes accessed | tf_op | source)
XLA Modules:
  0.0 41.8 jit_solution(16106506084000917221)
XLA Ops:
  0.0 0.0 copy-start
  0.0 0.8 %reduce-precision_convert_fusion.1 = (bf16[16,7]{0,1:T(8,128)(2,1)S(1)}, bf16[16,7]{0,1:T(8,128)(2,1)S(1)}, bf16[16,7]{0,1:T(8,128)(2,1)S(1)}) fusion(f32[16,7]{0,1:T(8,128)} %param.16), kind=kLoop, calls=%fused_computation.19 | loop fusion | flops 784 | bytes 1120 | tf_op jit(solution)/shard_map/convert.10
  0.8 0.7 %convert_convert_fusion = bf16[16,7]{0,1:T(8,128)(2,1)S(1)} fusion(s32[16,7]{0,1:T(8,128)} %param.15), kind=kLoop, calls=%fused_computation.21 | loop fusion | flops 224 | bytes 672 | tf_op jit(solution)/shard_map/convert.9
  1.5 0.1 copy.17
  1.6 0.1 reshape.83
  1.7 0.7 %multiply_exponential_fusion = f32[64,1,7]{0,1,2:T(1,128)S(1)} fusion(s32[64,1,7]{0,1,2:T(1,128)} %param.11), kind=kLoop, calls=%fused_computation.23 | loop fusion | flops 1344 | bytes 3584 | tf_op jit(solution)/shard_map/exp2 | solution.py:140
  2.4 0.1 copy.23
  2.5 0.1 mul.55
  2.7 0.0 copy-done
  2.7 1.3 %convolution_convert_fusion = bf16[64,896]{1,0:T(8,128)(2,1)S(1)} fusion(bf16[896,896]{1,0:T(8,128)(2,1)S(1)} %copy-done, f32[64,1,896]{2,0,1:T(8,128)S(1)} %mul.56, bf16[64,1,896]{2,0,1:T(8,128)(2,1)} %param.10, f32[896]{0:T(1024)} %param.13, f32[896]{0:T(1024)} %param.12), kind=kOutput, calls=%fused_computation | convolution fusion | flops 103448576 | bytes 2071552 | tf_op jit(solution)/shard_map/dot_general | solution.py:151
  4.0 0.0 copy-start.1
  4.0 0.0 copy-start.2
  4.0 0.0 copy-start.3
  4.1 0.1 pad_maximum_fusion
  4.3 0.8 %broadcast_in_dim.5 = bf16[2,16,5,896]{3,2,1,0:T(8,128)(2,1)} broadcast(bf16[16,5,896]{2,1,0:T(8,128)(2,1)S(1)} %pad_maximum_fusion), dimensions={1,2,3} | broadcast | bytes 430080 | tf_op jit(solution)/shard_map/broadcast_in_dim | solution.py:201
  5.1 7.3 %all-to-all-start = ((bf16[32,5,896]{2,1,0:T(8,128)(2,1)}), bf16[32,5,896]{2,1,0:T(8,128)(2,1)S(1)}, u32[]{:S(2)}, u32[]{:S(2)}) async-start(bf16[32,5,896]{2,1,0:T(8,128)(2,1)} %bitcast.2), calls=%async_computation | async-start | bytes 917504 | tf_op jit(solution)/shard_map/all_to_all | solution.py:203
  12.4 0.0 copy-done.1
  12.4 0.1 copy.20
  12.4 0.7 %reshape.92.w2_ref = bf16[32,288]{1,0:T(8,128)(2,1)} reshape(bf16[32,3,3,32]{3,2,1,0:T(4,128)(2,1)S(1)} %copy.20) | data formatting | bytes 36864 | tf_op jit(solution)/shard_map/reshape | solution.py:94
  13.2 0.0 copy-done.2
  13.2 0.1 copy.19
  13.3 0.6 %pad.24.w1_ref = bf16[32,16]{1,0:T(8,128)(2,1)} pad(bf16[32,9]{1,0:T(8,128)(2,1)S(1)} %copy.19, bf16[]{:T(256)} %constant.6.clone.1), padding=0_0x0_7 | pad | bytes 1602 | tf_op jit(solution)/shard_map/jit(_pad)/pad | solution.py:93
  13.9 0.0 copy-done.3
  13.9 0.7 %copy.22.kl_ref = f32[32,1]{1,0:T(8,128)} copy(f32[32,1]{0,1:T(1,128)S(1)} %bitcast_convert_fusion) | data formatting | bytes 256 | tf_op jit(solution)/shard_map/reshape | solution.py:95
  14.6 0.6 %pad_add_fusion.bounds_ref = s32[2]{0:T(128)} fusion(s32[1]{0:T(128)} %constant.20.clone.1, s32[1]{0:T(128)} %bitcast.5), kind=kLoop, calls=%fused_computation.24 | loop fusion | flops 2 | bytes 16 | tf_op jit(solution)/shard_map/stack | solution.py:217
  15.2 11.6 %all-to-all-done = bf16[32,5,896]{2,1,0:T(8,128)(2,1)S(1)} async-done(((bf16[32,5,896]{2,1,0:T(8,128)(2,1)}), bf16[32,5,896]{2,1,0:T(8,128)(2,1)S(1)}, u32[]{:S(2)}, u32[]{:S(2)}) %all-to-all-start) | async-done | bytes 286752 | tf_op jit(solution)/shard_map/all_to_all | solution.py:203
  26.9 0.1 reshape.86
  27.0 0.1 fusion.5
  27.1 0.6 %reshape.87.offset_ref = s32[140]{0:T(256)} reshape(s32[20,7]{1,0:T(8,128)S(1)} %get-tuple-element.6) | data formatting | bytes 1120 | tf_op jit(solution)/shard_map/reshape | solution.py:124
  27.8 0.7 %reshape.88.weight_ref = f32[140]{0:T(256)} reshape(f32[20,7]{1,0:T(8,128)S(1)} %get-tuple-element.5) | data formatting | bytes 1120 | tf_op jit(solution)/shard_map/reshape | solution.py:125
  28.4 0.1 slice.34
  28.5 0.1 convert_bitcast_fusion
  28.7 1.3 %copy.21.ext_ref = f32[4,36,1,896]{3,2,1,0:T(1,128)} copy(f32[4,36,1,896]{3,0,1,2:T(4,128)S(1)} %convert_bitcast_fusion) | data formatting | bytes 1032192 | tf_op jit(solution)/shard_map/reshape | solution.py:127
  30.0 11.8 %shard_map.100 = bf16[4,16,896]{2,1,0:T(8,128)(2,1)} custom-call(s32[140]{0:T(256)} %reshape.87.offset_ref, f32[140]{0:T(256)} %reshape.88.weight_ref, s32[2]{0:T(128)} %pad_add_fusion.bounds_ref, f32[4,36,1,896]{3,2,1,0:T(1,128)} %copy.21.ext_ref, bf16[32,16]{1,0:T(8,128)(2,1)} %pad.24.w1_ref, bf16[32,288]{1,0:T(8,128)(2,1)} %reshape.92.w2_ref, ...), custom_call_target="tpu_custom_call" | custom-call | tf_op jit(solution)/shard_map/pallas_call | solution.py:119
  (11 shorter events, 0.2 us)
Async XLA Ops:
  0.0 2.7 %copy-start = (bf16[896,896]{1,0:T(8,128)(2,1)S(1)}, bf16[896,896]{1,0:T(8,128)(2,1)}, u32[]{:S(2)}) copy-start(bf16[896,896]{1,0:T(8,128)(2,1)} %param.14) | copy-start | bytes 4816900
  4.0 8.4 %copy-start.1 = (bf16[32,32,3,3]{1,0,3,2:T(8,128)(2,1)S(1)}, bf16[32,32,3,3]{1,0,3,2:T(8,128)(2,1)}, u32[]{:S(2)}) copy-start(bf16[32,32,3,3]{1,0,3,2:T(8,128)(2,1)} %param.18) | copy-start | bytes 55300
  4.0 9.1 %copy-start.2 = (bf16[32,3,3]{0,2,1:T(4,128)(2,1)S(1)}, bf16[32,3,3]{0,2,1:T(4,128)(2,1)}, u32[]{:S(2)}) copy-start(bf16[32,3,3]{0,2,1:T(4,128)(2,1)} %param.17) | copy-start | bytes 1732
  4.0 9.9 %copy-start.3 = (bf16[32]{0:T(256)(128)(2,1)S(1)}, bf16[32]{0:T(256)(128)(2,1)}, u32[]{:S(2)}) copy-start(bf16[32]{0:T(256)(128)(2,1)} %param.19) | copy-start | bytes 196
  5.1 21.8 %all-to-all-start = ((bf16[32,5,896]{2,1,0:T(8,128)(2,1)}), bf16[32,5,896]{2,1,0:T(8,128)(2,1)S(1)}, u32[]{:S(2)}, u32[]{:S(2)}) async-start(bf16[32,5,896]{2,1,0:T(8,128)(2,1)} %bitcast.2), calls=%async_computation | async-start | bytes 917504 | tf_op jit(solution)/shard_map/all_to_all | solution.py:203

commit v6 on v5

--- a/solution.py
+++ b/solution.py
@@ -28,48 +28,68 @@
     block_count,
     col_block,
     channels,
+    fold,
 ):
     width = block_count * col_block
+    rows = sig_ref.shape[0]
     first_views = sig_views - 2
     out_views = sig_views - 4
     view_start = bounds_ref[0]
     total_views = bounds_ref[1]
-    lane = lax.broadcasted_iota(jnp.int32, (1, width), 1)
-    sig_ref[3 * sig_views :, :] = jnp.zeros((sig_ref.shape[0] - 3 * sig_views, width), jnp.float32)
-    for u in range(sig_views):
-        pos = view_start - RIM + u
-        keep = ((pos >= 0) & (pos < total_views)).astype(jnp.float32)
-        for k in range(block_count):
-            low = u + offset_ref[u * block_count + k] + REACH
-            frac = weight_ref[u * block_count + k]
-            cols = pl.ds(k * col_block, col_block)
-            lower = ext_ref[0, low, :, cols]
-            upper = ext_ref[0, low + 1, :, cols]
-            value = ((1.0 - frac) * lower + frac * upper).astype(jnp.bfloat16)
-            sig_ref[3 * u + 1 : 3 * u + 2, cols] = value.astype(jnp.float32) * keep
-        row = sig_ref[3 * u + 1 : 3 * u + 2, :]
-        sig_ref[3 * u : 3 * u + 1, :] = jnp.where(lane >= 1, pltpu.roll(row, 1, 1), 0.0)
-        sig_ref[3 * u + 2 : 3 * u + 3, :] = jnp.where(
-            lane < width - 1, pltpu.roll(row, width - 1, 1), 0.0
-        )
+    row = pl.program_id(0)
+
+    @pl.when(row == 0)
+    def _rebin():
+        lane = lax.broadcasted_iota(jnp.int32, (1, width), 1)
+        pad = sig_ref.shape[1] - 3 * sig_views
+        for r in range(rows):
+            sig_ref[r, 3 * sig_views :, :] = jnp.zeros((pad, width), jnp.float32)
+
+        def pick(view, cols):
+            tile = ext_ref[view // fold, :, cols]
+            part = view % fold
+            picked = tile[0:rows]
+            for f in range(1, fold):
+                picked = jnp.where(part == f, tile[f * rows : (f + 1) * rows], picked)
+            return picked
+
+        for u in range(sig_views):
+            pos = view_start - RIM + u
+            keep = ((pos >= 0) & (pos < total_views)).astype(jnp.float32)
+            for k in range(block_count):
+                low = u + offset_ref[u * block_count + k] + REACH
+                frac = weight_ref[u * block_count + k]
+                cols = pl.ds(k * col_block, col_block)
+                lower = pick(low, cols)
+                upper = pick(low + 1, cols)
+                value = ((1.0 - frac) * lower + frac * upper).astype(jnp.bfloat16)
+                value = value.astype(jnp.float32) * keep
+                for r in range(rows):
+                    sig_ref[r, 3 * u + 1 : 3 * u + 2, cols] = value[r : r + 1]
+            for r in range(rows):
+                line = sig_ref[r, 3 * u + 1 : 3 * u + 2, :]
+                sig_ref[r, 3 * u : 3 * u + 1, :] = jnp.where(lane >= 1, pltpu.roll(line, 1, 1), 0.0)
+                sig_ref[r, 3 * u + 2 : 3 * u + 3, :] = jnp.where(
+                    lane < width - 1, pltpu.roll(line, width - 1, 1), 0.0
+                )
+
     col = lax.broadcasted_iota(jnp.int32, (channels, width), 1)
     keep_left = col >= 1
     keep_right = col < width - 1
+    zero = jnp.zeros((channels, width), jnp.bfloat16)
     w1 = w1_ref[...]
     for u in range(first_views):
-        taps = sig_ref[3 * u : 3 * u + 16, :].astype(jnp.bfloat16)
+        taps = sig_ref[row, 3 * u : 3 * u + 16, :].astype(jnp.bfloat16)
         hidden = jnp.dot(w1, taps, preferred_element_type=jnp.float32)
         pos = view_start - 1 + u
         scale = ((pos >= 0) & (pos < total_views)).astype(jnp.float32)
-        hidden = jnp.maximum(hidden, 0.0) * scale
+        hidden = (jnp.maximum(hidden, 0.0) * scale).astype(jnp.bfloat16)
         base = 3 * u * channels
-        feat_ref[base : base + channels, :] = jnp.where(
-            keep_left, pltpu.roll(hidden, 1, 1), 0.0
-        ).astype(jnp.bfloat16)
-        feat_ref[base + channels : base + 2 * channels, :] = hidden.astype(jnp.bfloat16)
+        feat_ref[base : base + channels, :] = jnp.where(keep_left, pltpu.roll(hidden, 1, 1), zero)
+        feat_ref[base + channels : base + 2 * channels, :] = hidden
         feat_ref[base + 2 * channels : base + 3 * channels, :] = jnp.where(
-            keep_right, pltpu.roll(hidden, width - 1, 1), 0.0
-        ).astype(jnp.bfloat16)
+            keep_right, pltpu.roll(hidden, width - 1, 1), zero
+        )
     w2 = w2_ref[...]
     kl = kl_ref[...]
     for v in range(out_views):
@@ -77,18 +97,22 @@
         second = jnp.dot(w2, window, preferred_element_type=jnp.float32)
         second = jnp.maximum(second, 0.0).astype(jnp.bfloat16).astype(jnp.float32)
         mix = jnp.sum(kl * second, axis=0, keepdims=True)
-        centre = sig_ref[3 * (v + 2) + 1 : 3 * (v + 2) + 2, :]
+        centre = sig_ref[row, 3 * (v + 2) + 1 : 3 * (v + 2) + 2, :]
         dual_ref[v : v + 1, :] = centre + mix
     out_ref[0] = dual_ref[...].astype(out_ref.dtype)
 
 
-def rebin_dual(extended, offsets, weights, bounds, kern_first, kern_second, kern_last):
-    rows, ext_views, width = extended.shape
+def rebin_dual(views, offsets, weights, bounds, kern_first, kern_second, kern_last):
+    ext_views, rows, width = views.shape
     sig_views, block_count = offsets.shape
     col_block = width // block_count
     channels = kern_first.shape[0]
     first_views = sig_views - 2
     out_views = sig_views - 4
+    fold = 8 // rows if 8 % rows == 0 else 1
+    tiles = -(-ext_views // fold)
+    views = jnp.pad(views, ((0, tiles * fold - ext_views), (0, 0), (0, 0)))
+    ext = views.astype(jnp.float32).reshape(tiles, fold * rows, width)
     pad_rows = -(-(3 * first_views + 13) // 8) * 8
     w1 = jnp.pad(kern_first.reshape(channels, 9), ((0, 0), (0, 7)))
     w2 = jnp.transpose(kern_second, (0, 2, 3, 1)).reshape(channels, 9 * channels)
@@ -99,19 +123,20 @@
         block_count=block_count,
         col_block=col_block,
         channels=channels,
+        fold=fold,
     )
     grid_spec = pltpu.PrefetchScalarGridSpec(
         num_scalar_prefetch=3,
         grid=(rows,),
         in_specs=[
-            pl.BlockSpec((1, ext_views, 1, width), lambda r, *_: (r, 0, 0, 0)),
+            pl.BlockSpec((tiles, fold * rows, width), lambda r, *_: (0, 0, 0)),
             pl.BlockSpec((channels, 16), lambda r, *_: (0, 0)),
             pl.BlockSpec((channels, 9 * channels), lambda r, *_: (0, 0)),
             pl.BlockSpec((channels, 1), lambda r, *_: (0, 0)),
         ],
         out_specs=pl.BlockSpec((1, out_views, width), lambda r, *_: (r, 0, 0)),
         scratch_shapes=[
-            pltpu.VMEM((pad_rows, width), jnp.float32),
+            pltpu.VMEM((rows, pad_rows, width), jnp.float32),
             pltpu.VMEM((first_views * 3 * channels, width), jnp.bfloat16),
             pltpu.VMEM((out_views, width), jnp.float32),
         ],
@@ -120,11 +145,12 @@
         kernel,
         out_shape=jax.ShapeDtypeStruct((rows, out_views, width), jnp.bfloat16),
         grid_spec=grid_spec,
+        compiler_params=pltpu.CompilerParams(dimension_semantics=("arbitrary",)),
     )(
         offsets.reshape(-1),
         weights.reshape(-1),
         bounds,
-        extended.astype(jnp.float32).reshape(rows, ext_views, 1, width),
+        ext,
         w1.astype(jnp.bfloat16),
         w2.astype(jnp.bfloat16),
         kl,
@@ -209,14 +235,13 @@
             params = lax.dynamic_slice_in_dim(table, view_start, view_count + 2 * RIM, axis=0)
         views = jnp.pad(received[:, :piece_rows], ((halo, halo), (0, 0), (0, 0)))
         views = lax.dynamic_slice_in_dim(views, view_start, view_count + 2 * halo, axis=0)
-        extended = jnp.transpose(views, (1, 0, 2))
         offsets = params[:, :block_count].astype(jnp.int32)
         weights = params[:, block_count : 2 * block_count] + (
             params[:, 2 * block_count : 3 * block_count] + params[:, 3 * block_count :]
         )
         bounds = jnp.stack([view_start, total_views]).astype(jnp.int32)
         outputs.append(
-            rebin_dual(extended, offsets, weights, bounds, kern_first, kern_second, kern_last)
+            rebin_dual(views, offsets, weights, bounds, kern_first, kern_second, kern_last)
         )
     return jnp.concatenate(outputs, axis=0) if pieces > 1 else outputs[0]
 

time: 42.2 us -> 42.4 us (level)
  Pallas kernels: 11.8 us -> 12.3 us
    pallas_call x1, Pallas kernels: 11.8 us -> 12.3 us  [rebin_dual(): pl.pallas_call(kernel, out_shape=jax.ShapeDtypeStruct((rows, out_views, w...]
where the time goes in v6:
time: 42.4 us; the launch traced here: 42 us
  Pallas kernels  12.3 us (29%)
  waiting for transfers between devices  11.6 us (27%)
  starting transfers between devices  7.3 us (17%)
  local copies, waits for them, and re-layouts  6.03 us (14%)
  other arithmetic  3.23 us (8%)
  matrix products  1.3 us (3%)
    pallas_call x1, Pallas kernels, rebin_dual(): pl.pallas_call(kernel, out_shape=jax.ShapeDtypeStruct((rows, out_views, w...  12.3 us
    all_to_all x1, waiting for transfers between devices, local(): received = lax.all_to_all(part, ('group', 'dev'), 0, 0, tiled=True)  11.6 us
    all_to_all x1, starting transfers between devices, local(): received = lax.all_to_all(part, ('group', 'dev'), 0, 0, tiled=True)  7.3 us
    another operation x2, other arithmetic  1.5 us
    dot_general x1, matrix products, resample(): product = jnp.dot(flat, col_map, preferred_element_type=jnp.float32)  1.3 us
    reshape x1, local copies, waits for them, and re-layouts, rebin_dual(): ext = views.astype(jnp.float32).reshape(tiles, fold * rows, width)  0.97 us
  transfers between devices with their start and end apart: 1, of which 1 were waited for; matrix products, arithmetic and copies ran while one was open for 7% of the time, Pallas kernels for 0%

profile of v6, /device:TPU:0, one launch (start us, length us, event | category | flops | bytes accessed | tf_op | source)
XLA Modules:
  0.0 42.0 jit_solution(1432865741617152592)
XLA Ops:
  0.0 0.0 copy-start
  0.0 0.8 %reduce-precision_convert_fusion.1 = (bf16[16,7]{0,1:T(8,128)(2,1)S(1)}, bf16[16,7]{0,1:T(8,128)(2,1)S(1)}, bf16[16,7]{0,1:T(8,128)(2,1)S(1)}) fusion(f32[16,7]{0,1:T(8,128)} %param.16), kind=kLoop, calls=%fused_computation.19 | loop fusion | flops 784 | bytes 1120 | tf_op jit(solution)/shard_map/convert.9
  0.8 0.7 %convert_convert_fusion = bf16[16,7]{0,1:T(8,128)(2,1)S(1)} fusion(s32[16,7]{0,1:T(8,128)} %param.15), kind=kLoop, calls=%fused_computation.21 | loop fusion | flops 224 | bytes 672 | tf_op jit(solution)/shard_map/convert.8
  1.5 0.1 copy.28
  1.6 0.1 reshape.83
  1.7 0.7 %multiply_exponential_fusion = f32[64,1,7]{0,1,2:T(1,128)S(1)} fusion(s32[64,1,7]{0,1,2:T(1,128)} %param.11), kind=kLoop, calls=%fused_computation.23 | loop fusion | flops 1344 | bytes 3584 | tf_op jit(solution)/shard_map/exp2 | solution.py:166
  2.4 0.1 copy.33
  2.5 0.1 mul.55
  2.7 0.0 copy-done
  2.7 1.3 %convolution_convert_fusion = bf16[64,896]{1,0:T(8,128)(2,1)S(1)} fusion(bf16[896,896]{1,0:T(8,128)(2,1)S(1)} %copy-done, f32[64,1,896]{2,0,1:T(8,128)S(1)} %mul.56, bf16[64,1,896]{2,0,1:T(8,128)(2,1)} %param.10, f32[896]{0:T(1024)} %param.13, f32[896]{0:T(1024)} %param.12), kind=kOutput, calls=%fused_computation | convolution fusion | flops 103448576 | bytes 2071552 | tf_op jit(solution)/shard_map/dot_general | solution.py:177
  4.0 0.0 copy-start.1
  4.0 0.0 copy-start.2
  4.0 0.0 copy-start.3
  4.1 0.1 pad_maximum_fusion
  4.3 0.8 %broadcast_in_dim.5 = bf16[2,16,5,896]{3,2,1,0:T(8,128)(2,1)} broadcast(bf16[16,5,896]{2,1,0:T(8,128)(2,1)S(1)} %pad_maximum_fusion), dimensions={1,2,3} | broadcast | bytes 430080 | tf_op jit(solution)/shard_map/broadcast_in_dim | solution.py:227
  5.1 7.3 %all-to-all-start = ((bf16[32,5,896]{2,1,0:T(8,128)(2,1)}), bf16[32,5,896]{2,1,0:T(8,128)(2,1)S(1)}, u32[]{:S(2)}, u32[]{:S(2)}) async-start(bf16[32,5,896]{2,1,0:T(8,128)(2,1)} %bitcast.2), calls=%async_computation | async-start | bytes 917504 | tf_op jit(solution)/shard_map/all_to_all | solution.py:229
  12.4 0.0 copy-done.1
  12.4 0.1 copy.31
  12.4 0.7 %reshape.92.w2_ref = bf16[32,288]{1,0:T(8,128)(2,1)} reshape(bf16[32,3,3,32]{3,2,1,0:T(4,128)(2,1)S(1)} %copy.31) | data formatting | bytes 36864 | tf_op jit(solution)/shard_map/reshape | solution.py:118
  13.2 0.0 copy-done.2
  13.2 0.1 copy.30
  13.3 0.6 %pad.24.w1_ref = bf16[32,16]{1,0:T(8,128)(2,1)} pad(bf16[32,9]{1,0:T(8,128)(2,1)S(1)} %copy.30, bf16[]{:T(256)} %constant.6.clone.1), padding=0_0x0_7 | pad | bytes 1602 | tf_op jit(solution)/shard_map/jit(_pad)/pad | solution.py:117
  13.9 0.0 copy-done.3
  13.9 0.7 %copy.32.kl_ref = f32[32,1]{1,0:T(8,128)} copy(f32[32,1]{0,1:T(1,128)S(1)} %bitcast_convert_fusion) | data formatting | bytes 256 | tf_op jit(solution)/shard_map/reshape | solution.py:119
  14.6 0.6 %pad_add_fusion.bounds_ref = s32[2]{0:T(128)} fusion(s32[1]{0:T(128)} %constant.20.clone.1, s32[1]{0:T(128)} %bitcast.4), kind=kLoop, calls=%fused_computation.24 | loop fusion | flops 2 | bytes 16 | tf_op jit(solution)/shard_map/stack | solution.py:242
  15.2 11.6 %all-to-all-done = bf16[32,5,896]{2,1,0:T(8,128)(2,1)S(1)} async-done(((bf16[32,5,896]{2,1,0:T(8,128)(2,1)}), bf16[32,5,896]{2,1,0:T(8,128)(2,1)S(1)}, u32[]{:S(2)}, u32[]{:S(2)}) %all-to-all-start) | async-done | bytes 286752 | tf_op jit(solution)/shard_map/all_to_all | solution.py:229
  27.0 0.1 reshape.86
  27.1 0.1 fusion.6
  27.2 0.6 %reshape.87.offset_ref = s32[140]{0:T(256)} reshape(s32[20,7]{1,0:T(8,128)S(1)} %get-tuple-element.6) | data formatting | bytes 1120 | tf_op jit(solution)/shard_map/reshape | solution.py:150
  27.8 0.7 %reshape.88.weight_ref = f32[140]{0:T(256)} reshape(f32[20,7]{1,0:T(8,128)S(1)} %get-tuple-element.5) | data formatting | bytes 1120 | tf_op jit(solution)/shard_map/reshape | solution.py:151
  28.5 0.1 slice.34
  28.6 0.1 fusion
  28.7 1.0 %reshape.96.ext_ref = f32[18,8,896]{2,1,0:T(8,128)} reshape(f32[36,4,896]{2,1,0:T(4,128)S(1)} %fusion) | data formatting | bytes 1032192 | tf_op jit(solution)/shard_map/reshape | solution.py:115
  29.7 12.3 %shard_map.100 = bf16[4,16,896]{2,1,0:T(8,128)(2,1)} custom-call(s32[140]{0:T(256)} %reshape.87.offset_ref, f32[140]{0:T(256)} %reshape.88.weight_ref, s32[2]{0:T(128)} %pad_add_fusion.bounds_ref, f32[18,8,896]{2,1,0:T(8,128)} %reshape.96.ext_ref, bf16[32,16]{1,0:T(8,128)(2,1)} %pad.24.w1_ref, bf16[32,288]{1,0:T(8,128)(2,1)} %reshape.92.w2_ref, ...), custom_call_target="tpu_custom_call" | custom-call | tf_op jit(solution)/shard_map/pallas_call | solution.py:144
  (12 shorter events, 0.2 us)
Async XLA Ops:
  0.0 2.7 %copy-start = (bf16[896,896]{1,0:T(8,128)(2,1)S(1)}, bf16[896,896]{1,0:T(8,128)(2,1)}, u32[]{:S(2)}) copy-start(bf16[896,896]{1,0:T(8,128)(2,1)} %param.14) | copy-start | bytes 4816900
  4.0 8.4 %copy-start.1 = (bf16[32,32,3,3]{1,0,3,2:T(8,128)(2,1)S(1)}, bf16[32,32,3,3]{1,0,3,2:T(8,128)(2,1)}, u32[]{:S(2)}) copy-start(bf16[32,32,3,3]{1,0,3,2:T(8,128)(2,1)} %param.18) | copy-start | bytes 55300
  4.0 9.1 %copy-start.2 = (bf16[32,3,3]{0,2,1:T(4,128)(2,1)S(1)}, bf16[32,3,3]{0,2,1:T(4,128)(2,1)}, u32[]{:S(2)}) copy-start(bf16[32,3,3]{0,2,1:T(4,128)(2,1)} %param.17) | copy-start | bytes 1732
  4.0 9.9 %copy-start.3 = (bf16[32]{0:T(256)(128)(2,1)S(1)}, bf16[32]{0:T(256)(128)(2,1)}, u32[]{:S(2)}) copy-start(bf16[32]{0:T(256)(128)(2,1)} %param.19) | copy-start | bytes 196
  5.1 21.8 %all-to-all-start = ((bf16[32,5,896]{2,1,0:T(8,128)(2,1)}), bf16[32,5,896]{2,1,0:T(8,128)(2,1)S(1)}, u32[]{:S(2)}, u32[]{:S(2)}) async-start(bf16[32,5,896]{2,1,0:T(8,128)(2,1)} %bitcast.2), calls=%async_computation | async-start | bytes 917504 | tf_op jit(solution)/shard_map/all_to_all | solution.py:229

commit v7 on v4

--- a/solution.py
+++ b/solution.py
@@ -174,34 +174,46 @@
     total_views = view_count * group_count
     view_start = lax.axis_index("group") * view_count
 
-    own = lax.axis_index("dev")
-    own_offset = lax.dynamic_slice_in_dim(rebin_offset, own, 1, axis=0).astype(jnp.float32)
-    own_weight = lax.dynamic_slice_in_dim(rebin_weight, own, 1, axis=0)
-    weight_high = lax.reduce_precision(own_weight, exponent_bits=8, mantissa_bits=7)
-    rest = own_weight - weight_high
+    weight_high = lax.reduce_precision(rebin_weight, exponent_bits=8, mantissa_bits=7)
+    rest = rebin_weight - weight_high
     weight_mid = lax.reduce_precision(rest, exponent_bits=8, mantissa_bits=7)
     weight_low = rest - weight_mid
-    param_row = jnp.concatenate([own_offset, weight_high, weight_mid, weight_low], axis=1)
-    param_row = param_row.astype(jnp.bfloat16)
-    param_row = jnp.pad(param_row, ((0, 0), (0, width - 4 * block_count)))
-    chunk = jnp.concatenate(
-        [
-            projected.reshape(dev_count, row_count, width),
-            jnp.broadcast_to(param_row[None], (dev_count, 1, width)),
-        ],
-        axis=1,
-    )
-    chunk = jnp.broadcast_to(chunk[None], (group_count,) + chunk.shape)
-    chunk = chunk.reshape(group_count * dev_count, row_count + 1, width)
-    received = lax.all_to_all(chunk, ("group", "dev"), 0, 0, tiled=True)
-
+    table = jnp.concatenate(
+        [rebin_offset.astype(jnp.float32), weight_high, weight_mid, weight_low], axis=1
+    )
     halo = REACH + RIM
-    views = jnp.pad(received[:, :row_count], ((halo, halo), (0, 0), (0, 0)))
-    views = lax.dynamic_slice_in_dim(views, view_start, view_count + 2 * halo, axis=0)
-    extended = jnp.transpose(views, (1, 0, 2))
-    params = received[:, row_count, : 4 * block_count].astype(jnp.float32)
-    params = jnp.pad(params, ((RIM, RIM), (0, 0)))
-    params = lax.dynamic_slice_in_dim(params, view_start, view_count + 2 * RIM, axis=0)
+    row_major = lax.all_to_all(projected, "dev", split_axis=0, concat_axis=1, tiled=True)
+
+    def pack(data, params):
+        flat = data.reshape(row_count * data.shape[1], width)
+        params = params.reshape(-1)
+        param_rows = -(-params.shape[0] // width)
+        params = jnp.pad(params, (0, param_rows * width - params.shape[0]))
+        params = params.astype(jnp.bfloat16).reshape(param_rows, width)
+        return jnp.concatenate([flat, params], axis=0)
+
+    def unpack(block, views_in, params_in):
+        data = block[: row_count * views_in].reshape(row_count, views_in, width)
+        params = block[row_count * views_in :].reshape(-1)[: params_in * 4 * block_count]
+        return data, params.astype(jnp.float32).reshape(params_in, 4 * block_count)
+
+    head = pack(row_major[:, :halo], table[:RIM])
+    tail = pack(row_major[:, view_count - halo :], table[view_count - RIM :])
+    group_idx = lax.axis_index("group")
+    if group_count == 2:
+        outgoing = jnp.where(group_idx == 0, tail, head)
+        incoming = lax.ppermute(outgoing, "group", [(0, 1), (1, 0)])
+        from_low = jnp.where(group_idx == 0, jnp.zeros_like(incoming), incoming)
+        from_high = jnp.where(group_idx == 0, incoming, jnp.zeros_like(incoming))
+    else:
+        forward = [(i, i + 1) for i in range(group_count - 1)]
+        backward = [(i + 1, i) for i in range(group_count - 1)]
+        from_low = lax.ppermute(tail, "group", forward)
+        from_high = lax.ppermute(head, "group", backward)
+    low_data, low_params = unpack(from_low, halo, RIM)
+    high_data, high_params = unpack(from_high, halo, RIM)
+    extended = jnp.concatenate([low_data, row_major, high_data], axis=1)
+    params = jnp.concatenate([low_params, table, high_params], axis=0)
     offsets = params[:, :block_count].astype(jnp.int32)
     weights = params[:, block_count : 2 * block_count] + (
         params[:, 2 * block_count : 3 * block_count] + params[:, 3 * block_count :]

time: 42.2 us -> 41.1 us (0.974)
  waiting for transfers between devices: 11.7 us -> 7.26 us
  other arithmetic: 1.8 us -> 4.43 us
  starting transfers between devices: 7.3 us -> 8.94 us
  local copies, waits for them, and re-layouts: 7.85 us -> 6.82 us
    all_to_all x1, waiting for transfers between devices: 11.7 us -> 4.91 us  [local(): lax.all_to_all(projected, 'dev', split_axis=0, concat_axis=1, tiled=True)]
    ppermute x0 -> x1, waiting for transfers between devices: none -> 2.35 us  [local(): incoming = lax.ppermute(outgoing, 'group', [(0, 1), (1, 0)])]
    dynamic_slice x2 -> x0, local copies, waits for them, and re-layouts: 1.64 us -> none  [the longest x1 0.88 us: local(): own_weight = lax.dynamic_slice_in_dim(rebin_weight, own, 1, axis=0)]
    ppermute x0 -> x1, starting transfers between devices: none -> 1.58 us  [local(): incoming = lax.ppermute(outgoing, 'group', [(0, 1), (1, 0)])]
    convert_element_type x0 -> x3, other arithmetic: none -> 1.52 us  [the longest x1 1.49 us: rebin_dual(): extended.astype(jnp.float32).reshape(rows, ext_views, 1, width)]
    unnamed x11 -> x15, local copies, waits for them, and re-layouts: 0.22 us -> 1.15 us
    broadcast_in_dim x2 -> x0, local copies, waits for them, and re-layouts: 0.83 us -> none  [the longest x1 0.79 us: local(): chunk = jnp.broadcast_to(chunk[None], (group_count,) + chunk.shape)]
    all_to_all x0 -> x1, other arithmetic: none -> 0.66 us  [local(): lax.all_to_all(projected, 'dev', split_axis=0, concat_axis=1, tiled=True)]
  transfers between devices with their start and end apart: 1 -> 2, of which waited for: 1 -> 2; matrix products, arithmetic and copies ran while one was open for 7% -> 8% of each run, Pallas kernels for 0% -> 0%
where the time goes in v7:
time: 41.1 us; the launch traced here: 40.8 us
  Pallas kernels  11.8 us (29%)
  starting transfers between devices  8.94 us (22%)
  waiting for transfers between devices  7.26 us (18%)
  local copies, waits for them, and re-layouts  6.82 us (17%)
  other arithmetic  4.43 us (11%)
  matrix products  1.32 us (3%)
    pallas_call x1, Pallas kernels, rebin_dual(): pl.pallas_call(kernel, out_shape=jax.ShapeDtypeStruct((rows, out_views, w...  11.8 us
    all_to_all x1, starting transfers between devices, local(): lax.all_to_all(projected, 'dev', split_axis=0, concat_axis=1, tiled=True)  7.36 us
    all_to_all x1, waiting for transfers between devices, local(): lax.all_to_all(projected, 'dev', split_axis=0, concat_axis=1, tiled=True)  4.91 us
    ppermute x1, waiting for transfers between devices, local(): incoming = lax.ppermute(outgoing, 'group', [(0, 1), (1, 0)])  2.35 us
    ppermute x1, starting transfers between devices, local(): incoming = lax.ppermute(outgoing, 'group', [(0, 1), (1, 0)])  1.58 us
    convert_element_type x1, other arithmetic, rebin_dual(): extended.astype(jnp.float32).reshape(rows, ext_views, 1, width)  1.49 us
    dot_general x1, matrix products, resample(): product = jnp.dot(flat, col_map, preferred_element_type=jnp.float32)  1.32 us
    unnamed x15, local copies, waits for them, and re-layouts  1.15 us
  transfers between devices with their start and end apart: 2, of which 2 were waited for; matrix products, arithmetic and copies ran while one was open for 8% of the time, Pallas kernels for 0%

profile of v7, /device:TPU:0, one launch (start us, length us, event | category | flops | bytes accessed | tf_op | source)
XLA Modules:
  0.0 40.8 jit_solution(9964561592087226300)
XLA Ops:
  0.0 0.0 copy-start
  0.0 0.8 %multiply_exponential_fusion = f32[64,1,7]{0,1,2:T(1,128)S(1)} fusion(s32[64,1,7]{0,1,2:T(1,128)} %param.11), kind=kLoop, calls=%fused_computation.19 | loop fusion | flops 1344 | bytes 3584 | tf_op jit(solution)/shard_map/exp2 | solution.py:140
  0.8 0.1 copy.46
  0.9 0.1 mul.55
  1.0 0.0 copy-start.3
  1.1 0.0 copy-start.2
  1.1 0.0 copy-start.1
  1.1 0.3 copy-done
  1.4 0.0 copy-start.4
  1.4 0.0 copy-start.5
  1.4 1.3 %fusion = bf16[64,1,896]{2,0,1:T(8,128)(2,1)S(1)} fusion(bf16[896,896]{1,0:T(8,128)(2,1)S(1)} %copy-done, f32[64,1,896]{2,0,1:T(8,128)S(1)} %mul.56, bf16[64,1,896]{2,0,1:T(8,128)(2,1)} %param.10, f32[896]{0:T(1024)} %param.13, f32[896]{0:T(1024)} %param.12), kind=kOutput, calls=%fused_computation.1 | convolution fusion | flops 103448576 | bytes 2071552 | tf_op jit(solution)/shard_map/dot_general | solution.py:151
  2.8 0.5 %broadcast.33 = bf16[]{:T(256)} broadcast(bf16[]{:T(256)} %constant.27), dimensions={} | broadcast | bytes 4 | tf_op jit(solution)/shard_map/reshape | solution.py:152
  3.3 0.7 %reduce.9 = bf16[64,896]{1,0:T(8,128)(2,1)S(1)} reduce(bf16[64,1,896]{2,0,1:T(8,128)(2,1)S(1)} %fusion, bf16[]{:T(256)} %broadcast.33), dimensions={1}, to_apply=%copy.33.reduce_sub_computation | reduce | bytes 229378 | tf_op jit(solution)/shard_map/reshape | solution.py:152
  4.0 0.7 %reshape.169 = bf16[16,2,1792]{2,1,0:T(2,128)(2,1)} reshape(bf16[64,896]{1,0:T(8,128)(2,1)S(1)} %reduce.9) | data formatting | bytes 229376
  4.7 7.4 %all-to-all-start = ((bf16[16,2,1792]{2,1,0:T(2,128)(2,1)}), bf16[16,2,1792]{2,1,0:T(2,128)(2,1)S(1)}, u32[]{:S(2)}, u32[]{:S(2)}) async-start(bf16[16,2,1792]{2,1,0:T(2,128)(2,1)} %reshape.169), calls=%async_computation | async-start | bytes 229376 | tf_op jit(solution)/shard_map/all_to_all | solution.py:185
  12.1 0.0 copy-done.3
  12.1 0.0 copy-done.2
  12.1 0.1 fusion.10
  12.2 0.1 copy.35
  12.3 0.1 reshape.141
  12.4 0.1 copy.36
  12.5 0.1 reshape.144
  12.6 0.0 copy-done.1
  12.6 0.1 copy.44
  12.7 0.7 %reshape.149.w2_ref = bf16[32,288]{1,0:T(8,128)(2,1)} reshape(bf16[32,3,3,32]{3,2,1,0:T(4,128)(2,1)S(1)} %copy.44) | data formatting | bytes 36864 | tf_op jit(solution)/shard_map/reshape | solution.py:94
  13.4 0.0 copy-done.4
  13.4 0.1 copy.43
  13.5 0.6 %pad.15.w1_ref = bf16[32,16]{1,0:T(8,128)(2,1)} pad(bf16[32,9]{1,0:T(8,128)(2,1)S(1)} %copy.43, bf16[]{:T(256)} %constant.15.clone.1), padding=0_0x0_7 | pad | bytes 1602 | tf_op jit(solution)/shard_map/jit(_pad)/pad | solution.py:93
  14.1 0.0 copy-done.5
  14.1 0.7 %copy.45.kl_ref = f32[32,1]{1,0:T(8,128)} copy(f32[32,1]{0,1:T(1,128)S(1)} %bitcast_convert_fusion) | data formatting | bytes 256 | tf_op jit(solution)/shard_map/reshape | solution.py:95
  14.8 4.9 %all-to-all-done = bf16[16,2,1792]{2,1,0:T(2,128)(2,1)S(1)} async-done(((bf16[16,2,1792]{2,1,0:T(2,128)(2,1)}), bf16[16,2,1792]{2,1,0:T(2,128)(2,1)S(1)}, u32[]{:S(2)}, u32[]{:S(2)}) %all-to-all-start) | async-done | bytes 114720 | tf_op jit(solution)/shard_map/all_to_all | solution.py:185
  19.7 0.1 reshape.170
  19.8 0.7 %reduce = bf16[64,896]{1,0:T(8,128)(2,1)S(1)} reduce(bf16[64,1,896]{2,1,0:T(2,128)(2,1)S(1)} %reshape.170, bf16[]{:T(256)} %constant.27), dimensions={1}, to_apply=%all_to_all.13.reduce_sub_computation | reduce | bytes 229378 | tf_op jit(solution)/shard_map/all_to_all | solution.py:185
  20.5 0.2 copy.51
  20.9 1.6 %collective-permute-start = (bf16[41,896]{1,0:T(8,128)(2,1)S(1)}, bf16[41,896]{1,0:T(8,128)(2,1)S(1)}, u32[]{:S(2)}, u32[]{:S(2)}) collective-permute-start(bf16[41,896]{1,0:T(8,128)(2,1)S(1)} %maximum_select_fusion), channel_id=1, source_target_pairs={{0,16},{16,0},{1,17},{17,1},{2,18},{18,2},{3,19},{19,3},{4,20},{20... | collective-permute-start | bytes 220424 | tf_op jit(solution)/shard_map/ppermute | solution.py:205
  22.5 0.6 %pad_add_fusion.bounds_ref = s32[2]{0:T(128)} fusion(s32[1]{0:T(128)} %constant.18.clone.1, s32[1]{0:T(128)} %bitcast.4), kind=kLoop, calls=%fused_computation.26 | loop fusion | flops 2 | bytes 16 | tf_op jit(solution)/shard_map/stack | solution.py:221
  23.1 2.4 %collective-permute-done = bf16[41,896]{1,0:T(8,128)(2,1)S(1)} collective-permute-done((bf16[41,896]{1,0:T(8,128)(2,1)S(1)}, bf16[41,896]{1,0:T(8,128)(2,1)S(1)}, u32[]{:S(2)}, u32[]{:S(2)}) %collective-permute-start) | collective-permute-done | bytes 73504 | tf_op jit(solution)/shard_map/ppermute | solution.py:205
  25.5 0.1 reshape.152
  25.6 0.1 copy.37
  25.7 0.1 reshape.153
  25.8 0.1 copy.38
  25.9 0.1 pad_maximum_fusion
  26.0 0.1 copy.39
  26.1 0.6 %reshape.146.offset_ref = s32[140]{0:T(256)} reshape(s32[20,7]{1,0:T(8,128)S(1)} %copy.39) | data formatting | bytes 1120 | tf_op jit(solution)/shard_map/reshape | solution.py:124
  26.7 0.1 copy.40
  26.8 0.7 %reshape.147.weight_ref = f32[140]{0:T(256)} reshape(f32[20,7]{1,0:T(8,128)S(1)} %copy.40) | data formatting | bytes 1120 | tf_op jit(solution)/shard_map/reshape | solution.py:125
  27.5 1.5 %maximum_convert_fusion.ext_ref = f32[4,36,1,896]{3,2,1,0:T(1,128)} fusion(bf16[4,10,1,896]{3,2,1,0:T(2,128)(2,1)S(1)} %concatenate.34, bf16[4,16,1,896]{3,2,1,0:T(2,128)(2,1)S(1)} %bitcast.21, bf16[4,10,1,896]{3,2,1,0:T(2,128)(2,1)S(1)} %concatenate.33), kind=kLoop, calls=%fused_computation.2 | loop fusion | flops 387072 | bytes 774144 | tf_op jit(solution)/shard_map/convert_element_type | solution.py:127
  29.0 11.8 %shard_map.100 = bf16[4,16,896]{2,1,0:T(8,128)(2,1)} custom-call(s32[140]{0:T(256)} %reshape.146.offset_ref, f32[140]{0:T(256)} %reshape.147.weight_ref, s32[2]{0:T(128)} %pad_add_fusion.bounds_ref, f32[4,36,1,896]{3,2,1,0:T(1,128)} %maximum_convert_fusion.ext_ref, bf16[32,16]{1,0:T(8,128)(2,1)} %pad.15.w1_ref, bf16[32,288]{1,0:T(8,128)(2,1)} %reshape.149.w2_ref, ...), custom_call_target="tpu_custom_call" | custom-call | tf_op jit(solution)/shard_map/pallas_call | solution.py:119
  (23 shorter events, 0.4 us)
Async XLA Ops:
  0.0 1.4 %copy-start = (bf16[896,896]{1,0:T(8,128)(2,1)S(1)}, bf16[896,896]{1,0:T(8,128)(2,1)}, u32[]{:S(2)}) copy-start(bf16[896,896]{1,0:T(8,128)(2,1)} %param.14) | copy-start | bytes 4816900
  1.0 11.0 %copy-start.3 = (f32[16,7]{0,1:T(8,128)S(1)}, f32[16,7]{0,1:T(8,128)}, u32[]{:S(2)}) copy-start(f32[16,7]{0,1:T(8,128)} %param.16) | copy-start | bytes 1348
  1.1 11.0 %copy-start.2 = (s32[16,7]{0,1:T(8,128)S(1)}, s32[16,7]{0,1:T(8,128)}, u32[]{:S(2)}) copy-start(s32[16,7]{0,1:T(8,128)} %param.15) | copy-start | bytes 1348
  1.1 11.5 %copy-start.1 = (bf16[32,32,3,3]{1,0,3,2:T(8,128)(2,1)S(1)}, bf16[32,32,3,3]{1,0,3,2:T(8,128)(2,1)}, u32[]{:S(2)}) copy-start(bf16[32,32,3,3]{1,0,3,2:T(8,128)(2,1)} %param.18) | copy-start | bytes 55300
  1.4 12.0 %copy-start.4 = (bf16[32,3,3]{0,2,1:T(4,128)(2,1)S(1)}, bf16[32,3,3]{0,2,1:T(4,128)(2,1)}, u32[]{:S(2)}) copy-start(bf16[32,3,3]{0,2,1:T(4,128)(2,1)} %param.17) | copy-start | bytes 1732
  1.4 12.7 %copy-start.5 = (bf16[32]{0:T(256)(128)(2,1)S(1)}, bf16[32]{0:T(256)(128)(2,1)}, u32[]{:S(2)}) copy-start(bf16[32]{0:T(256)(128)(2,1)} %param.19) | copy-start | bytes 196
  4.7 15.0 %all-to-all-start = ((bf16[16,2,1792]{2,1,0:T(2,128)(2,1)}), bf16[16,2,1792]{2,1,0:T(2,128)(2,1)S(1)}, u32[]{:S(2)}, u32[]{:S(2)}) async-start(bf16[16,2,1792]{2,1,0:T(2,128)(2,1)} %reshape.169), calls=%async_computation | async-start | bytes 229376 | tf_op jit(solution)/shard_map/all_to_all | solution.py:185
  20.9 4.6 %collective-permute-start = (bf16[41,896]{1,0:T(8,128)(2,1)S(1)}, bf16[41,896]{1,0:T(8,128)(2,1)S(1)}, u32[]{:S(2)}, u32[]{:S(2)}) collective-permute-start(bf16[41,896]{1,0:T(8,128)(2,1)S(1)} %maximum_select_fusion), channel_id=1, source_target_pairs={{0,16},{16,0},{1,17},{17,1},{2,18},{18,2},{3,19},{19,3},{4,20},{20... | collective-permute-start | bytes 220424 | tf_op jit(solution)/shard_map/ppermute | solution.py:205

commit v8 on v7

--- a/solution.py
+++ b/solution.py
@@ -12,8 +12,7 @@
 
 
 def conv_kernel(
-    offset_ref,
-    weight_ref,
+    table_ref,
     bounds_ref,
     ext_ref,
     w1_ref,
@@ -40,8 +39,11 @@
         pos = view_start - RIM + u
         keep = ((pos >= 0) & (pos < total_views)).astype(jnp.float32)
         for k in range(block_count):
-            low = u + offset_ref[u * block_count + k] + REACH
-            frac = weight_ref[u * block_count + k]
+            entry = u * 4 * block_count + k
+            low = u + table_ref[entry].astype(jnp.int32) + REACH
+            frac = table_ref[entry + block_count] + (
+                table_ref[entry + 2 * block_count] + table_ref[entry + 3 * block_count]
+            )
             cols = pl.ds(k * col_block, col_block)
             lower = ext_ref[0, low, :, cols]
             upper = ext_ref[0, low + 1, :, cols]
@@ -82,9 +84,10 @@
     out_ref[0] = dual_ref[...].astype(out_ref.dtype)
 
 
-def rebin_dual(extended, offsets, weights, bounds, kern_first, kern_second, kern_last):
+def rebin_dual(extended, table, bounds, kern_first, kern_second, kern_last):
     rows, ext_views, width = extended.shape
-    sig_views, block_count = offsets.shape
+    sig_views = table.shape[0]
+    block_count = table.shape[1] // 4
     col_block = width // block_count
     channels = kern_first.shape[0]
     first_views = sig_views - 2
@@ -101,7 +104,7 @@
         channels=channels,
     )
     grid_spec = pltpu.PrefetchScalarGridSpec(
-        num_scalar_prefetch=3,
+        num_scalar_prefetch=2,
         grid=(rows,),
         in_specs=[
             pl.BlockSpec((1, ext_views, 1, width), lambda r, *_: (r, 0, 0, 0)),
@@ -121,8 +124,7 @@
         out_shape=jax.ShapeDtypeStruct((rows, out_views, width), jnp.bfloat16),
         grid_spec=grid_spec,
     )(
-        offsets.reshape(-1),
-        weights.reshape(-1),
+        table.reshape(-1),
         bounds,
         extended.astype(jnp.float32).reshape(rows, ext_views, 1, width),
         w1.astype(jnp.bfloat16),
@@ -182,7 +184,12 @@
         [rebin_offset.astype(jnp.float32), weight_high, weight_mid, weight_low], axis=1
     )
     halo = REACH + RIM
-    row_major = lax.all_to_all(projected, "dev", split_axis=0, concat_axis=1, tiled=True)
+    lead_views = projected.shape[1]
+    by_dest = projected.reshape(dev_count, row_count, lead_views, width)
+    by_source = lax.all_to_all(by_dest, "dev", 0, 0, tiled=True)
+    row_major = jnp.transpose(by_source, (1, 0, 2, 3)).reshape(
+        row_count, dev_count * lead_views, width
+    )
 
     def pack(data, params):
         flat = data.reshape(row_count * data.shape[1], width)
@@ -214,12 +221,8 @@
     high_data, high_params = unpack(from_high, halo, RIM)
     extended = jnp.concatenate([low_data, row_major, high_data], axis=1)
     params = jnp.concatenate([low_params, table, high_params], axis=0)
-    offsets = params[:, :block_count].astype(jnp.int32)
-    weights = params[:, block_count : 2 * block_count] + (
-        params[:, 2 * block_count : 3 * block_count] + params[:, 3 * block_count :]
-    )
     bounds = jnp.stack([view_start, total_views]).astype(jnp.int32)
-    return rebin_dual(extended, offsets, weights, bounds, kern_first, kern_second, kern_last)
+    return rebin_dual(extended, params, bounds, kern_first, kern_second, kern_last)
 
 
 def solution(mesh):

time: 41.1 us -> 39.3 us (0.956)
  local copies, waits for them, and re-layouts: 6.82 us -> 5.46 us
  other arithmetic: 4.43 us -> 3.13 us
  Pallas kernels: 11.8 us -> 12.7 us
    reshape x3 -> x1, local copies, waits for them, and re-layouts: 1.81 us -> 0.69 us  [rebin_dual(): table.reshape(-1)]
    pallas_call x1, Pallas kernels: 11.8 us -> 12.7 us  [rebin_dual(): pl.pallas_call(kernel, out_shape=jax.ShapeDtypeStruct((rows, out_views, w...]
    unnamed x15 -> x13, local copies, waits for them, and re-layouts: 1.15 us -> 0.35 us
    another operation x0 -> x1, local copies, waits for them, and re-layouts: none -> 0.68 us  [local(): by_dest = projected.reshape(dev_count, row_count, lead_views, width)]
    reshape x1 -> x0, other arithmetic: 0.67 us -> none  [resample(): return product.astype(jnp.bfloat16).reshape(shape_in)]
    all_to_all x1 -> x0, other arithmetic: 0.66 us -> none  [local(): lax.all_to_all(projected, 'dev', split_axis=0, concat_axis=1, tiled=True)]
  transfers between devices with their start and end apart: 2 -> 2, of which waited for: 2 -> 2; matrix products, arithmetic and copies ran while one was open for 8% -> 9% of each run, Pallas kernels for 0% -> 0%
where the time goes in v8:
time: 39.3 us; the launch traced here: 39 us
  Pallas kernels  12.7 us (32%)
  starting transfers between devices  8.94 us (23%)
  waiting for transfers between devices  7.22 us (18%)
  local copies, waits for them, and re-layouts  5.46 us (14%)
  other arithmetic  3.13 us (8%)
  matrix products  1.32 us (3%)
    pallas_call x1, Pallas kernels, rebin_dual(): pl.pallas_call(kernel, out_shape=jax.ShapeDtypeStruct((rows, out_views, w...  12.7 us
    all_to_all x1, starting transfers between devices, local(): by_source = lax.all_to_all(by_dest, 'dev', 0, 0, tiled=True)  7.36 us
    all_to_all x1, waiting for transfers between devices, local(): by_source = lax.all_to_all(by_dest, 'dev', 0, 0, tiled=True)  4.9 us
    ppermute x1, waiting for transfers between devices, local(): incoming = lax.ppermute(outgoing, 'group', [(0, 1), (1, 0)])  2.32 us
    ppermute x1, starting transfers between devices, local(): incoming = lax.ppermute(outgoing, 'group', [(0, 1), (1, 0)])  1.58 us
    convert_element_type x1, other arithmetic, rebin_dual(): extended.astype(jnp.float32).reshape(rows, ext_views, 1, width)  1.49 us
    dot_general x1, matrix products, resample(): product = jnp.dot(flat, col_map, preferred_element_type=jnp.float32)  1.32 us
    exp2 x1, other arithmetic, prepare(): counts = counts * jnp.exp2(-exponent.astype(jnp.float32))[..., None]  0.82 us
  transfers between devices with their start and end apart: 2, of which 2 were waited for; matrix products, arithmetic and copies ran while one was open for 9% of the time, Pallas kernels for 0%

profile of v8, /device:TPU:0, one launch (start us, length us, event | category | flops | bytes accessed | tf_op | source)
XLA Modules:
  0.0 39.0 jit_solution(9090514607813709211)
XLA Ops:
  0.0 0.0 copy-start
  0.0 0.8 %multiply_exponential_fusion = f32[64,1,7]{0,1,2:T(1,128)S(1)} fusion(s32[64,1,7]{0,1,2:T(1,128)} %param.11), kind=kLoop, calls=%fused_computation.15 | loop fusion | flops 1344 | bytes 3584 | tf_op jit(solution)/shard_map/exp2 | solution.py:142
  0.8 0.1 copy.44
  0.9 0.0 copy-start.3
  0.9 0.0 copy-start.2
  0.9 0.1 mul.55
  1.1 0.0 copy-start.1
  1.1 0.3 copy-done
  1.4 0.0 copy-start.4
  1.4 0.0 copy-start.5
  1.4 1.3 %convolution_convert_fusion = bf16[64,896]{1,0:T(8,128)(2,1)S(1)} fusion(bf16[896,896]{1,0:T(8,128)(2,1)S(1)} %copy-done, f32[64,1,896]{2,0,1:T(8,128)S(1)} %mul.56, bf16[64,1,896]{2,0,1:T(8,128)(2,1)} %param.10, f32[896]{0:T(1024)} %param.13, f32[896]{0:T(1024)} %param.12), kind=kOutput, calls=%fused_computation | convolution fusion | flops 103448576 | bytes 2071552 | tf_op jit(solution)/shard_map/dot_general | solution.py:153
  2.8 0.7 %reshape_reshape.3 = bf16[16,4,1,896]{3,1,0,2:T(4,128)(2,1)} reshape(bf16[64,896]{1,0:T(8,128)(2,1)S(1)} %convolution_convert_fusion) | data formatting | bytes 229376 | tf_op jit(solution)/shard_map/reshape;reshape | solution.py:188
  3.4 7.4 %all-to-all-start = ((bf16[16,4,1,896]{3,1,2,0:T(4,128)(2,1)}), bf16[16,4,1,896]{3,1,2,0:T(4,128)(2,1)S(1)}, u32[]{:S(2)}, u32[]{:S(2)}) async-start(bf16[16,4,1,896]{3,1,2,0:T(4,128)(2,1)} %bitcast.2), calls=%async_computation | async-start | bytes 229376 | tf_op jit(solution)/shard_map/all_to_all | solution.py:189
  10.8 0.0 copy-done.3
  10.8 0.0 copy-done.2
  10.9 0.1 fusion.8
  11.0 0.1 copy.34
  11.1 0.1 reshape.138
  11.2 0.1 copy.35
  11.3 0.1 reshape.141
  11.4 0.0 copy-done.1
  11.4 0.1 copy.42
  11.4 0.7 %reshape.145.w2_ref = bf16[32,288]{1,0:T(8,128)(2,1)} reshape(bf16[32,3,3,32]{3,2,1,0:T(4,128)(2,1)S(1)} %copy.42) | data formatting | bytes 36864 | tf_op jit(solution)/shard_map/reshape | solution.py:97
  12.2 0.0 copy-done.4
  12.2 0.1 copy.41
  12.3 0.6 %pad.15.w1_ref = bf16[32,16]{1,0:T(8,128)(2,1)} pad(bf16[32,9]{1,0:T(8,128)(2,1)S(1)} %copy.41, bf16[]{:T(256)} %constant.15.clone.1), padding=0_0x0_7 | pad | bytes 1602 | tf_op jit(solution)/shard_map/jit(_pad)/pad | solution.py:96
  12.9 0.0 copy-done.5
  12.9 0.7 %copy.43.kl_ref = f32[32,1]{1,0:T(8,128)} copy(f32[32,1]{0,1:T(1,128)S(1)} %bitcast_convert_fusion) | data formatting | bytes 256 | tf_op jit(solution)/shard_map/reshape | solution.py:98
  13.6 4.9 %all-to-all-done = bf16[16,4,1,896]{3,1,2,0:T(4,128)(2,1)S(1)} async-done(((bf16[16,4,1,896]{3,1,2,0:T(4,128)(2,1)}), bf16[16,4,1,896]{3,1,2,0:T(4,128)(2,1)S(1)}, u32[]{:S(2)}, u32[]{:S(2)}) %all-to-all-start) | async-done | bytes 114720 | tf_op jit(solution)/shard_map/all_to_all | solution.py:189
  18.5 0.2 copy.48
  18.8 1.6 %collective-permute-start = (bf16[41,896]{1,0:T(8,128)(2,1)S(1)}, bf16[41,896]{1,0:T(8,128)(2,1)S(1)}, u32[]{:S(2)}, u32[]{:S(2)}) collective-permute-start(bf16[41,896]{1,0:T(8,128)(2,1)S(1)} %maximum_select_fusion), channel_id=1, source_target_pairs={{0,16},{16,0},{1,17},{17,1},{2,18},{18,2},{3,19},{19,3},{4,20},{20... | collective-permute-start | bytes 220424 | tf_op jit(solution)/shard_map/ppermute | solution.py:212
  20.4 0.6 %pad_add_fusion.bounds_ref = s32[2]{0:T(128)} fusion(s32[1]{0:T(128)} %constant.18.clone.1, s32[1]{0:T(128)} %bitcast.4), kind=kLoop, calls=%fused_computation.22 | loop fusion | flops 2 | bytes 16 | tf_op jit(solution)/shard_map/stack | solution.py:224
  21.1 2.3 %collective-permute-done = bf16[41,896]{1,0:T(8,128)(2,1)S(1)} collective-permute-done((bf16[41,896]{1,0:T(8,128)(2,1)S(1)}, bf16[41,896]{1,0:T(8,128)(2,1)S(1)}, u32[]{:S(2)}, u32[]{:S(2)}) %collective-permute-start) | collective-permute-done | bytes 73504 | tf_op jit(solution)/shard_map/ppermute | solution.py:212
  23.5 0.1 reshape.148
  23.6 0.1 copy.36
  23.7 0.1 reshape.149
  23.7 0.1 copy.37
  23.8 0.1 pad_maximum_fusion
  23.9 0.1 copy.38
  24.0 0.7 %reshape.143.table_ref = f32[560]{0:T(1024)} reshape(f32[20,28]{1,0:T(8,128)S(1)} %copy.38) | data formatting | bytes 4480 | tf_op jit(solution)/shard_map/reshape | solution.py:127
  24.8 1.5 %maximum_convert_fusion.ext_ref = f32[4,36,1,896]{3,2,1,0:T(1,128)} fusion(bf16[4,10,1,896]{3,2,1,0:T(2,128)(2,1)S(1)} %concatenate.34, bf16[4,16,1,896]{3,2,1,0:T(2,128)(2,1)S(1)} %bitcast.20, bf16[4,10,1,896]{3,2,1,0:T(2,128)(2,1)S(1)} %concatenate.33), kind=kLoop, calls=%fused_computation.1 | loop fusion | flops 387072 | bytes 774144 | tf_op jit(solution)/shard_map/convert_element_type | solution.py:129
  26.3 12.7 %shard_map.100 = bf16[4,16,896]{2,1,0:T(8,128)(2,1)} custom-call(f32[560]{0:T(1024)} %reshape.143.table_ref, s32[2]{0:T(128)} %pad_add_fusion.bounds_ref, f32[4,36,1,896]{3,2,1,0:T(1,128)} %maximum_convert_fusion.ext_ref, bf16[32,16]{1,0:T(8,128)(2,1)} %pad.15.w1_ref, bf16[32,288]{1,0:T(8,128)(2,1)} %reshape.145.w2_ref, f32[32,1]{1,0:T(8,128)} %copy.43.kl_ref), custom_call_target="tpu_custom_call" | custom-call | tf_op jit(solution)/shard_map/pallas_call | solution.py:122
  (21 shorter events, 0.4 us)
Async XLA Ops:
  0.0 1.4 %copy-start = (bf16[896,896]{1,0:T(8,128)(2,1)S(1)}, bf16[896,896]{1,0:T(8,128)(2,1)}, u32[]{:S(2)}) copy-start(bf16[896,896]{1,0:T(8,128)(2,1)} %param.14) | copy-start | bytes 4816900
  0.9 9.9 %copy-start.3 = (f32[16,7]{0,1:T(8,128)S(1)}, f32[16,7]{0,1:T(8,128)}, u32[]{:S(2)}) copy-start(f32[16,7]{0,1:T(8,128)} %param.16) | copy-start | bytes 1348
  0.9 9.9 %copy-start.2 = (s32[16,7]{0,1:T(8,128)S(1)}, s32[16,7]{0,1:T(8,128)}, u32[]{:S(2)}) copy-start(s32[16,7]{0,1:T(8,128)} %param.15) | copy-start | bytes 1348
  1.1 10.3 %copy-start.1 = (bf16[32,32,3,3]{1,0,3,2:T(8,128)(2,1)S(1)}, bf16[32,32,3,3]{1,0,3,2:T(8,128)(2,1)}, u32[]{:S(2)}) copy-start(bf16[32,32,3,3]{1,0,3,2:T(8,128)(2,1)} %param.18) | copy-start | bytes 55300
  1.4 10.7 %copy-start.4 = (bf16[32,3,3]{0,2,1:T(4,128)(2,1)S(1)}, bf16[32,3,3]{0,2,1:T(4,128)(2,1)}, u32[]{:S(2)}) copy-start(bf16[32,3,3]{0,2,1:T(4,128)(2,1)} %param.17) | copy-start | bytes 1732
  1.4 11.4 %copy-start.5 = (bf16[32]{0:T(256)(128)(2,1)S(1)}, bf16[32]{0:T(256)(128)(2,1)}, u32[]{:S(2)}) copy-start(bf16[32]{0:T(256)(128)(2,1)} %param.19) | copy-start | bytes 196
  3.4 15.0 %all-to-all-start = ((bf16[16,4,1,896]{3,1,2,0:T(4,128)(2,1)}), bf16[16,4,1,896]{3,1,2,0:T(4,128)(2,1)S(1)}, u32[]{:S(2)}, u32[]{:S(2)}) async-start(bf16[16,4,1,896]{3,1,2,0:T(4,128)(2,1)} %bitcast.2), calls=%async_computation | async-start | bytes 229376 | tf_op jit(solution)/shard_map/all_to_all | solution.py:189
  18.8 4.6 %collective-permute-start = (bf16[41,896]{1,0:T(8,128)(2,1)S(1)}, bf16[41,896]{1,0:T(8,128)(2,1)S(1)}, u32[]{:S(2)}, u32[]{:S(2)}) collective-permute-start(bf16[41,896]{1,0:T(8,128)(2,1)S(1)} %maximum_select_fusion), channel_id=1, source_target_pairs={{0,16},{16,0},{1,17},{17,1},{2,18},{18,2},{3,19},{19,3},{4,20},{20... | collective-permute-start | bytes 220424 | tf_op jit(solution)/shard_map/ppermute | solution.py:212

commit v9 on v8

--- a/solution.py
+++ b/solution.py
@@ -39,11 +39,9 @@
         pos = view_start - RIM + u
         keep = ((pos >= 0) & (pos < total_views)).astype(jnp.float32)
         for k in range(block_count):
-            entry = u * 4 * block_count + k
+            entry = u * 2 * block_count + k
             low = u + table_ref[entry].astype(jnp.int32) + REACH
-            frac = table_ref[entry + block_count] + (
-                table_ref[entry + 2 * block_count] + table_ref[entry + 3 * block_count]
-            )
+            frac = table_ref[entry + block_count]
             cols = pl.ds(k * col_block, col_block)
             lower = ext_ref[0, low, :, cols]
             upper = ext_ref[0, low + 1, :, cols]
@@ -57,28 +55,27 @@
     col = lax.broadcasted_iota(jnp.int32, (channels, width), 1)
     keep_left = col >= 1
     keep_right = col < width - 1
+    zero = jnp.zeros((channels, width), jnp.bfloat16)
     w1 = w1_ref[...]
     for u in range(first_views):
         taps = sig_ref[3 * u : 3 * u + 16, :].astype(jnp.bfloat16)
-        hidden = jnp.dot(w1, taps, preferred_element_type=jnp.float32)
         pos = view_start - 1 + u
-        scale = ((pos >= 0) & (pos < total_views)).astype(jnp.float32)
-        hidden = jnp.maximum(hidden, 0.0) * scale
+        scale = ((pos >= 0) & (pos < total_views)).astype(jnp.bfloat16)
+        hidden = jnp.dot(w1 * scale, taps, preferred_element_type=jnp.float32)
+        hidden = jnp.maximum(hidden, 0.0).astype(jnp.bfloat16)
         base = 3 * u * channels
-        feat_ref[base : base + channels, :] = jnp.where(
-            keep_left, pltpu.roll(hidden, 1, 1), 0.0
-        ).astype(jnp.bfloat16)
-        feat_ref[base + channels : base + 2 * channels, :] = hidden.astype(jnp.bfloat16)
+        feat_ref[base : base + channels, :] = jnp.where(keep_left, pltpu.roll(hidden, 1, 1), zero)
+        feat_ref[base + channels : base + 2 * channels, :] = hidden
         feat_ref[base + 2 * channels : base + 3 * channels, :] = jnp.where(
-            keep_right, pltpu.roll(hidden, width - 1, 1), 0.0
-        ).astype(jnp.bfloat16)
+            keep_right, pltpu.roll(hidden, width - 1, 1), zero
+        )
     w2 = w2_ref[...]
     kl = kl_ref[...]
     for v in range(out_views):
         window = feat_ref[3 * v * channels : 3 * (v + 3) * channels, :]
         second = jnp.dot(w2, window, preferred_element_type=jnp.float32)
-        second = jnp.maximum(second, 0.0).astype(jnp.bfloat16).astype(jnp.float32)
-        mix = jnp.sum(kl * second, axis=0, keepdims=True)
+        second = jnp.maximum(second, 0.0).astype(jnp.bfloat16)
+        mix = jnp.dot(kl, second, preferred_element_type=jnp.float32)[0:1]
         centre = sig_ref[3 * (v + 2) + 1 : 3 * (v + 2) + 2, :]
         dual_ref[v : v + 1, :] = centre + mix
     out_ref[0] = dual_ref[...].astype(out_ref.dtype)
@@ -87,7 +84,7 @@
 def rebin_dual(extended, table, bounds, kern_first, kern_second, kern_last):
     rows, ext_views, width = extended.shape
     sig_views = table.shape[0]
-    block_count = table.shape[1] // 4
+    block_count = table.shape[1] // 2
     col_block = width // block_count
     channels = kern_first.shape[0]
     first_views = sig_views - 2
@@ -95,7 +92,7 @@
     pad_rows = -(-(3 * first_views + 13) // 8) * 8
     w1 = jnp.pad(kern_first.reshape(channels, 9), ((0, 0), (0, 7)))
     w2 = jnp.transpose(kern_second, (0, 2, 3, 1)).reshape(channels, 9 * channels)
-    kl = kern_last.astype(jnp.float32).reshape(channels, 1)
+    kl = jnp.pad(kern_last.reshape(1, channels), ((0, 7), (0, 0)))
     kernel = functools.partial(
         conv_kernel,
         sig_views=sig_views,
@@ -110,7 +107,7 @@
             pl.BlockSpec((1, ext_views, 1, width), lambda r, *_: (r, 0, 0, 0)),
             pl.BlockSpec((channels, 16), lambda r, *_: (0, 0)),
             pl.BlockSpec((channels, 9 * channels), lambda r, *_: (0, 0)),
-            pl.BlockSpec((channels, 1), lambda r, *_: (0, 0)),
+            pl.BlockSpec((8, channels), lambda r, *_: (0, 0)),
         ],
         out_specs=pl.BlockSpec((1, out_views, width), lambda r, *_: (r, 0, 0)),
         scratch_shapes=[
@@ -221,6 +218,10 @@
     high_data, high_params = unpack(from_high, halo, RIM)
     extended = jnp.concatenate([low_data, row_major, high_data], axis=1)
     params = jnp.concatenate([low_params, table, high_params], axis=0)
+    weights = params[:, block_count : 2 * block_count] + (
+        params[:, 2 * block_count : 3 * block_count] + params[:, 3 * block_count :]
+    )
+    params = jnp.concatenate([params[:, :block_count], weights], axis=1)
     bounds = jnp.stack([view_start, total_views]).astype(jnp.int32)
     return rebin_dual(extended, params, bounds, kern_first, kern_second, kern_last)
 

time: 39.3 us -> 45.9 us (1.17)
  Pallas kernels: 12.7 us -> 19.3 us
    pallas_call x1, Pallas kernels: 12.7 us -> 19.3 us  [rebin_dual(): pl.pallas_call(kernel, out_shape=jax.ShapeDtypeStruct((rows, out_views, w...]
    reshape x1 -> x0, local copies, waits for them, and re-layouts: 0.69 us -> none  [rebin_dual(): kl = kern_last.astype(jnp.float32).reshape(channels, 1)]
    pad x0 -> x1, local copies, waits for them, and re-layouts: none -> 0.59 us  [rebin_dual(): kl = jnp.pad(kern_last.reshape(1, channels), ((0, 7), (0, 0)))]
  transfers between devices with their start and end apart: 2 -> 2, of which waited for: 2 -> 2; matrix products, arithmetic and copies ran while one was open for 9% -> 7% of each run, Pallas kernels for 0% -> 0%
where the time goes in v9:
time: 45.9 us; the launch traced here: 45.6 us
  Pallas kernels  19.3 us (42%)
  starting transfers between devices  8.94 us (19%)
  waiting for transfers between devices  7.42 us (16%)
  local copies, waits for them, and re-layouts  5.34 us (12%)
  other arithmetic  3.06 us (7%)
  matrix products  1.32 us (3%)
    pallas_call x1, Pallas kernels, rebin_dual(): pl.pallas_call(kernel, out_shape=jax.ShapeDtypeStruct((rows, out_views, w...  19.3 us
    all_to_all x1, starting transfers between devices, local(): by_source = lax.all_to_all(by_dest, 'dev', 0, 0, tiled=True)  7.36 us
    all_to_all x1, waiting for transfers between devices, local(): by_source = lax.all_to_all(by_dest, 'dev', 0, 0, tiled=True)  5.01 us
    ppermute x1, waiting for transfers between devices, local(): incoming = lax.ppermute(outgoing, 'group', [(0, 1), (1, 0)])  2.41 us
    ppermute x1, starting transfers between devices, local(): incoming = lax.ppermute(outgoing, 'group', [(0, 1), (1, 0)])  1.58 us
    convert_element_type x1, other arithmetic, rebin_dual(): extended.astype(jnp.float32).reshape(rows, ext_views, 1, width)  1.5 us
    dot_general x1, matrix products, resample(): product = jnp.dot(flat, col_map, preferred_element_type=jnp.float32)  1.32 us
  transfers between devices with their start and end apart: 2, of which 2 were waited for; matrix products, arithmetic and copies ran while one was open for 7% of the time, Pallas kernels for 0%

profile of v9, /device:TPU:0, one launch (start us, length us, event | category | flops | bytes accessed | tf_op | source)
XLA Modules:
  0.0 45.6 jit_solution(14869566258269653250)
XLA Ops:
  0.0 0.0 copy-start
  0.0 0.8 %multiply_exponential_fusion = f32[64,1,7]{0,1,2:T(1,128)S(1)} fusion(s32[64,1,7]{0,1,2:T(1,128)} %param.11), kind=kLoop, calls=%fused_computation.18 | loop fusion | flops 1344 | bytes 3584 | tf_op jit(solution)/shard_map/exp2 | solution.py:139
  0.8 0.1 copy.41
  0.9 0.0 copy-start.3
  0.9 0.0 copy-start.2
  0.9 0.1 mul.55
  1.1 0.0 copy-start.1
  1.1 0.3 copy-done
  1.4 0.0 copy-start.4
  1.4 0.0 copy-start.5
  1.4 1.3 %convolution_convert_fusion = bf16[64,896]{1,0:T(8,128)(2,1)S(1)} fusion(bf16[896,896]{1,0:T(8,128)(2,1)S(1)} %copy-done, f32[64,1,896]{2,0,1:T(8,128)S(1)} %mul.56, bf16[64,1,896]{2,0,1:T(8,128)(2,1)} %param.10, f32[896]{0:T(1024)} %param.13, f32[896]{0:T(1024)} %param.12), kind=kOutput, calls=%fused_computation | convolution fusion | flops 103448576 | bytes 2071552 | tf_op jit(solution)/shard_map/dot_general | solution.py:150
  2.8 0.7 %reshape_reshape.3 = bf16[16,4,1,896]{3,1,0,2:T(4,128)(2,1)} reshape(bf16[64,896]{1,0:T(8,128)(2,1)S(1)} %convolution_convert_fusion) | data formatting | bytes 229376 | tf_op jit(solution)/shard_map/reshape;reshape | solution.py:185
  3.4 7.4 %all-to-all-start = ((bf16[16,4,1,896]{3,1,2,0:T(4,128)(2,1)}), bf16[16,4,1,896]{3,1,2,0:T(4,128)(2,1)S(1)}, u32[]{:S(2)}, u32[]{:S(2)}) async-start(bf16[16,4,1,896]{3,1,2,0:T(4,128)(2,1)} %bitcast.2), calls=%async_computation | async-start | bytes 229376 | tf_op jit(solution)/shard_map/all_to_all | solution.py:186
  10.8 0.0 copy-done.3
  10.8 0.0 copy-done.2
  10.9 0.1 fusion.10
  11.0 0.1 copy.32
  11.1 0.1 reshape.136
  11.2 0.1 copy.33
  11.3 0.1 reshape.139
  11.4 0.0 copy-done.1
  11.4 0.1 copy.40
  11.4 0.7 %reshape.143.w2_ref = bf16[32,288]{1,0:T(8,128)(2,1)} reshape(bf16[32,3,3,32]{3,2,1,0:T(4,128)(2,1)S(1)} %copy.40) | data formatting | bytes 36864 | tf_op jit(solution)/shard_map/reshape | solution.py:94
  12.2 0.0 copy-done.4
  12.2 0.1 copy.39
  12.3 0.6 %pad.19.w1_ref = bf16[32,16]{1,0:T(8,128)(2,1)} pad(bf16[32,9]{1,0:T(8,128)(2,1)S(1)} %copy.39, bf16[]{:T(256)} %constant.15.clone.1), padding=0_0x0_7 | pad | bytes 1602 | tf_op jit(solution)/shard_map/jit(_pad)/pad | solution.py:93
  12.9 0.0 copy-done.5
  12.9 0.6 %pad.20.kl_ref = bf16[8,32]{1,0:T(8,128)(2,1)} pad(bf16[1,32]{1,0:T(2,128)(2,1)S(1)} %bitcast.22, bf16[]{:T(256)} %constant.15.clone.1), padding=0_7x0_0 | pad | bytes 578 | tf_op jit(solution)/shard_map/jit(_pad)/pad | solution.py:95
  13.5 5.0 %all-to-all-done = bf16[16,4,1,896]{3,1,2,0:T(4,128)(2,1)S(1)} async-done(((bf16[16,4,1,896]{3,1,2,0:T(4,128)(2,1)}), bf16[16,4,1,896]{3,1,2,0:T(4,128)(2,1)S(1)}, u32[]{:S(2)}, u32[]{:S(2)}) %all-to-all-start) | async-done | bytes 114720 | tf_op jit(solution)/shard_map/all_to_all | solution.py:186
  18.5 0.2 copy.45
  18.8 1.6 %collective-permute-start = (bf16[41,896]{1,0:T(8,128)(2,1)S(1)}, bf16[41,896]{1,0:T(8,128)(2,1)S(1)}, u32[]{:S(2)}, u32[]{:S(2)}) collective-permute-start(bf16[41,896]{1,0:T(8,128)(2,1)S(1)} %maximum_select_fusion), channel_id=1, source_target_pairs={{0,16},{16,0},{1,17},{17,1},{2,18},{18,2},{3,19},{19,3},{4,20},{20... | collective-permute-start | bytes 220424 | tf_op jit(solution)/shard_map/ppermute | solution.py:209
  20.4 0.6 %pad_add_fusion.bounds_ref = s32[2]{0:T(128)} fusion(s32[1]{0:T(128)} %constant.18.clone.1, s32[1]{0:T(128)} %bitcast.4), kind=kLoop, calls=%fused_computation.25 | loop fusion | flops 2 | bytes 16 | tf_op jit(solution)/shard_map/stack | solution.py:225
  21.0 2.4 %collective-permute-done = bf16[41,896]{1,0:T(8,128)(2,1)S(1)} collective-permute-done((bf16[41,896]{1,0:T(8,128)(2,1)S(1)}, bf16[41,896]{1,0:T(8,128)(2,1)S(1)}, u32[]{:S(2)}, u32[]{:S(2)}) %collective-permute-start) | collective-permute-done | bytes 73504 | tf_op jit(solution)/shard_map/ppermute | solution.py:209
  23.5 0.1 reshape.145
  23.6 0.1 copy.34
  23.7 0.1 reshape.146
  23.7 0.1 copy.35
  23.8 0.1 pad_maximum_fusion
  24.0 0.1 copy.36
  24.1 0.7 %reshape.141.table_ref = f32[280]{0:T(512)} reshape(f32[20,14]{1,0:T(8,128)S(1)} %copy.36) | data formatting | bytes 2240 | tf_op jit(solution)/shard_map/reshape | solution.py:124
  24.8 1.5 %maximum_convert_fusion.ext_ref = f32[4,36,1,896]{3,2,1,0:T(1,128)} fusion(bf16[4,10,1,896]{3,2,1,0:T(2,128)(2,1)S(1)} %concatenate.38, bf16[4,16,1,896]{3,2,1,0:T(2,128)(2,1)S(1)} %bitcast.18, bf16[4,10,1,896]{3,2,1,0:T(2,128)(2,1)S(1)} %concatenate.37), kind=kLoop, calls=%fused_computation.1 | loop fusion | flops 387072 | bytes 774144 | tf_op jit(solution)/shard_map/convert_element_type | solution.py:126
  26.3 19.3 %shard_map.100 = bf16[4,16,896]{2,1,0:T(8,128)(2,1)} custom-call(f32[280]{0:T(512)} %reshape.141.table_ref, s32[2]{0:T(128)} %pad_add_fusion.bounds_ref, f32[4,36,1,896]{3,2,1,0:T(1,128)} %maximum_convert_fusion.ext_ref, bf16[32,16]{1,0:T(8,128)(2,1)} %pad.19.w1_ref, bf16[32,288]{1,0:T(8,128)(2,1)} %reshape.143.w2_ref, bf16[8,32]{1,0:T(8,128)(2,1)} %pad.20.kl_ref), custom_call_target="tpu_custom_call" | custom-call | tf_op jit(solution)/shard_map/pallas_call | solution.py:119
  (22 shorter events, 0.4 us)
Async XLA Ops:
  0.0 1.4 %copy-start = (bf16[896,896]{1,0:T(8,128)(2,1)S(1)}, bf16[896,896]{1,0:T(8,128)(2,1)}, u32[]{:S(2)}) copy-start(bf16[896,896]{1,0:T(8,128)(2,1)} %param.14) | copy-start | bytes 4816900
  0.9 9.9 %copy-start.3 = (f32[16,7]{0,1:T(8,128)S(1)}, f32[16,7]{0,1:T(8,128)}, u32[]{:S(2)}) copy-start(f32[16,7]{0,1:T(8,128)} %param.16) | copy-start | bytes 1348
  0.9 9.9 %copy-start.2 = (s32[16,7]{0,1:T(8,128)S(1)}, s32[16,7]{0,1:T(8,128)}, u32[]{:S(2)}) copy-start(s32[16,7]{0,1:T(8,128)} %param.15) | copy-start | bytes 1348
  1.1 10.3 %copy-start.1 = (bf16[32,32,3,3]{1,0,3,2:T(8,128)(2,1)S(1)}, bf16[32,32,3,3]{1,0,3,2:T(8,128)(2,1)}, u32[]{:S(2)}) copy-start(bf16[32,32,3,3]{1,0,3,2:T(8,128)(2,1)} %param.18) | copy-start | bytes 55300
  1.4 10.7 %copy-start.4 = (bf16[32,3,3]{0,2,1:T(4,128)(2,1)S(1)}, bf16[32,3,3]{0,2,1:T(4,128)(2,1)}, u32[]{:S(2)}) copy-start(bf16[32,3,3]{0,2,1:T(4,128)(2,1)} %param.17) | copy-start | bytes 1732
  1.4 11.5 %copy-start.5 = (bf16[32]{0:T(256)(128)(2,1)S(1)}, bf16[32]{0:T(256)(128)(2,1)}, u32[]{:S(2)}) copy-start(bf16[32]{0:T(256)(128)(2,1)} %param.19) | copy-start | bytes 196
  3.4 15.0 %all-to-all-start = ((bf16[16,4,1,896]{3,1,2,0:T(4,128)(2,1)}), bf16[16,4,1,896]{3,1,2,0:T(4,128)(2,1)S(1)}, u32[]{:S(2)}, u32[]{:S(2)}) async-start(bf16[16,4,1,896]{3,1,2,0:T(4,128)(2,1)} %bitcast.2), calls=%async_computation | async-start | bytes 229376 | tf_op jit(solution)/shard_map/all_to_all | solution.py:186
  18.8 4.6 %collective-permute-start = (bf16[41,896]{1,0:T(8,128)(2,1)S(1)}, bf16[41,896]{1,0:T(8,128)(2,1)S(1)}, u32[]{:S(2)}, u32[]{:S(2)}) collective-permute-start(bf16[41,896]{1,0:T(8,128)(2,1)S(1)} %maximum_select_fusion), channel_id=1, source_target_pairs={{0,16},{16,0},{1,17},{17,1},{2,18},{18,2},{3,19},{19,3},{4,20},{20... | collective-permute-start | bytes 220424 | tf_op jit(solution)/shard_map/ppermute | solution.py:209

commit v10 on v9

--- a/solution.py
+++ b/solution.py
@@ -74,8 +74,8 @@
     for v in range(out_views):
         window = feat_ref[3 * v * channels : 3 * (v + 3) * channels, :]
         second = jnp.dot(w2, window, preferred_element_type=jnp.float32)
-        second = jnp.maximum(second, 0.0).astype(jnp.bfloat16)
-        mix = jnp.dot(kl, second, preferred_element_type=jnp.float32)[0:1]
+        second = jnp.maximum(second, 0.0).astype(jnp.bfloat16).astype(jnp.float32)
+        mix = jnp.sum(kl * second, axis=0, keepdims=True)
         centre = sig_ref[3 * (v + 2) + 1 : 3 * (v + 2) + 2, :]
         dual_ref[v : v + 1, :] = centre + mix
     out_ref[0] = dual_ref[...].astype(out_ref.dtype)
@@ -92,7 +92,7 @@
     pad_rows = -(-(3 * first_views + 13) // 8) * 8
     w1 = jnp.pad(kern_first.reshape(channels, 9), ((0, 0), (0, 7)))
     w2 = jnp.transpose(kern_second, (0, 2, 3, 1)).reshape(channels, 9 * channels)
-    kl = jnp.pad(kern_last.reshape(1, channels), ((0, 7), (0, 0)))
+    kl = kern_last.astype(jnp.float32).reshape(channels, 1)
     kernel = functools.partial(
         conv_kernel,
         sig_views=sig_views,
@@ -107,7 +107,7 @@
             pl.BlockSpec((1, ext_views, 1, width), lambda r, *_: (r, 0, 0, 0)),
             pl.BlockSpec((channels, 16), lambda r, *_: (0, 0)),
             pl.BlockSpec((channels, 9 * channels), lambda r, *_: (0, 0)),
-            pl.BlockSpec((8, channels), lambda r, *_: (0, 0)),
+            pl.BlockSpec((channels, 1), lambda r, *_: (0, 0)),
         ],
         out_specs=pl.BlockSpec((1, out_views, width), lambda r, *_: (r, 0, 0)),
         scratch_shapes=[

time: 45.9 us -> 38.5 us (0.84)
  Pallas kernels: 19.3 us -> 11.9 us
    pallas_call x1, Pallas kernels: 19.3 us -> 11.9 us  [rebin_dual(): pl.pallas_call(kernel, out_shape=jax.ShapeDtypeStruct((rows, out_views, w...]
    reshape x0 -> x1, local copies, waits for them, and re-layouts: none -> 0.69 us  [rebin_dual(): kl = kern_last.astype(jnp.float32).reshape(channels, 1)]
    pad x1 -> x0, local copies, waits for them, and re-layouts: 0.59 us -> none  [rebin_dual(): kl = jnp.pad(kern_last.reshape(1, channels), ((0, 7), (0, 0)))]
  transfers between devices with their start and end apart: 2 -> 2, of which waited for: 2 -> 2; matrix products, arithmetic and copies ran while one was open for 7% -> 9% of each run, Pallas kernels for 0% -> 0%
where the time goes in v10:
time: 38.5 us; the launch traced here: 38.2 us
  Pallas kernels  11.9 us (31%)
  starting transfers between devices  8.94 us (23%)
  waiting for transfers between devices  7.31 us (19%)
  local copies, waits for them, and re-layouts  5.45 us (14%)
  other arithmetic  3.07 us (8%)
  matrix products  1.32 us (3%)
    pallas_call x1, Pallas kernels, rebin_dual(): pl.pallas_call(kernel, out_shape=jax.ShapeDtypeStruct((rows, out_views, w...  11.9 us
    all_to_all x1, starting transfers between devices, local(): by_source = lax.all_to_all(by_dest, 'dev', 0, 0, tiled=True)  7.36 us
    all_to_all x1, waiting for transfers between devices, local(): by_source = lax.all_to_all(by_dest, 'dev', 0, 0, tiled=True)  4.9 us
    ppermute x1, waiting for transfers between devices, local(): incoming = lax.ppermute(outgoing, 'group', [(0, 1), (1, 0)])  2.41 us
    ppermute x1, starting transfers between devices, local(): incoming = lax.ppermute(outgoing, 'group', [(0, 1), (1, 0)])  1.58 us
    convert_element_type x1, other arithmetic, rebin_dual(): extended.astype(jnp.float32).reshape(rows, ext_views, 1, width)  1.5 us
    dot_general x1, matrix products, resample(): product = jnp.dot(flat, col_map, preferred_element_type=jnp.float32)  1.32 us
    exp2 x1, other arithmetic, prepare(): counts = counts * jnp.exp2(-exponent.astype(jnp.float32))[..., None]  0.82 us
  transfers between devices with their start and end apart: 2, of which 2 were waited for; matrix products, arithmetic and copies ran while one was open for 9% of the time, Pallas kernels for 0%

profile of v10, /device:TPU:0, one launch (start us, length us, event | category | flops | bytes accessed | tf_op | source)
XLA Modules:
  0.0 38.2 jit_solution(10120683129657124871)
XLA Ops:
  0.0 0.0 copy-start
  0.0 0.8 %multiply_exponential_fusion = f32[64,1,7]{0,1,2:T(1,128)S(1)} fusion(s32[64,1,7]{0,1,2:T(1,128)} %param.11), kind=kLoop, calls=%fused_computation.18 | loop fusion | flops 1344 | bytes 3584 | tf_op jit(solution)/shard_map/exp2 | solution.py:139
  0.8 0.1 copy.44
  0.9 0.0 copy-start.3
  0.9 0.0 copy-start.2
  0.9 0.1 mul.55
  1.1 0.0 copy-start.1
  1.1 0.3 copy-done
  1.4 0.0 copy-start.4
  1.4 0.0 copy-start.5
  1.4 1.3 %convolution_convert_fusion = bf16[64,896]{1,0:T(8,128)(2,1)S(1)} fusion(bf16[896,896]{1,0:T(8,128)(2,1)S(1)} %copy-done, f32[64,1,896]{2,0,1:T(8,128)S(1)} %mul.56, bf16[64,1,896]{2,0,1:T(8,128)(2,1)} %param.10, f32[896]{0:T(1024)} %param.13, f32[896]{0:T(1024)} %param.12), kind=kOutput, calls=%fused_computation | convolution fusion | flops 103448576 | bytes 2071552 | tf_op jit(solution)/shard_map/dot_general | solution.py:150
  2.8 0.7 %reshape_reshape.3 = bf16[16,4,1,896]{3,1,0,2:T(4,128)(2,1)} reshape(bf16[64,896]{1,0:T(8,128)(2,1)S(1)} %convolution_convert_fusion) | data formatting | bytes 229376 | tf_op jit(solution)/shard_map/reshape;reshape | solution.py:185
  3.4 7.4 %all-to-all-start = ((bf16[16,4,1,896]{3,1,2,0:T(4,128)(2,1)}), bf16[16,4,1,896]{3,1,2,0:T(4,128)(2,1)S(1)}, u32[]{:S(2)}, u32[]{:S(2)}) async-start(bf16[16,4,1,896]{3,1,2,0:T(4,128)(2,1)} %bitcast.2), calls=%async_computation | async-start | bytes 229376 | tf_op jit(solution)/shard_map/all_to_all | solution.py:186
  10.8 0.0 copy-done.3
  10.8 0.0 copy-done.2
  10.9 0.1 fusion.10
  11.0 0.1 copy.34
  11.1 0.1 reshape.138
  11.2 0.1 copy.35
  11.3 0.1 reshape.141
  11.4 0.0 copy-done.1
  11.4 0.1 copy.42
  11.4 0.7 %reshape.145.w2_ref = bf16[32,288]{1,0:T(8,128)(2,1)} reshape(bf16[32,3,3,32]{3,2,1,0:T(4,128)(2,1)S(1)} %copy.42) | data formatting | bytes 36864 | tf_op jit(solution)/shard_map/reshape | solution.py:94
  12.2 0.0 copy-done.4
  12.2 0.1 copy.41
  12.3 0.6 %pad.15.w1_ref = bf16[32,16]{1,0:T(8,128)(2,1)} pad(bf16[32,9]{1,0:T(8,128)(2,1)S(1)} %copy.41, bf16[]{:T(256)} %constant.15.clone.1), padding=0_0x0_7 | pad | bytes 1602 | tf_op jit(solution)/shard_map/jit(_pad)/pad | solution.py:93
  12.9 0.0 copy-done.5
  12.9 0.7 %copy.43.kl_ref = f32[32,1]{1,0:T(8,128)} copy(f32[32,1]{0,1:T(1,128)S(1)} %bitcast_convert_fusion) | data formatting | bytes 256 | tf_op jit(solution)/shard_map/reshape | solution.py:95
  13.6 4.9 %all-to-all-done = bf16[16,4,1,896]{3,1,2,0:T(4,128)(2,1)S(1)} async-done(((bf16[16,4,1,896]{3,1,2,0:T(4,128)(2,1)}), bf16[16,4,1,896]{3,1,2,0:T(4,128)(2,1)S(1)}, u32[]{:S(2)}, u32[]{:S(2)}) %all-to-all-start) | async-done | bytes 114720 | tf_op jit(solution)/shard_map/all_to_all | solution.py:186
  18.5 0.2 copy.48
  18.8 1.6 %collective-permute-start = (bf16[41,896]{1,0:T(8,128)(2,1)S(1)}, bf16[41,896]{1,0:T(8,128)(2,1)S(1)}, u32[]{:S(2)}, u32[]{:S(2)}) collective-permute-start(bf16[41,896]{1,0:T(8,128)(2,1)S(1)} %maximum_select_fusion), channel_id=1, source_target_pairs={{0,16},{16,0},{1,17},{17,1},{2,18},{18,2},{3,19},{19,3},{4,20},{20... | collective-permute-start | bytes 220424 | tf_op jit(solution)/shard_map/ppermute | solution.py:209
  20.4 0.6 %pad_add_fusion.bounds_ref = s32[2]{0:T(128)} fusion(s32[1]{0:T(128)} %constant.18.clone.1, s32[1]{0:T(128)} %bitcast.4), kind=kLoop, calls=%fused_computation.25 | loop fusion | flops 2 | bytes 16 | tf_op jit(solution)/shard_map/stack | solution.py:225
  21.0 2.4 %collective-permute-done = bf16[41,896]{1,0:T(8,128)(2,1)S(1)} collective-permute-done((bf16[41,896]{1,0:T(8,128)(2,1)S(1)}, bf16[41,896]{1,0:T(8,128)(2,1)S(1)}, u32[]{:S(2)}, u32[]{:S(2)}) %collective-permute-start) | collective-permute-done | bytes 73504 | tf_op jit(solution)/shard_map/ppermute | solution.py:209
  23.5 0.1 reshape.148
  23.6 0.1 copy.36
  23.7 0.1 reshape.149
  23.7 0.1 copy.37
  23.8 0.1 pad_maximum_fusion
  24.0 0.1 copy.38
  24.1 0.7 %reshape.143.table_ref = f32[280]{0:T(512)} reshape(f32[20,14]{1,0:T(8,128)S(1)} %copy.38) | data formatting | bytes 2240 | tf_op jit(solution)/shard_map/reshape | solution.py:124
  24.8 1.5 %maximum_convert_fusion.ext_ref = f32[4,36,1,896]{3,2,1,0:T(1,128)} fusion(bf16[4,10,1,896]{3,2,1,0:T(2,128)(2,1)S(1)} %concatenate.38, bf16[4,16,1,896]{3,2,1,0:T(2,128)(2,1)S(1)} %bitcast.20, bf16[4,10,1,896]{3,2,1,0:T(2,128)(2,1)S(1)} %concatenate.37), kind=kLoop, calls=%fused_computation.1 | loop fusion | flops 387072 | bytes 774144 | tf_op jit(solution)/shard_map/convert_element_type | solution.py:126
  26.3 11.9 %shard_map.100 = bf16[4,16,896]{2,1,0:T(8,128)(2,1)} custom-call(f32[280]{0:T(512)} %reshape.143.table_ref, s32[2]{0:T(128)} %pad_add_fusion.bounds_ref, f32[4,36,1,896]{3,2,1,0:T(1,128)} %maximum_convert_fusion.ext_ref, bf16[32,16]{1,0:T(8,128)(2,1)} %pad.15.w1_ref, bf16[32,288]{1,0:T(8,128)(2,1)} %reshape.145.w2_ref, f32[32,1]{1,0:T(8,128)} %copy.43.kl_ref), custom_call_target="tpu_custom_call" | custom-call | tf_op jit(solution)/shard_map/pallas_call | solution.py:119
  (23 shorter events, 0.4 us)
Async XLA Ops:
  0.0 1.4 %copy-start = (bf16[896,896]{1,0:T(8,128)(2,1)S(1)}, bf16[896,896]{1,0:T(8,128)(2,1)}, u32[]{:S(2)}) copy-start(bf16[896,896]{1,0:T(8,128)(2,1)} %param.14) | copy-start | bytes 4816900
  0.9 9.9 %copy-start.3 = (f32[16,7]{0,1:T(8,128)S(1)}, f32[16,7]{0,1:T(8,128)}, u32[]{:S(2)}) copy-start(f32[16,7]{0,1:T(8,128)} %param.16) | copy-start | bytes 1348
  0.9 9.9 %copy-start.2 = (s32[16,7]{0,1:T(8,128)S(1)}, s32[16,7]{0,1:T(8,128)}, u32[]{:S(2)}) copy-start(s32[16,7]{0,1:T(8,128)} %param.15) | copy-start | bytes 1348
  1.1 10.3 %copy-start.1 = (bf16[32,32,3,3]{1,0,3,2:T(8,128)(2,1)S(1)}, bf16[32,32,3,3]{1,0,3,2:T(8,128)(2,1)}, u32[]{:S(2)}) copy-start(bf16[32,32,3,3]{1,0,3,2:T(8,128)(2,1)} %param.18) | copy-start | bytes 55300
  1.4 10.7 %copy-start.4 = (bf16[32,3,3]{0,2,1:T(4,128)(2,1)S(1)}, bf16[32,3,3]{0,2,1:T(4,128)(2,1)}, u32[]{:S(2)}) copy-start(bf16[32,3,3]{0,2,1:T(4,128)(2,1)} %param.17) | copy-start | bytes 1732
  1.4 11.5 %copy-start.5 = (bf16[32]{0:T(256)(128)(2,1)S(1)}, bf16[32]{0:T(256)(128)(2,1)}, u32[]{:S(2)}) copy-start(bf16[32]{0:T(256)(128)(2,1)} %param.19) | copy-start | bytes 196
  3.4 15.0 %all-to-all-start = ((bf16[16,4,1,896]{3,1,2,0:T(4,128)(2,1)}), bf16[16,4,1,896]{3,1,2,0:T(4,128)(2,1)S(1)}, u32[]{:S(2)}, u32[]{:S(2)}) async-start(bf16[16,4,1,896]{3,1,2,0:T(4,128)(2,1)} %bitcast.2), calls=%async_computation | async-start | bytes 229376 | tf_op jit(solution)/shard_map/all_to_all | solution.py:186
  18.8 4.6 %collective-permute-start = (bf16[41,896]{1,0:T(8,128)(2,1)S(1)}, bf16[41,896]{1,0:T(8,128)(2,1)S(1)}, u32[]{:S(2)}, u32[]{:S(2)}) collective-permute-start(bf16[41,896]{1,0:T(8,128)(2,1)S(1)} %maximum_select_fusion), channel_id=1, source_target_pairs={{0,16},{16,0},{1,17},{17,1},{2,18},{18,2},{3,19},{19,3},{4,20},{20... | collective-permute-start | bytes 220424 | tf_op jit(solution)/shard_map/ppermute | solution.py:209

commit v11 on v10

--- a/solution.py
+++ b/solution.py
@@ -55,7 +55,6 @@
     col = lax.broadcasted_iota(jnp.int32, (channels, width), 1)
     keep_left = col >= 1
     keep_right = col < width - 1
-    zero = jnp.zeros((channels, width), jnp.bfloat16)
     w1 = w1_ref[...]
     for u in range(first_views):
         taps = sig_ref[3 * u : 3 * u + 16, :].astype(jnp.bfloat16)
@@ -63,17 +62,17 @@
         scale = ((pos >= 0) & (pos < total_views)).astype(jnp.bfloat16)
         hidden = jnp.dot(w1 * scale, taps, preferred_element_type=jnp.float32)
         hidden = jnp.maximum(hidden, 0.0).astype(jnp.bfloat16)
-        base = 3 * u * channels
-        feat_ref[base : base + channels, :] = jnp.where(keep_left, pltpu.roll(hidden, 1, 1), zero)
-        feat_ref[base + channels : base + 2 * channels, :] = hidden
-        feat_ref[base + 2 * channels : base + 3 * channels, :] = jnp.where(
-            keep_right, pltpu.roll(hidden, width - 1, 1), zero
-        )
+        feat_ref[u * channels : (u + 1) * channels, :] = hidden
     w2 = w2_ref[...]
     kl = kl_ref[...]
     for v in range(out_views):
-        window = feat_ref[3 * v * channels : 3 * (v + 3) * channels, :]
-        second = jnp.dot(w2, window, preferred_element_type=jnp.float32)
+        window = feat_ref[v * channels : (v + 3) * channels, :]
+        part = jnp.dot(w2, window, preferred_element_type=jnp.float32)
+        second = part[channels : 2 * channels]
+        second = second + jnp.where(keep_left, pltpu.roll(part[:channels], 1, 1), 0.0)
+        second = second + jnp.where(
+            keep_right, pltpu.roll(part[2 * channels :], width - 1, 1), 0.0
+        )
         second = jnp.maximum(second, 0.0).astype(jnp.bfloat16).astype(jnp.float32)
         mix = jnp.sum(kl * second, axis=0, keepdims=True)
         centre = sig_ref[3 * (v + 2) + 1 : 3 * (v + 2) + 2, :]
@@ -91,7 +90,7 @@
     out_views = sig_views - 4
     pad_rows = -(-(3 * first_views + 13) // 8) * 8
     w1 = jnp.pad(kern_first.reshape(channels, 9), ((0, 0), (0, 7)))
-    w2 = jnp.transpose(kern_second, (0, 2, 3, 1)).reshape(channels, 9 * channels)
+    w2 = jnp.transpose(kern_second, (3, 0, 2, 1)).reshape(3 * channels, 3 * channels)
     kl = kern_last.astype(jnp.float32).reshape(channels, 1)
     kernel = functools.partial(
         conv_kernel,
@@ -106,13 +105,13 @@
         in_specs=[
             pl.BlockSpec((1, ext_views, 1, width), lambda r, *_: (r, 0, 0, 0)),
             pl.BlockSpec((channels, 16), lambda r, *_: (0, 0)),
-            pl.BlockSpec((channels, 9 * channels), lambda r, *_: (0, 0)),
+            pl.BlockSpec((3 * channels, 3 * channels), lambda r, *_: (0, 0)),
             pl.BlockSpec((channels, 1), lambda r, *_: (0, 0)),
         ],
         out_specs=pl.BlockSpec((1, out_views, width), lambda r, *_: (r, 0, 0)),
         scratch_shapes=[
             pltpu.VMEM((pad_rows, width), jnp.float32),
-            pltpu.VMEM((first_views * 3 * channels, width), jnp.bfloat16),
+            pltpu.VMEM((first_views * channels, width), jnp.bfloat16),
             pltpu.VMEM((out_views, width), jnp.float32),
         ],
     )

time: 38.5 us -> 36.9 us (0.958)
  Pallas kernels: 11.9 us -> 10.3 us
    pallas_call x1, Pallas kernels: 11.9 us -> 10.3 us  [rebin_dual(): pl.pallas_call(kernel, out_shape=jax.ShapeDtypeStruct((rows, out_views, w...]
where the time goes in v11:
time: 36.9 us; the launch traced here: 36.6 us
  Pallas kernels  10.3 us (28%)
  starting transfers between devices  8.94 us (24%)
  waiting for transfers between devices  7.31 us (20%)
  local copies, waits for them, and re-layouts  5.44 us (15%)
  other arithmetic  3.07 us (8%)
  matrix products  1.32 us (4%)
    pallas_call x1, Pallas kernels, rebin_dual(): pl.pallas_call(kernel, out_shape=jax.ShapeDtypeStruct((rows, out_views, w...  10.3 us
    all_to_all x1, starting transfers between devices, local(): by_source = lax.all_to_all(by_dest, 'dev', 0, 0, tiled=True)  7.36 us
    all_to_all x1, waiting for transfers between devices, local(): by_source = lax.all_to_all(by_dest, 'dev', 0, 0, tiled=True)  4.9 us
    ppermute x1, waiting for transfers between devices, local(): incoming = lax.ppermute(outgoing, 'group', [(0, 1), (1, 0)])  2.41 us
    ppermute x1, starting transfers between devices, local(): incoming = lax.ppermute(outgoing, 'group', [(0, 1), (1, 0)])  1.58 us
    convert_element_type x1, other arithmetic, rebin_dual(): extended.astype(jnp.float32).reshape(rows, ext_views, 1, width)  1.5 us
    dot_general x1, matrix products, resample(): product = jnp.dot(flat, col_map, preferred_element_type=jnp.float32)  1.32 us
    exp2 x1, other arithmetic, prepare(): counts = counts * jnp.exp2(-exponent.astype(jnp.float32))[..., None]  0.82 us
  transfers between devices with their start and end apart: 2, of which 2 were waited for; matrix products, arithmetic and copies ran while one was open for 9% of the time, Pallas kernels for 0%

profile of v11, /device:TPU:0, one launch (start us, length us, event | category | flops | bytes accessed | tf_op | source)
XLA Modules:
  0.0 36.6 jit_solution(9368414623562765978)
XLA Ops:
  0.0 0.0 copy-start
  0.0 0.8 %multiply_exponential_fusion = f32[64,1,7]{0,1,2:T(1,128)S(1)} fusion(s32[64,1,7]{0,1,2:T(1,128)} %param.11), kind=kLoop, calls=%fused_computation.18 | loop fusion | flops 1344 | bytes 3584 | tf_op jit(solution)/shard_map/exp2 | solution.py:138
  0.8 0.1 copy.44
  0.9 0.0 copy-start.3
  0.9 0.0 copy-start.2
  0.9 0.1 mul.55
  1.1 0.0 copy-start.1
  1.1 0.3 copy-done
  1.4 0.0 copy-start.4
  1.4 0.0 copy-start.5
  1.4 1.3 %convolution_convert_fusion = bf16[64,896]{1,0:T(8,128)(2,1)S(1)} fusion(bf16[896,896]{1,0:T(8,128)(2,1)S(1)} %copy-done, f32[64,1,896]{2,0,1:T(8,128)S(1)} %mul.56, bf16[64,1,896]{2,0,1:T(8,128)(2,1)} %param.10, f32[896]{0:T(1024)} %param.13, f32[896]{0:T(1024)} %param.12), kind=kOutput, calls=%fused_computation | convolution fusion | flops 103448576 | bytes 2071552 | tf_op jit(solution)/shard_map/dot_general | solution.py:149
  2.8 0.7 %reshape_reshape.3 = bf16[16,4,1,896]{3,1,0,2:T(4,128)(2,1)} reshape(bf16[64,896]{1,0:T(8,128)(2,1)S(1)} %convolution_convert_fusion) | data formatting | bytes 229376 | tf_op jit(solution)/shard_map/reshape;reshape | solution.py:184
  3.4 7.4 %all-to-all-start = ((bf16[16,4,1,896]{3,1,2,0:T(4,128)(2,1)}), bf16[16,4,1,896]{3,1,2,0:T(4,128)(2,1)S(1)}, u32[]{:S(2)}, u32[]{:S(2)}) async-start(bf16[16,4,1,896]{3,1,2,0:T(4,128)(2,1)} %bitcast.2), calls=%async_computation | async-start | bytes 229376 | tf_op jit(solution)/shard_map/all_to_all | solution.py:185
  10.8 0.0 copy-done.3
  10.8 0.0 copy-done.2
  10.9 0.1 fusion.10
  11.0 0.1 copy.34
  11.1 0.1 reshape.138
  11.2 0.1 copy.35
  11.3 0.1 reshape.141
  11.4 0.0 copy-done.1
  11.4 0.1 copy.42
  11.4 0.7 %reshape.145.w2_ref = bf16[96,96]{1,0:T(8,128)(2,1)} reshape(bf16[3,32,3,32]{3,2,1,0:T(4,128)(2,1)S(1)} %copy.42) | data formatting | bytes 36864 | tf_op jit(solution)/shard_map/reshape | solution.py:93
  12.2 0.0 copy-done.4
  12.2 0.1 copy.41
  12.3 0.6 %pad.15.w1_ref = bf16[32,16]{1,0:T(8,128)(2,1)} pad(bf16[32,9]{1,0:T(8,128)(2,1)S(1)} %copy.41, bf16[]{:T(256)} %constant.15.clone.1), padding=0_0x0_7 | pad | bytes 1602 | tf_op jit(solution)/shard_map/jit(_pad)/pad | solution.py:92
  12.9 0.0 copy-done.5
  12.9 0.7 %copy.43.kl_ref = f32[32,1]{1,0:T(8,128)} copy(f32[32,1]{0,1:T(1,128)S(1)} %bitcast_convert_fusion) | data formatting | bytes 256 | tf_op jit(solution)/shard_map/reshape | solution.py:94
  13.6 4.9 %all-to-all-done = bf16[16,4,1,896]{3,1,2,0:T(4,128)(2,1)S(1)} async-done(((bf16[16,4,1,896]{3,1,2,0:T(4,128)(2,1)}), bf16[16,4,1,896]{3,1,2,0:T(4,128)(2,1)S(1)}, u32[]{:S(2)}, u32[]{:S(2)}) %all-to-all-start) | async-done | bytes 114720 | tf_op jit(solution)/shard_map/all_to_all | solution.py:185
  18.5 0.2 copy.48
  18.8 1.6 %collective-permute-start = (bf16[41,896]{1,0:T(8,128)(2,1)S(1)}, bf16[41,896]{1,0:T(8,128)(2,1)S(1)}, u32[]{:S(2)}, u32[]{:S(2)}) collective-permute-start(bf16[41,896]{1,0:T(8,128)(2,1)S(1)} %maximum_select_fusion), channel_id=1, source_target_pairs={{0,16},{16,0},{1,17},{17,1},{2,18},{18,2},{3,19},{19,3},{4,20},{20... | collective-permute-start | bytes 220424 | tf_op jit(solution)/shard_map/ppermute | solution.py:208
  20.4 0.6 %pad_add_fusion.bounds_ref = s32[2]{0:T(128)} fusion(s32[1]{0:T(128)} %constant.18.clone.1, s32[1]{0:T(128)} %bitcast.4), kind=kLoop, calls=%fused_computation.25 | loop fusion | flops 2 | bytes 16 | tf_op jit(solution)/shard_map/stack | solution.py:224
  21.0 2.4 %collective-permute-done = bf16[41,896]{1,0:T(8,128)(2,1)S(1)} collective-permute-done((bf16[41,896]{1,0:T(8,128)(2,1)S(1)}, bf16[41,896]{1,0:T(8,128)(2,1)S(1)}, u32[]{:S(2)}, u32[]{:S(2)}) %collective-permute-start) | collective-permute-done | bytes 73504 | tf_op jit(solution)/shard_map/ppermute | solution.py:208
  23.5 0.1 reshape.148
  23.6 0.1 copy.36
  23.7 0.1 reshape.149
  23.7 0.1 copy.37
  23.8 0.1 pad_maximum_fusion
  24.0 0.1 copy.38
  24.1 0.7 %reshape.143.table_ref = f32[280]{0:T(512)} reshape(f32[20,14]{1,0:T(8,128)S(1)} %copy.38) | data formatting | bytes 2240 | tf_op jit(solution)/shard_map/reshape | solution.py:123
  24.8 1.5 %maximum_convert_fusion.ext_ref = f32[4,36,1,896]{3,2,1,0:T(1,128)} fusion(bf16[4,10,1,896]{3,2,1,0:T(2,128)(2,1)S(1)} %concatenate.38, bf16[4,16,1,896]{3,2,1,0:T(2,128)(2,1)S(1)} %bitcast.20, bf16[4,10,1,896]{3,2,1,0:T(2,128)(2,1)S(1)} %concatenate.37), kind=kLoop, calls=%fused_computation.1 | loop fusion | flops 387072 | bytes 774144 | tf_op jit(solution)/shard_map/convert_element_type | solution.py:125
  26.3 10.3 %shard_map.100 = bf16[4,16,896]{2,1,0:T(8,128)(2,1)} custom-call(f32[280]{0:T(512)} %reshape.143.table_ref, s32[2]{0:T(128)} %pad_add_fusion.bounds_ref, f32[4,36,1,896]{3,2,1,0:T(1,128)} %maximum_convert_fusion.ext_ref, bf16[32,16]{1,0:T(8,128)(2,1)} %pad.15.w1_ref, bf16[96,96]{1,0:T(8,128)(2,1)} %reshape.145.w2_ref, f32[32,1]{1,0:T(8,128)} %copy.43.kl_ref), custom_call_target="tpu_custom_call" | custom-call | tf_op jit(solution)/shard_map/pallas_call | solution.py:118
  (23 shorter events, 0.4 us)
Async XLA Ops:
  0.0 1.4 %copy-start = (bf16[896,896]{1,0:T(8,128)(2,1)S(1)}, bf16[896,896]{1,0:T(8,128)(2,1)}, u32[]{:S(2)}) copy-start(bf16[896,896]{1,0:T(8,128)(2,1)} %param.14) | copy-start | bytes 4816900
  0.9 9.9 %copy-start.3 = (f32[16,7]{0,1:T(8,128)S(1)}, f32[16,7]{0,1:T(8,128)}, u32[]{:S(2)}) copy-start(f32[16,7]{0,1:T(8,128)} %param.16) | copy-start | bytes 1348
  0.9 9.9 %copy-start.2 = (s32[16,7]{0,1:T(8,128)S(1)}, s32[16,7]{0,1:T(8,128)}, u32[]{:S(2)}) copy-start(s32[16,7]{0,1:T(8,128)} %param.15) | copy-start | bytes 1348
  1.1 10.3 %copy-start.1 = (bf16[32,32,3,3]{1,0,3,2:T(8,128)(2,1)S(1)}, bf16[32,32,3,3]{1,0,3,2:T(8,128)(2,1)}, u32[]{:S(2)}) copy-start(bf16[32,32,3,3]{1,0,3,2:T(8,128)(2,1)} %param.18) | copy-start | bytes 55300
  1.4 10.7 %copy-start.4 = (bf16[32,3,3]{0,2,1:T(4,128)(2,1)S(1)}, bf16[32,3,3]{0,2,1:T(4,128)(2,1)}, u32[]{:S(2)}) copy-start(bf16[32,3,3]{0,2,1:T(4,128)(2,1)} %param.17) | copy-start | bytes 1732
  1.4 11.5 %copy-start.5 = (bf16[32]{0:T(256)(128)(2,1)S(1)}, bf16[32]{0:T(256)(128)(2,1)}, u32[]{:S(2)}) copy-start(bf16[32]{0:T(256)(128)(2,1)} %param.19) | copy-start | bytes 196
  3.4 15.0 %all-to-all-start = ((bf16[16,4,1,896]{3,1,2,0:T(4,128)(2,1)}), bf16[16,4,1,896]{3,1,2,0:T(4,128)(2,1)S(1)}, u32[]{:S(2)}, u32[]{:S(2)}) async-start(bf16[16,4,1,896]{3,1,2,0:T(4,128)(2,1)} %bitcast.2), calls=%async_computation | async-start | bytes 229376 | tf_op jit(solution)/shard_map/all_to_all | solution.py:185
  18.8 4.6 %collective-permute-start = (bf16[41,896]{1,0:T(8,128)(2,1)S(1)}, bf16[41,896]{1,0:T(8,128)(2,1)S(1)}, u32[]{:S(2)}, u32[]{:S(2)}) collective-permute-start(bf16[41,896]{1,0:T(8,128)(2,1)S(1)} %maximum_select_fusion), channel_id=1, source_target_pairs={{0,16},{16,0},{1,17},{17,1},{2,18},{18,2},{3,19},{19,3},{4,20},{20... | collective-permute-start | bytes 220424 | tf_op jit(solution)/shard_map/ppermute | solution.py:208

commit v12 on v11

--- a/solution.py
+++ b/solution.py
@@ -225,9 +225,89 @@
     return rebin_dual(extended, params, bounds, kern_first, kern_second, kern_last)
 
 
+def local_swapped(
+    mantissa,
+    exponent,
+    poly_square,
+    poly_cube,
+    col_map,
+    rebin_offset,
+    rebin_weight,
+    kern_first,
+    kern_second,
+    kern_last,
+):
+    lead_rows, lead_views, width = mantissa.shape
+    dev_count = lax.axis_size("dev")
+    row_count = lead_rows // dev_count
+    view_count, block_count = rebin_offset.shape
+    total_views = 2 * view_count
+    first_group = lax.axis_index("group") == 0
+    view_start = jnp.where(first_group, 0, view_count)
+
+    weight_high = lax.reduce_precision(rebin_weight, exponent_bits=8, mantissa_bits=7)
+    rest = rebin_weight - weight_high
+    weight_mid = lax.reduce_precision(rest, exponent_bits=8, mantissa_bits=7)
+    weight_low = rest - weight_mid
+    table = jnp.concatenate(
+        [rebin_offset.astype(jnp.float32), weight_high, weight_mid, weight_low], axis=1
+    )
+
+    def as_rows(values):
+        values = values.reshape(-1)
+        count = -(-values.shape[0] // width)
+        values = jnp.pad(values, (0, count * width - values.shape[0]))
+        return values.astype(jnp.bfloat16).reshape(count, width)
+
+    data_rows = lead_rows * lead_views
+    exp_rows = as_rows(exponent.astype(jnp.float32))
+    packet = jnp.concatenate(
+        [mantissa.reshape(data_rows, width), exp_rows, as_rows(table)], axis=0
+    )
+    arrived = lax.ppermute(packet, "group", [(0, 1), (1, 0)])
+    other_mantissa = arrived[:data_rows].reshape(lead_rows, lead_views, width)
+    exp_size = exponent.size
+    other_exponent = arrived[data_rows : data_rows + exp_rows.shape[0]].reshape(-1)[:exp_size]
+    other_exponent = other_exponent.astype(jnp.int32).reshape(exponent.shape)
+    other_table = arrived[data_rows + exp_rows.shape[0] :].reshape(-1)[: table.size]
+    other_table = other_table.astype(jnp.float32).reshape(table.shape)
+    both_mantissa = jnp.concatenate([mantissa, other_mantissa], axis=1)
+    both_exponent = jnp.concatenate([exponent, other_exponent], axis=1)
+    projected = resample(prepare(both_mantissa, both_exponent, poly_square, poly_cube), col_map)
+
+    by_dest = projected.reshape(dev_count, row_count, 2, lead_views, width)
+    by_source = lax.all_to_all(by_dest, "dev", 0, 0, tiled=True)
+    slots = jnp.transpose(by_source, (1, 2, 0, 3, 4)).reshape(
+        row_count, 2, view_count, width
+    )
+    own_views, other_views = slots[:, 0], slots[:, 1]
+    all_views = jnp.where(
+        first_group,
+        jnp.concatenate([own_views, other_views], axis=1),
+        jnp.concatenate([other_views, own_views], axis=1),
+    )
+    halo = REACH + RIM
+    all_views = jnp.pad(all_views, ((0, 0), (halo, halo), (0, 0)))
+    extended = lax.dynamic_slice_in_dim(all_views, view_start, view_count + 2 * halo, axis=1)
+    full_table = jnp.where(
+        first_group,
+        jnp.concatenate([table, other_table], axis=0),
+        jnp.concatenate([other_table, table], axis=0),
+    )
+    full_table = jnp.pad(full_table, ((RIM, RIM), (0, 0)))
+    params = lax.dynamic_slice_in_dim(full_table, view_start, view_count + 2 * RIM, axis=0)
+    weights = params[:, block_count : 2 * block_count] + (
+        params[:, 2 * block_count : 3 * block_count] + params[:, 3 * block_count :]
+    )
+    params = jnp.concatenate([params[:, :block_count], weights], axis=1)
+    bounds = jnp.stack([view_start, total_views]).astype(jnp.int32)
+    return rebin_dual(extended, params, bounds, kern_first, kern_second, kern_last)
+
+
 def solution(mesh):
+    body = local_swapped if mesh.shape["group"] == 2 else local
     return jax.shard_map(
-        local,
+        body,
         mesh=mesh,
         in_specs=(
             P(None, ("group", "dev"), None),

time: 36.9 us -> 43 us (1.17)
  local copies, waits for them, and re-layouts: 5.44 us -> 8.48 us
  other arithmetic: 3.07 us -> 5.75 us
  waiting for transfers between devices: 7.31 us -> 8.34 us
  matrix products: 1.32 us -> 0.53 us
    all_to_all x1, waiting for transfers between devices: 4.9 us -> 8.34 us  [local_swapped(): by_source = lax.all_to_all(by_dest, 'dev', 0, 0, tiled=True)]
    ppermute x1, waiting for transfers between devices: 2.41 us -> 0.01 us  [local_swapped(): arrived = lax.ppermute(packet, 'group', [(0, 1), (1, 0)])]
    all_to_all x1, starting transfers between devices: 7.36 us -> 5.9 us  [local_swapped(): by_source = lax.all_to_all(by_dest, 'dev', 0, 0, tiled=True)]
    ppermute x1, starting transfers between devices: 1.58 us -> 3.03 us  [local_swapped(): arrived = lax.ppermute(packet, 'group', [(0, 1), (1, 0)])]
    reshape x6 -> x5, local copies, waits for them, and re-layouts: 0.25 us -> 1.57 us  [the longest x1 1.31 us: rebin_dual(): extended.astype(jnp.float32).reshape(rows, ext_views, 1, width)]
    transpose x1, local copies, waits for them, and re-layouts: 0.05 us -> 0.94 us  [rebin_dual(): jnp.transpose(kern_second, (3, 0, 2, 1)).reshape(3 * channels, 3 * channels)]
    concatenate x2, other arithmetic: 0.09 us -> 0.93 us  [the longest x1 0.92 us: local_swapped(): jnp.concatenate([mantissa.reshape(data_rows, width), exp_rows, as_rows(ta...]
    reduce_precision x1, other arithmetic: 0.01 us -> 0.81 us  [local_swapped(): lax.reduce_precision(rebin_weight, exponent_bits=8, mantissa_bits=7)]
  transfers between devices with their start and end apart: 2 -> 2, of which waited for: 2 -> 1; matrix products, arithmetic and copies ran while one was open for 9% -> 14% of each run, Pallas kernels for 0% -> 0%
where the time goes in v12:
time: 43 us; the launch traced here: 42.6 us
  Pallas kernels  10.3 us (24%)
  starting transfers between devices  8.94 us (21%)
  local copies, waits for them, and re-layouts  8.48 us (20%)
  waiting for transfers between devices  8.34 us (19%)
  other arithmetic  5.75 us (13%)
  matrix products  0.53 us (1%)
    pallas_call x1, Pallas kernels, rebin_dual(): pl.pallas_call(kernel, out_shape=jax.ShapeDtypeStruct((rows, out_views, w...  10.3 us
    all_to_all x1, waiting for transfers between devices, local_swapped(): by_source = lax.all_to_all(by_dest, 'dev', 0, 0, tiled=True)  8.34 us
    all_to_all x1, starting transfers between devices, local_swapped(): by_source = lax.all_to_all(by_dest, 'dev', 0, 0, tiled=True)  5.9 us
    ppermute x1, starting transfers between devices, local_swapped(): arrived = lax.ppermute(packet, 'group', [(0, 1), (1, 0)])  3.03 us
    reshape x1, local copies, waits for them, and re-layouts, rebin_dual(): extended.astype(jnp.float32).reshape(rows, ext_views, 1, width)  1.31 us
    convert_element_type x1, other arithmetic, prepare(): mantissa.astype(jnp.float32)  0.94 us
    transpose x1, local copies, waits for them, and re-layouts, rebin_dual(): jnp.transpose(kern_second, (3, 0, 2, 1)).reshape(3 * channels, 3 * channels)  0.94 us
    concatenate x1, other arithmetic, local_swapped(): jnp.concatenate([mantissa.reshape(data_rows, width), exp_rows, as_rows(ta...  0.92 us
  transfers between devices with their start and end apart: 2, of which 1 were waited for; matrix products, arithmetic and copies ran while one was open for 14% of the time, Pallas kernels for 0%

profile of v12, /device:TPU:0, one launch (start us, length us, event | category | flops | bytes accessed | tf_op | source)
XLA Modules:
  0.0 42.6 jit_solution(6220906751164784095)
XLA Ops:
  0.0 0.0 copy-start
  0.0 0.8 %fusion.16 = (f32[16,7]{0,1:T(8,128)S(1)}, f32[16,7]{0,1:T(8,128)S(1)}, f32[16,7]{0,1:T(8,128)S(1)}) fusion(f32[16,7]{0,1:T(8,128)} %param.16), kind=kLoop, calls=%fused_computation.42 | loop fusion | flops 448 | bytes 1792 | tf_op jit(solution)/shard_map/reduce_precision | solution.py:248
  0.8 0.7 %convert_element_type.64 = f32[16,7]{0,1:T(8,128)S(1)} convert(s32[16,7]{0,1:T(8,128)} %param.15) | non-fusion elementwise | flops 112 | bytes 896 | tf_op jit(solution)/shard_map/convert_element_type | solution.py:253
  1.5 0.1 copy.70
  1.6 0.1 reshape.99
  1.7 0.7 %convert_convert_fusion = bf16[64,1,7]{0,1,2:T(2,128)(2,1)S(1)} fusion(s32[64,1,7]{0,1,2:T(1,128)} %param.11), kind=kLoop, calls=%fused_computation.33 | loop fusion | flops 896 | bytes 2688 | tf_op jit(solution)/shard_map/convert.10
  2.4 0.1 copy.69
  2.5 0.1 reshape.97
  2.7 0.9 %pad_maximum_fusion = bf16[66,896]{1,0:T(8,128)(2,1)S(1)} fusion(bf16[1,896]{1,0:T(2,128)(2,1)S(1)} %reshape.100, bf16[1,896]{1,0:T(2,128)(2,1)S(1)} %reshape.98, bf16[64,896]{1,0:T(8,128)(2,1)} %bitcast.41), kind=kLoop, calls=%fused_computation.16 | loop fusion | flops 354816 | bytes 236544 | tf_op jit(solution)/shard_map/concatenate | solution.py:264
  3.6 0.0 copy-start.1
  3.7 3.0 %collective-permute-start = (bf16[66,896]{1,0:T(8,128)(2,1)S(1)}, bf16[66,896]{1,0:T(8,128)(2,1)S(1)}, u32[]{:S(2)}, u32[]{:S(2)}) collective-permute-start(bf16[66,896]{1,0:T(8,128)(2,1)S(1)} %pad_maximum_fusion), channel_id=1, source_target_pairs={{0,16},{16,0},{1,17},{17,1},{2,18},{18,2},{3,19},{19,3},{4,20},{20... | collective-permute-start | bytes 354824 | tf_op jit(solution)/shard_map/ppermute | solution.py:267
  6.7 0.7 %bitcast_convert_fusion = f32[32,1]{0,1:T(1,128)S(1)} fusion(bf16[32]{0:T(256)(128)(2,1)} %param.19), kind=kLoop, calls=%fused_computation.41 | loop fusion | flops 32 | bytes 192 | tf_op jit(solution)/shard_map/reshape | solution.py:94
  7.3 0.9 %copy.81 = bf16[3,32,3,32]{3,2,1,0:T(4,128)(2,1)S(1)} copy(bf16[3,32,3,32]{3,1,0,2:T(8,128)(2,1)} %bitcast.42) | data formatting | bytes 36864 | tf_op jit(solution)/shard_map/transpose | solution.py:93
  8.3 0.7 %reshape.106.w2_ref = bf16[96,96]{1,0:T(8,128)(2,1)} reshape(bf16[3,32,3,32]{3,2,1,0:T(4,128)(2,1)S(1)} %copy.81) | data formatting | bytes 36864 | tf_op jit(solution)/shard_map/reshape | solution.py:93
  9.0 0.7 %reshape.105 = bf16[32,9]{0,1:T(8,128)(2,1)S(1)} reshape(bf16[32,3,3]{0,2,1:T(4,128)(2,1)} %param.17) | data formatting | bytes 1152 | tf_op jit(solution)/shard_map/reshape | solution.py:92
  9.7 0.1 copy.80
  9.8 0.6 %pad.25.w1_ref = bf16[32,16]{1,0:T(8,128)(2,1)} pad(bf16[32,9]{1,0:T(8,128)(2,1)S(1)} %copy.80, bf16[]{:T(256)} %constant.17.clone.1), padding=0_0x0_7 | pad | bytes 1602 | tf_op jit(solution)/shard_map/jit(_pad)/pad | solution.py:92
  10.4 0.7 %copy.83.kl_ref = f32[32,1]{1,0:T(8,128)} copy(f32[32,1]{0,1:T(1,128)S(1)} %bitcast_convert_fusion) | data formatting | bytes 256 | tf_op jit(solution)/shard_map/reshape | solution.py:94
  11.1 0.6 %pad_add_fusion.bounds_ref = s32[2]{0:T(128)} fusion(s32[1]{0:T(128)} %constant.20.clone.1, s32[1]{0:T(128)} %bitcast.1), kind=kLoop, calls=%fused_computation.40 | loop fusion | flops 2 | bytes 16 | tf_op jit(solution)/shard_map/stack | solution.py:303
  11.7 0.0 collective-permute-done
  11.7 0.0 copy-start.2
  11.7 0.0 copy-start.3
  11.7 0.9 %maximum_convert_fusion = f32[64,2,896]{2,0,1:T(8,128)S(1)} fusion(bf16[64,1,896]{2,0,1:T(8,128)(2,1)S(1)} %slice_bitcast_fusion.2, bf16[64,1,896]{2,0,1:T(8,128)(2,1)} %param.10), kind=kLoop, calls=%fused_computation.11 | loop fusion | flops 229376 | bytes 688128 | tf_op jit(solution)/shard_map/convert_element_type | solution.py:135
  12.7 0.4 copy.74
  13.0 0.3 reshape.110
  13.4 0.1 reshape.111
  13.5 0.1 copy.75
  13.6 0.0 copy-done.1
  13.6 0.1 copy.76
  13.7 0.2 mul.42
  13.9 0.0 copy-done
  14.0 0.0 copy-done.2
  14.0 0.0 copy-done.3
  14.0 0.5 %convolution_convert_fusion = bf16[128,896]{1,0:T(8,128)(2,1)S(1)} fusion(bf16[896,896]{1,0:T(8,128)(2,1)S(1)} %copy-done, f32[128,896]{1,0:T(8,128)S(1)} %reshape.110, f32[16,8,7,128]{3,2,1,0:T(8,128)S(1)} %bitcast.39, f32[896]{0:T(1024)S(1)} %copy-done.2, f32[896]{0:T(1024)S(1)} %copy-done.3), kind=kOutput, calls=%fused_computation | convolution fusion | flops 206782464 | bytes 2759680 | tf_op jit(solution)/shard_map/dot_general | solution.py:149
  14.5 0.8 %reshape_reshape.3 = bf16[16,4,2,1,896]{4,2,1,0,3:T(2,128)(2,1)} reshape(bf16[128,896]{1,0:T(8,128)(2,1)S(1)} %convolution_convert_fusion) | data formatting | bytes 458752 | tf_op jit(solution)/shard_map/reshape;reshape | solution.py:278
  15.3 5.9 %all-to-all-start = ((bf16[16,4,2,1,896]{4,2,1,3,0:T(2,128)(2,1)}), bf16[16,4,2,1,896]{4,2,1,3,0:T(2,128)(2,1)S(1)}, u32[]{:S(2)}, u32[]{:S(2)}) async-start(bf16[16,4,2,1,896]{4,2,1,3,0:T(2,128)(2,1)} %bitcast.3), calls=%async_computation | async-start | bytes 458752 | tf_op jit(solution)/shard_map/all_to_all | solution.py:279
  21.2 0.1 reshape.109
  21.3 0.1 copy.71
  21.4 0.1 maximum_select_fusion.1
  21.5 0.1 pad_dynamic-slice_fusion.3
  21.6 0.1 copy.73
  21.7 0.7 %reshape.101.table_ref = f32[280]{0:T(512)} reshape(f32[20,14]{1,0:T(8,128)S(1)} %copy.73) | data formatting | bytes 2240 | tf_op jit(solution)/shard_map/reshape | solution.py:123
  22.4 8.3 %all-to-all-done = bf16[16,4,2,1,896]{4,2,1,3,0:T(2,128)(2,1)S(1)} async-done(((bf16[16,4,2,1,896]{4,2,1,3,0:T(2,128)(2,1)}), bf16[16,4,2,1,896]{4,2,1,3,0:T(2,128)(2,1)S(1)}, u32[]{:S(2)}, u32[]{:S(2)}) %all-to-all-start) | async-done | bytes 229408 | tf_op jit(solution)/shard_map/all_to_all | solution.py:279
  30.8 0.1 fusion.5
  30.9 1.3 %copy.82.ext_ref = f32[4,36,1,896]{3,2,1,0:T(1,128)} copy(f32[4,36,1,896]{3,1,0,2:T(8,128)S(1)} %fusion.5) | data formatting | bytes 1032192 | tf_op jit(solution)/shard_map/reshape | solution.py:125
  32.2 10.3 %shard_map.100 = bf16[4,16,896]{2,1,0:T(8,128)(2,1)} custom-call(f32[280]{0:T(512)} %reshape.101.table_ref, s32[2]{0:T(128)} %pad_add_fusion.bounds_ref, f32[4,36,1,896]{3,2,1,0:T(1,128)} %copy.82.ext_ref, bf16[32,16]{1,0:T(8,128)(2,1)} %pad.25.w1_ref, bf16[96,96]{1,0:T(8,128)(2,1)} %reshape.106.w2_ref, f32[32,1]{1,0:T(8,128)} %copy.83.kl_ref), custom_call_target="tpu_custom_call" | custom-call | tf_op jit(solution)/shard_map/pallas_call | solution.py:118
  (13 shorter events, 0.2 us)
Async XLA Ops:
  0.0 13.9 %copy-start = (bf16[896,896]{1,0:T(8,128)(2,1)S(1)}, bf16[896,896]{1,0:T(8,128)(2,1)}, u32[]{:S(2)}) copy-start(bf16[896,896]{1,0:T(8,128)(2,1)} %param.14) | copy-start | bytes 4816900
  3.6 9.9 %copy-start.1 = (s32[64,1,7]{0,1,2:T(1,128)S(1)}, s32[64,1,7]{0,1,2:T(1,128)}, u32[]{:S(2)}) copy-start(s32[64,1,7]{0,1,2:T(1,128)} %param.11) | copy-start | bytes 5380
  3.7 8.0 %collective-permute-start = (bf16[66,896]{1,0:T(8,128)(2,1)S(1)}, bf16[66,896]{1,0:T(8,128)(2,1)S(1)}, u32[]{:S(2)}, u32[]{:S(2)}) collective-permute-start(bf16[66,896]{1,0:T(8,128)(2,1)S(1)} %pad_maximum_fusion), channel_id=1, source_target_pairs={{0,16},{16,0},{1,17},{17,1},{2,18},{18,2},{3,19},{19,3},{4,20},{20... | collective-permute-start | bytes 354824 | tf_op jit(solution)/shard_map/ppermute | solution.py:267
  11.7 2.3 %copy-start.2 = (f32[896]{0:T(1024)S(1)}, f32[896]{0:T(1024)}, u32[]{:S(2)}) copy-start(f32[896]{0:T(1024)} %param.13) | copy-start | bytes 10756
  11.7 2.3 %copy-start.3 = (f32[896]{0:T(1024)S(1)}, f32[896]{0:T(1024)}, u32[]{:S(2)}) copy-start(f32[896]{0:T(1024)} %param.12) | copy-start | bytes 10756
  15.3 15.4 %all-to-all-start = ((bf16[16,4,2,1,896]{4,2,1,3,0:T(2,128)(2,1)}), bf16[16,4,2,1,896]{4,2,1,3,0:T(2,128)(2,1)S(1)}, u32[]{:S(2)}, u32[]{:S(2)}) async-start(bf16[16,4,2,1,896]{4,2,1,3,0:T(2,128)(2,1)} %bitcast.3), calls=%async_computation | async-start | bytes 458752 | tf_op jit(solution)/shard_map/all_to_all | solution.py:279

commit v13 on v11

--- a/solution.py
+++ b/solution.py
@@ -200,23 +200,36 @@
         params = block[row_count * views_in :].reshape(-1)[: params_in * 4 * block_count]
         return data, params.astype(jnp.float32).reshape(params_in, 4 * block_count)
 
-    head = pack(row_major[:, :halo], table[:RIM])
-    tail = pack(row_major[:, view_count - halo :], table[view_count - RIM :])
     group_idx = lax.axis_index("group")
     if group_count == 2:
-        outgoing = jnp.where(group_idx == 0, tail, head)
+        first = group_idx == 0
+        outgoing = pack(
+            jnp.where(first, row_major[:, view_count - halo :], row_major[:, :halo]),
+            jnp.where(first, table[view_count - RIM :], table[:RIM]),
+        )
         incoming = lax.ppermute(outgoing, "group", [(0, 1), (1, 0)])
-        from_low = jnp.where(group_idx == 0, jnp.zeros_like(incoming), incoming)
-        from_high = jnp.where(group_idx == 0, incoming, jnp.zeros_like(incoming))
+        other_data, other_params = unpack(incoming, halo, RIM)
+        blank_data = jnp.zeros_like(other_data)
+        blank_params = jnp.zeros_like(other_params)
+        extended = jnp.where(
+            first,
+            jnp.concatenate([blank_data, row_major, other_data], axis=1),
+            jnp.concatenate([other_data, row_major, blank_data], axis=1),
+        )
+        params = jnp.where(
+            first,
+            jnp.concatenate([blank_params, table, other_params], axis=0),
+            jnp.concatenate([other_params, table, blank_params], axis=0),
+        )
     else:
+        head = pack(row_major[:, :halo], table[:RIM])
+        tail = pack(row_major[:, view_count - halo :], table[view_count - RIM :])
         forward = [(i, i + 1) for i in range(group_count - 1)]
         backward = [(i + 1, i) for i in range(group_count - 1)]
-        from_low = lax.ppermute(tail, "group", forward)
-        from_high = lax.ppermute(head, "group", backward)
-    low_data, low_params = unpack(from_low, halo, RIM)
-    high_data, high_params = unpack(from_high, halo, RIM)
-    extended = jnp.concatenate([low_data, row_major, high_data], axis=1)
-    params = jnp.concatenate([low_params, table, high_params], axis=0)
+        low_data, low_params = unpack(lax.ppermute(tail, "group", forward), halo, RIM)
+        high_data, high_params = unpack(lax.ppermute(head, "group", backward), halo, RIM)
+        extended = jnp.concatenate([low_data, row_major, high_data], axis=1)
+        params = jnp.concatenate([low_params, table, high_params], axis=0)
     weights = params[:, block_count : 2 * block_count] + (
         params[:, 2 * block_count : 3 * block_count] + params[:, 3 * block_count :]
     )

time: 36.9 us -> 36.9 us (level)
  local copies, waits for them, and re-layouts: 5.44 us -> 4.84 us
  other arithmetic: 3.07 us -> 3.64 us
where the time goes in v13:
time: 36.9 us; the launch traced here: 36.6 us
  Pallas kernels  10.3 us (28%)
  starting transfers between devices  8.94 us (24%)
  waiting for transfers between devices  7.4 us (20%)
  local copies, waits for them, and re-layouts  4.84 us (13%)
  other arithmetic  3.64 us (10%)
  matrix products  1.32 us (4%)
    pallas_call x1, Pallas kernels, rebin_dual(): pl.pallas_call(kernel, out_shape=jax.ShapeDtypeStruct((rows, out_views, w...  10.3 us
    all_to_all x1, starting transfers between devices, local(): by_source = lax.all_to_all(by_dest, 'dev', 0, 0, tiled=True)  7.36 us
    all_to_all x1, waiting for transfers between devices, local(): by_source = lax.all_to_all(by_dest, 'dev', 0, 0, tiled=True)  5.08 us
    ppermute x1, waiting for transfers between devices, local(): incoming = lax.ppermute(outgoing, 'group', [(0, 1), (1, 0)])  2.32 us
    convert_element_type x1, other arithmetic, rebin_dual(): extended.astype(jnp.float32).reshape(rows, ext_views, 1, width)  1.76 us
    ppermute x1, starting transfers between devices, local(): incoming = lax.ppermute(outgoing, 'group', [(0, 1), (1, 0)])  1.58 us
    dot_general x1, matrix products, resample(): product = jnp.dot(flat, col_map, preferred_element_type=jnp.float32)  1.32 us
    exp2 x1, other arithmetic, prepare(): counts = counts * jnp.exp2(-exponent.astype(jnp.float32))[..., None]  0.82 us
  transfers between devices with their start and end apart: 2, of which 2 were waited for; matrix products, arithmetic and copies ran while one was open for 9% of the time, Pallas kernels for 0%

profile of v13, /device:TPU:0, one launch (start us, length us, event | category | flops | bytes accessed | tf_op | source)
XLA Modules:
  0.0 36.6 jit_solution(1547770953850900797)
XLA Ops:
  0.0 0.0 copy-start
  0.0 0.8 %multiply_exponential_fusion = f32[64,1,7]{0,1,2:T(1,128)S(1)} fusion(s32[64,1,7]{0,1,2:T(1,128)} %param.11), kind=kLoop, calls=%fused_computation.20 | loop fusion | flops 1344 | bytes 3584 | tf_op jit(solution)/shard_map/exp2 | solution.py:138
  0.8 0.1 copy.52
  0.9 0.0 copy-start.2
  0.9 0.1 mul.55
  1.1 0.0 copy-start.3
  1.1 0.0 copy-start.1
  1.1 0.3 copy-done
  1.4 0.0 copy-start.4
  1.4 0.0 copy-start.5
  1.4 1.3 %convolution_convert_fusion = bf16[64,896]{1,0:T(8,128)(2,1)S(1)} fusion(bf16[896,896]{1,0:T(8,128)(2,1)S(1)} %copy-done, f32[64,1,896]{2,0,1:T(8,128)S(1)} %mul.56, bf16[64,1,896]{2,0,1:T(8,128)(2,1)} %param.10, f32[896]{0:T(1024)} %param.13, f32[896]{0:T(1024)} %param.12), kind=kOutput, calls=%fused_computation | convolution fusion | flops 103448576 | bytes 2071552 | tf_op jit(solution)/shard_map/dot_general | solution.py:149
  2.8 0.7 %reshape_reshape.3 = bf16[16,4,1,896]{3,1,0,2:T(4,128)(2,1)} reshape(bf16[64,896]{1,0:T(8,128)(2,1)S(1)} %convolution_convert_fusion) | data formatting | bytes 229376 | tf_op jit(solution)/shard_map/reshape;reshape | solution.py:184
  3.4 7.4 %all-to-all-start = ((bf16[16,4,1,896]{3,1,2,0:T(4,128)(2,1)}), bf16[16,4,1,896]{3,1,2,0:T(4,128)(2,1)S(1)}, u32[]{:S(2)}, u32[]{:S(2)}) async-start(bf16[16,4,1,896]{3,1,2,0:T(4,128)(2,1)} %bitcast.2), calls=%async_computation | async-start | bytes 229376 | tf_op jit(solution)/shard_map/all_to_all | solution.py:185
  10.8 0.0 copy-done.2
  10.8 0.1 copy.42
  10.9 0.0 copy-done.3
  10.9 0.1 copy.41
  11.0 0.1 fusion.8
  11.1 0.1 reshape.149
  11.2 0.0 copy-done.1
  11.2 0.1 copy.50
  11.3 0.7 %reshape.153.w2_ref = bf16[96,96]{1,0:T(8,128)(2,1)} reshape(bf16[3,32,3,32]{3,2,1,0:T(4,128)(2,1)S(1)} %copy.50) | data formatting | bytes 36864 | tf_op jit(solution)/shard_map/reshape | solution.py:93
  12.0 0.0 copy-done.4
  12.0 0.1 copy.49
  12.1 0.6 %pad.10.w1_ref = bf16[32,16]{1,0:T(8,128)(2,1)} pad(bf16[32,9]{1,0:T(8,128)(2,1)S(1)} %copy.49, bf16[]{:T(256)} %constant.18.clone.1), padding=0_0x0_7 | pad | bytes 1602 | tf_op jit(solution)/shard_map/jit(_pad)/pad | solution.py:92
  12.7 0.0 copy-done.5
  12.7 0.7 %copy.51.kl_ref = f32[32,1]{1,0:T(8,128)} copy(f32[32,1]{0,1:T(1,128)S(1)} %bitcast_convert_fusion) | data formatting | bytes 256 | tf_op jit(solution)/shard_map/reshape | solution.py:94
  13.4 5.1 %all-to-all-done = bf16[16,4,1,896]{3,1,2,0:T(4,128)(2,1)S(1)} async-done(((bf16[16,4,1,896]{3,1,2,0:T(4,128)(2,1)}), bf16[16,4,1,896]{3,1,2,0:T(4,128)(2,1)S(1)}, u32[]{:S(2)}, u32[]{:S(2)}) %all-to-all-start) | async-done | bytes 114720 | tf_op jit(solution)/shard_map/all_to_all | solution.py:185
  18.5 0.2 copy.56
  18.8 1.6 %collective-permute-start = (bf16[41,896]{1,0:T(8,128)(2,1)S(1)}, bf16[41,896]{1,0:T(8,128)(2,1)S(1)}, u32[]{:S(2)}, u32[]{:S(2)}) collective-permute-start(bf16[41,896]{1,0:T(8,128)(2,1)S(1)} %pad_maximum_fusion), channel_id=1, source_target_pairs={{0,16},{16,0},{1,17},{17,1},{2,18},{18,2},{3,19},{19,3},{4,20},{20... | collective-permute-start | bytes 220424 | tf_op jit(solution)/shard_map/ppermute | solution.py:210
  20.4 0.6 %pad_add_fusion.bounds_ref = s32[2]{0:T(128)} fusion(s32[1]{0:T(128)} %constant.20.clone.1, s32[1]{0:T(128)} %bitcast.4), kind=kLoop, calls=%fused_computation.28 | loop fusion | flops 2 | bytes 16 | tf_op jit(solution)/shard_map/stack | solution.py:237
  21.0 2.3 %collective-permute-done = bf16[41,896]{1,0:T(8,128)(2,1)S(1)} collective-permute-done((bf16[41,896]{1,0:T(8,128)(2,1)S(1)}, bf16[41,896]{1,0:T(8,128)(2,1)S(1)}, u32[]{:S(2)}, u32[]{:S(2)}) %collective-permute-start) | collective-permute-done | bytes 73504 | tf_op jit(solution)/shard_map/ppermute | solution.py:210
  23.4 0.1 reshape.156
  23.5 0.1 maximum_select_fusion
  23.5 0.1 fusion.10
  23.6 0.1 pad_maximum_fusion.2
  23.7 0.7 %reshape.151.table_ref = f32[280]{0:T(512)} reshape(f32[20,14]{1,0:T(8,128)S(1)} %pad_maximum_fusion.2) | data formatting | bytes 2240 | tf_op jit(solution)/shard_map/reshape | solution.py:123
  24.4 0.1 broadcast_in_dim.10
  24.5 1.8 %fusion.ext_ref = f32[4,36,1,896]{3,2,1,0:T(1,128)} fusion(pred[]{:T(512)S(6)} %eq.3, bf16[4,10,1,896]{3,2,1,0:T(2,128)(2,1)S(1)} %concatenate.45, bf16[4,10,1,896]{3,2,1,0:T(2,128)(2,1)S(1)} %broadcast_in_dim.10, bf16[4,16,1,896]{3,2,1,0:T(2,128)(2,1)S(1)} %bitcast.20), kind=kLoop, calls=%fused_computation.2 | loop fusion | flops 774144 | bytes 774145 | tf_op jit(solution)/shard_map/convert_element_type | solution.py:125
  26.3 10.3 %shard_map.100 = bf16[4,16,896]{2,1,0:T(8,128)(2,1)} custom-call(f32[280]{0:T(512)} %reshape.151.table_ref, s32[2]{0:T(128)} %pad_add_fusion.bounds_ref, f32[4,36,1,896]{3,2,1,0:T(1,128)} %fusion.ext_ref, bf16[32,16]{1,0:T(8,128)(2,1)} %pad.10.w1_ref, bf16[96,96]{1,0:T(8,128)(2,1)} %reshape.153.w2_ref, f32[32,1]{1,0:T(8,128)} %copy.51.kl_ref), custom_call_target="tpu_custom_call" | custom-call | tf_op jit(solution)/shard_map/pallas_call | solution.py:118
  (15 shorter events, 0.3 us)
Async XLA Ops:
  0.0 1.4 %copy-start = (bf16[896,896]{1,0:T(8,128)(2,1)S(1)}, bf16[896,896]{1,0:T(8,128)(2,1)}, u32[]{:S(2)}) copy-start(bf16[896,896]{1,0:T(8,128)(2,1)} %param.14) | copy-start | bytes 4816900
  0.9 9.9 %copy-start.2 = (f32[16,7]{0,1:T(8,128)S(1)}, f32[16,7]{0,1:T(8,128)}, u32[]{:S(2)}) copy-start(f32[16,7]{0,1:T(8,128)} %param.16) | copy-start | bytes 1348
  1.1 9.9 %copy-start.3 = (s32[16,7]{0,1:T(8,128)S(1)}, s32[16,7]{0,1:T(8,128)}, u32[]{:S(2)}) copy-start(s32[16,7]{0,1:T(8,128)} %param.15) | copy-start | bytes 1348
  1.1 10.1 %copy-start.1 = (bf16[32,32,3,3]{1,0,3,2:T(8,128)(2,1)S(1)}, bf16[32,32,3,3]{1,0,3,2:T(8,128)(2,1)}, u32[]{:S(2)}) copy-start(bf16[32,32,3,3]{1,0,3,2:T(8,128)(2,1)} %param.18) | copy-start | bytes 55300
  1.4 10.5 %copy-start.4 = (bf16[32,3,3]{0,2,1:T(4,128)(2,1)S(1)}, bf16[32,3,3]{0,2,1:T(4,128)(2,1)}, u32[]{:S(2)}) copy-start(bf16[32,3,3]{0,2,1:T(4,128)(2,1)} %param.17) | copy-start | bytes 1732
  1.4 11.3 %copy-start.5 = (bf16[32]{0:T(256)(128)(2,1)S(1)}, bf16[32]{0:T(256)(128)(2,1)}, u32[]{:S(2)}) copy-start(bf16[32]{0:T(256)(128)(2,1)} %param.19) | copy-start | bytes 196
  3.4 15.0 %all-to-all-start = ((bf16[16,4,1,896]{3,1,2,0:T(4,128)(2,1)}), bf16[16,4,1,896]{3,1,2,0:T(4,128)(2,1)S(1)}, u32[]{:S(2)}, u32[]{:S(2)}) async-start(bf16[16,4,1,896]{3,1,2,0:T(4,128)(2,1)} %bitcast.2), calls=%async_computation | async-start | bytes 229376 | tf_op jit(solution)/shard_map/all_to_all | solution.py:185
  18.8 4.6 %collective-permute-start = (bf16[41,896]{1,0:T(8,128)(2,1)S(1)}, bf16[41,896]{1,0:T(8,128)(2,1)S(1)}, u32[]{:S(2)}, u32[]{:S(2)}) collective-permute-start(bf16[41,896]{1,0:T(8,128)(2,1)S(1)} %pad_maximum_fusion), channel_id=1, source_target_pairs={{0,16},{16,0},{1,17},{17,1},{2,18},{18,2},{3,19},{19,3},{4,20},{20... | collective-permute-start | bytes 220424 | tf_op jit(solution)/shard_map/ppermute | solution.py:210

commit v14 on v13

--- a/solution.py
+++ b/solution.py
@@ -203,24 +203,26 @@
     group_idx = lax.axis_index("group")
     if group_count == 2:
         first = group_idx == 0
-        outgoing = pack(
-            jnp.where(first, row_major[:, view_count - halo :], row_major[:, :halo]),
-            jnp.where(first, table[view_count - RIM :], table[:RIM]),
-        )
-        incoming = lax.ppermute(outgoing, "group", [(0, 1), (1, 0)])
-        other_data, other_params = unpack(incoming, halo, RIM)
+        swap = [(0, 1), (1, 0)]
+        plain = jnp.concatenate([rebin_offset.astype(jnp.float32), rebin_weight], axis=1)
+        edge = jnp.where(first, plain[view_count - RIM :], plain[:RIM])
+        other_params = lax.ppermute(edge, "group", swap)
+        blank_params = jnp.zeros_like(other_params)
+        params = jnp.where(
+            first,
+            jnp.concatenate([blank_params, plain, other_params], axis=0),
+            jnp.concatenate([other_params, plain, blank_params], axis=0),
+        )
+        outgoing = jnp.where(first, row_major[:, view_count - halo :], row_major[:, :halo])
+        other_data = lax.ppermute(outgoing, "group", swap)
         blank_data = jnp.zeros_like(other_data)
-        blank_params = jnp.zeros_like(other_params)
         extended = jnp.where(
             first,
             jnp.concatenate([blank_data, row_major, other_data], axis=1),
             jnp.concatenate([other_data, row_major, blank_data], axis=1),
         )
-        params = jnp.where(
-            first,
-            jnp.concatenate([blank_params, table, other_params], axis=0),
-            jnp.concatenate([other_params, table, blank_params], axis=0),
-        )
+        bounds = jnp.stack([view_start, total_views]).astype(jnp.int32)
+        return rebin_dual(extended, params, bounds, kern_first, kern_second, kern_last)
     else:
         head = pack(row_major[:, :halo], table[:RIM])
         tail = pack(row_major[:, view_count - halo :], table[view_count - RIM :])

time: 36.9 us -> 36.2 us (0.981)
  waiting for transfers between devices: 7.4 us -> 5.7 us
  starting transfers between devices: 8.94 us -> 10.5 us
    all_to_all x1, waiting for transfers between devices: 5.08 us -> 3.28 us  [local(): by_source = lax.all_to_all(by_dest, 'dev', 0, 0, tiled=True)]
    ppermute x1 -> x2, starting transfers between devices: 1.58 us -> 3.11 us  [the longest x1 1.58 us: local(): other_data = lax.ppermute(outgoing, 'group', swap)]
    reshape x4 -> x0, local copies, waits for them, and re-layouts: 0.81 us -> none  [the longest x1 0.69 us: rebin_dual(): table.reshape(-1)]
    select_n x0 -> x2, local copies, waits for them, and re-layouts: none -> 0.78 us  [local(): jnp.where(first, jnp.concatenate([blank_params, plain, other_params], axi...]
    ppermute x1 -> x2, waiting for transfers between devices: 2.32 us -> 2.42 us  [the longest x1 2.41 us: local(): other_data = lax.ppermute(outgoing, 'group', swap)]
  transfers between devices with their start and end apart: 2 -> 3, of which waited for: 2 -> 2; matrix products, arithmetic and copies ran while one was open for 9% -> 11% of each run, Pallas kernels for 0% -> 0%
where the time goes in v14:
time: 36.2 us; the launch traced here: 35.9 us
  starting transfers between devices  10.5 us (29%)
  Pallas kernels  10.3 us (28%)
  waiting for transfers between devices  5.7 us (16%)
  local copies, waits for them, and re-layouts  4.62 us (13%)
  other arithmetic  3.34 us (9%)
  matrix products  1.29 us (4%)
    pallas_call x1, Pallas kernels, rebin_dual(): pl.pallas_call(kernel, out_shape=jax.ShapeDtypeStruct((rows, out_views, w...  10.3 us
    all_to_all x1, starting transfers between devices, local(): by_source = lax.all_to_all(by_dest, 'dev', 0, 0, tiled=True)  7.36 us
    all_to_all x1, waiting for transfers between devices, local(): by_source = lax.all_to_all(by_dest, 'dev', 0, 0, tiled=True)  3.28 us
    ppermute x1, waiting for transfers between devices, local(): other_data = lax.ppermute(outgoing, 'group', swap)  2.41 us
    convert_element_type x1, other arithmetic, rebin_dual(): extended.astype(jnp.float32).reshape(rows, ext_views, 1, width)  1.77 us
    ppermute x1, starting transfers between devices, local(): other_data = lax.ppermute(outgoing, 'group', swap)  1.58 us
    ppermute x1, starting transfers between devices, local(): other_params = lax.ppermute(edge, 'group', swap)  1.53 us
    dot_general x1, matrix products, resample(): product = jnp.dot(flat, col_map, preferred_element_type=jnp.float32)  1.29 us
  transfers between devices with their start and end apart: 3, of which 2 were waited for; matrix products, arithmetic and copies ran while one was open for 11% of the time, Pallas kernels for 0%

profile of v14, /device:TPU:0, one launch (start us, length us, event | category | flops | bytes accessed | tf_op | source)
XLA Modules:
  0.0 35.9 jit_solution(4905884571556304476)
XLA Ops:
  0.0 0.0 copy-start
  0.0 0.8 %multiply_exponential_fusion = f32[64,1,7]{0,1,2:T(1,128)S(1)} fusion(s32[64,1,7]{0,1,2:T(1,128)} %param.11), kind=kLoop, calls=%fused_computation.17 | loop fusion | flops 1344 | bytes 3584 | tf_op jit(solution)/shard_map/exp2 | solution.py:138
  0.8 0.1 copy.34
  0.9 0.0 copy-start.3
  0.9 0.0 copy-start.2
  0.9 0.0 copy-start.5
  0.9 0.1 mul.56
  1.1 0.0 copy-start.1
  1.1 0.0 copy-start.4
  1.2 0.3 copy-done
  1.4 1.3 %convolution_convert_fusion = bf16[64,896]{1,0:T(8,128)(2,1)S(1)} fusion(bf16[896,896]{1,0:T(8,128)(2,1)S(1)} %copy-done, f32[64,1,896]{2,0,1:T(8,128)S(1)} %mul.57, bf16[64,1,896]{2,0,1:T(8,128)(2,1)} %param.10, f32[896]{0:T(1024)} %param.13, f32[896]{0:T(1024)} %param.12), kind=kOutput, calls=%fused_computation | convolution fusion | flops 103448576 | bytes 2071552 | tf_op jit(solution)/shard_map/dot_general | solution.py:149
  2.7 0.7 %reshape_reshape.3 = bf16[16,4,1,896]{3,1,0,2:T(4,128)(2,1)} reshape(bf16[64,896]{1,0:T(8,128)(2,1)S(1)} %convolution_convert_fusion) | data formatting | bytes 229376 | tf_op jit(solution)/shard_map/reshape;reshape | solution.py:184
  3.4 7.4 %all-to-all-start = ((bf16[16,4,1,896]{3,1,2,0:T(4,128)(2,1)}), bf16[16,4,1,896]{3,1,2,0:T(4,128)(2,1)S(1)}, u32[]{:S(2)}, u32[]{:S(2)}) async-start(bf16[16,4,1,896]{3,1,2,0:T(4,128)(2,1)} %bitcast.3), calls=%async_computation | async-start | bytes 229376 | tf_op jit(solution)/shard_map/all_to_all | solution.py:185
  10.8 0.0 copy-done.3
  10.8 0.0 copy-done.2
  10.8 0.1 fusion.6
  10.9 1.5 %collective-permute-start = (f32[2,14]{0,1:T(8,128)S(1)}, f32[2,14]{0,1:T(8,128)S(1)}, u32[]{:S(2)}, u32[]{:S(2)}) collective-permute-start(f32[2,14]{0,1:T(8,128)S(1)} %fusion.6), channel_id=1, source_target_pairs={{0,16},{16,0},{1,17},{17,1},{2,18},{18,2},{3,19},{19,3},{4,20},{20... | collective-permute-start | bytes 344 | tf_op jit(solution)/shard_map/ppermute | solution.py:209
  12.4 0.0 copy-done.5
  12.4 0.0 copy-done.1
  12.4 0.1 copy.32
  12.5 0.7 %reshape.132.w2_ref = bf16[96,96]{1,0:T(8,128)(2,1)} reshape(bf16[3,32,3,32]{3,2,1,0:T(4,128)(2,1)S(1)} %copy.32) | data formatting | bytes 36864 | tf_op jit(solution)/shard_map/reshape | solution.py:93
  13.2 0.0 copy-done.4
  13.2 0.1 copy.31
  13.3 0.7 %copy.33.kl_ref = f32[32,1]{1,0:T(8,128)} copy(f32[32,1]{0,1:T(1,128)S(1)} %bitcast_convert_fusion) | data formatting | bytes 256 | tf_op jit(solution)/shard_map/reshape | solution.py:94
  14.0 0.6 %pad.4.w1_ref = bf16[32,16]{1,0:T(8,128)(2,1)} pad(bf16[32,9]{1,0:T(8,128)(2,1)S(1)} %copy.31, bf16[]{:T(256)} %constant.17.clone.1), padding=0_0x0_7 | pad | bytes 1602 | tf_op jit(solution)/shard_map/jit(_pad)/pad | solution.py:92
  14.6 0.6 %pad_add_fusion.bounds_ref = s32[2]{0:T(128)} fusion(s32[1]{0:T(128)} %constant.16.clone.1, s32[1]{0:T(128)} %bitcast), kind=kLoop, calls=%fused_computation.18 | loop fusion | flops 2 | bytes 16 | tf_op jit(solution)/shard_map/stack | solution.py:224
  15.2 3.3 %all-to-all-done = bf16[16,4,1,896]{3,1,2,0:T(4,128)(2,1)S(1)} async-done(((bf16[16,4,1,896]{3,1,2,0:T(4,128)(2,1)}), bf16[16,4,1,896]{3,1,2,0:T(4,128)(2,1)S(1)}, u32[]{:S(2)}, u32[]{:S(2)}) %all-to-all-start) | async-done | bytes 114720 | tf_op jit(solution)/shard_map/all_to_all | solution.py:185
  18.5 0.2 copy.39
  18.7 1.6 %collective-permute-start.1 = (bf16[4,10,896]{2,1,0:T(8,128)(2,1)S(1)}, bf16[4,10,896]{2,1,0:T(8,128)(2,1)S(1)}, u32[]{:S(2)}, u32[]{:S(2)}) collective-permute-start(bf16[4,10,896]{2,1,0:T(8,128)(2,1)S(1)} %slice_select_fusion), channel_id=1, source_target_pairs={{0,16},{16,0},{1,17},{17,1},{2,18},{18,2},{3,19},{19,3},{4,20},{20... | collective-permute-start | bytes 215048 | tf_op jit(solution)/shard_map/ppermute | solution.py:217
  20.3 0.0 collective-permute-done
  20.3 0.1 maximum_select_fusion
  20.4 0.1 copy.24
  20.5 0.7 %select_n.47.table_ref = f32[280]{0:T(512)} reshape(f32[20,14]{1,0:T(8,128)S(1)} %copy.24) | data formatting | bytes 2240 | tf_op jit(solution)/shard_map/jit(_where)/select_n | solution.py:211
  21.2 2.4 %collective-permute-done.1 = bf16[4,10,896]{2,1,0:T(8,128)(2,1)S(1)} collective-permute-done((bf16[4,10,896]{2,1,0:T(8,128)(2,1)S(1)}, bf16[4,10,896]{2,1,0:T(8,128)(2,1)S(1)}, u32[]{:S(2)}, u32[]{:S(2)}) %collective-permute-start.1) | collective-permute-done | bytes 71712 | tf_op jit(solution)/shard_map/ppermute | solution.py:217
  23.6 0.1 copy.29
  23.7 0.1 broadcast_in_dim.2
  23.8 1.8 %fusion.ext_ref = f32[4,36,1,896]{3,2,1,0:T(1,128)} fusion(pred[]{:T(512)S(6)} %eq.3, bf16[4,10,1,896]{3,2,1,0:T(2,128)(2,1)S(1)} %copy.29, bf16[4,10,1,896]{3,2,1,0:T(2,128)(2,1)S(1)} %broadcast_in_dim.2, bf16[4,16,1,896]{3,2,1,0:T(2,128)(2,1)S(1)} %bitcast.23), kind=kLoop, calls=%fused_computation.2 | loop fusion | flops 774144 | bytes 774145 | tf_op jit(solution)/shard_map/convert_element_type | solution.py:125
  25.6 10.3 %shard_map.100 = bf16[4,16,896]{2,1,0:T(8,128)(2,1)} custom-call(f32[280]{0:T(512)} %select_n.47.table_ref, s32[2]{0:T(128)} %pad_add_fusion.bounds_ref, f32[4,36,1,896]{3,2,1,0:T(1,128)} %fusion.ext_ref, bf16[32,16]{1,0:T(8,128)(2,1)} %pad.4.w1_ref, bf16[96,96]{1,0:T(8,128)(2,1)} %reshape.132.w2_ref, f32[32,1]{1,0:T(8,128)} %copy.33.kl_ref), custom_call_target="tpu_custom_call" | custom-call | tf_op jit(solution)/shard_map/pallas_call | solution.py:118
  (8 shorter events, 0.2 us)
Async XLA Ops:
  0.0 1.4 %copy-start = (bf16[896,896]{1,0:T(8,128)(2,1)S(1)}, bf16[896,896]{1,0:T(8,128)(2,1)}, u32[]{:S(2)}) copy-start(bf16[896,896]{1,0:T(8,128)(2,1)} %param.14) | copy-start | bytes 4816900
  0.9 9.9 %copy-start.3 = (s32[16,7]{0,1:T(8,128)S(1)}, s32[16,7]{0,1:T(8,128)}, u32[]{:S(2)}) copy-start(s32[16,7]{0,1:T(8,128)} %param.15) | copy-start | bytes 1348
  0.9 9.9 %copy-start.2 = (f32[16,7]{0,1:T(8,128)S(1)}, f32[16,7]{0,1:T(8,128)}, u32[]{:S(2)}) copy-start(f32[16,7]{0,1:T(8,128)} %param.16) | copy-start | bytes 1348
  0.9 11.5 %copy-start.5 = (bf16[32]{0:T(256)(128)(2,1)S(1)}, bf16[32]{0:T(256)(128)(2,1)}, u32[]{:S(2)}) copy-start(bf16[32]{0:T(256)(128)(2,1)} %param.19) | copy-start | bytes 196
  1.1 11.4 %copy-start.1 = (bf16[32,32,3,3]{1,0,3,2:T(8,128)(2,1)S(1)}, bf16[32,32,3,3]{1,0,3,2:T(8,128)(2,1)}, u32[]{:S(2)}) copy-start(bf16[32,32,3,3]{1,0,3,2:T(8,128)(2,1)} %param.18) | copy-start | bytes 55300
  1.1 12.1 %copy-start.4 = (bf16[32,3,3]{0,2,1:T(4,128)(2,1)S(1)}, bf16[32,3,3]{0,2,1:T(4,128)(2,1)}, u32[]{:S(2)}) copy-start(bf16[32,3,3]{0,2,1:T(4,128)(2,1)} %param.17) | copy-start | bytes 1732
  3.4 15.0 %all-to-all-start = ((bf16[16,4,1,896]{3,1,2,0:T(4,128)(2,1)}), bf16[16,4,1,896]{3,1,2,0:T(4,128)(2,1)S(1)}, u32[]{:S(2)}, u32[]{:S(2)}) async-start(bf16[16,4,1,896]{3,1,2,0:T(4,128)(2,1)} %bitcast.3), calls=%async_computation | async-start | bytes 229376 | tf_op jit(solution)/shard_map/all_to_all | solution.py:185
  10.9 9.4 %collective-permute-start = (f32[2,14]{0,1:T(8,128)S(1)}, f32[2,14]{0,1:T(8,128)S(1)}, u32[]{:S(2)}, u32[]{:S(2)}) collective-permute-start(f32[2,14]{0,1:T(8,128)S(1)} %fusion.6), channel_id=1, source_target_pairs={{0,16},{16,0},{1,17},{17,1},{2,18},{18,2},{3,19},{19,3},{4,20},{20... | collective-permute-start | bytes 344 | tf_op jit(solution)/shard_map/ppermute | solution.py:209
  18.7 4.9 %collective-permute-start.1 = (bf16[4,10,896]{2,1,0:T(8,128)(2,1)S(1)}, bf16[4,10,896]{2,1,0:T(8,128)(2,1)S(1)}, u32[]{:S(2)}, u32[]{:S(2)}) collective-permute-start(bf16[4,10,896]{2,1,0:T(8,128)(2,1)S(1)} %slice_select_fusion), channel_id=1, source_target_pairs={{0,16},{16,0},{1,17},{17,1},{2,18},{18,2},{3,19},{19,3},{4,20},{20... | collective-permute-start | bytes 215048 | tf_op jit(solution)/shard_map/ppermute | solution.py:217

commit v15 on v14

--- a/solution.py
+++ b/solution.py
@@ -65,18 +65,25 @@
         feat_ref[u * channels : (u + 1) * channels, :] = hidden
     w2 = w2_ref[...]
     kl = kl_ref[...]
-    for v in range(out_views):
-        window = feat_ref[v * channels : (v + 3) * channels, :]
-        part = jnp.dot(w2, window, preferred_element_type=jnp.float32)
-        second = part[channels : 2 * channels]
-        second = second + jnp.where(keep_left, pltpu.roll(part[:channels], 1, 1), 0.0)
-        second = second + jnp.where(
-            keep_right, pltpu.roll(part[2 * channels :], width - 1, 1), 0.0
-        )
-        second = jnp.maximum(second, 0.0).astype(jnp.bfloat16).astype(jnp.float32)
-        mix = jnp.sum(kl * second, axis=0, keepdims=True)
-        centre = sig_ref[3 * (v + 2) + 1 : 3 * (v + 2) + 2, :]
-        dual_ref[v : v + 1, :] = centre + mix
+    pair = 2 if out_views % 2 == 0 else 1
+    for v0 in range(0, out_views, pair):
+        window = jnp.concatenate(
+            [feat_ref[v * channels : (v + 3) * channels, :] for v in range(v0, v0 + pair)],
+            axis=1,
+        )
+        parts = jnp.dot(w2, window, preferred_element_type=jnp.float32)
+        for j in range(pair):
+            v = v0 + j
+            part = parts[:, j * width : (j + 1) * width]
+            second = part[channels : 2 * channels]
+            second = second + jnp.where(keep_left, pltpu.roll(part[:channels], 1, 1), 0.0)
+            second = second + jnp.where(
+                keep_right, pltpu.roll(part[2 * channels :], width - 1, 1), 0.0
+            )
+            second = jnp.maximum(second, 0.0).astype(jnp.bfloat16).astype(jnp.float32)
+            mix = jnp.sum(kl * second, axis=0, keepdims=True)
+            centre = sig_ref[3 * (v + 2) + 1 : 3 * (v + 2) + 2, :]
+            dual_ref[v : v + 1, :] = centre + mix
     out_ref[0] = dual_ref[...].astype(out_ref.dtype)
 
 

time: 36.2 us -> 36.1 us (level)
  no operation moved by 1% of the time
where the time goes in v15:
time: 36.1 us; the launch traced here: 35.8 us
  starting transfers between devices  10.5 us (29%)
  Pallas kernels  10.2 us (28%)
  waiting for transfers between devices  5.7 us (16%)
  local copies, waits for them, and re-layouts  4.62 us (13%)
  other arithmetic  3.34 us (9%)
  matrix products  1.29 us (4%)
    pallas_call x1, Pallas kernels, rebin_dual(): pl.pallas_call(kernel, out_shape=jax.ShapeDtypeStruct((rows, out_views, w...  10.2 us
    all_to_all x1, starting transfers between devices, local(): by_source = lax.all_to_all(by_dest, 'dev', 0, 0, tiled=True)  7.36 us
    all_to_all x1, waiting for transfers between devices, local(): by_source = lax.all_to_all(by_dest, 'dev', 0, 0, tiled=True)  3.28 us
    ppermute x1, waiting for transfers between devices, local(): other_data = lax.ppermute(outgoing, 'group', swap)  2.41 us
    convert_element_type x1, other arithmetic, rebin_dual(): extended.astype(jnp.float32).reshape(rows, ext_views, 1, width)  1.77 us
    ppermute x1, starting transfers between devices, local(): other_data = lax.ppermute(outgoing, 'group', swap)  1.58 us
    ppermute x1, starting transfers between devices, local(): other_params = lax.ppermute(edge, 'group', swap)  1.53 us
    dot_general x1, matrix products, resample(): product = jnp.dot(flat, col_map, preferred_element_type=jnp.float32)  1.29 us
  transfers between devices with their start and end apart: 3, of which 2 were waited for; matrix products, arithmetic and copies ran while one was open for 11% of the time, Pallas kernels for 0%

profile of v15, /device:TPU:0, one launch (start us, length us, event | category | flops | bytes accessed | tf_op | source)
XLA Modules:
  0.0 35.8 jit_solution(9335483929906260111)
XLA Ops:
  0.0 0.0 copy-start
  0.0 0.8 %multiply_exponential_fusion = f32[64,1,7]{0,1,2:T(1,128)S(1)} fusion(s32[64,1,7]{0,1,2:T(1,128)} %param.11), kind=kLoop, calls=%fused_computation.17 | loop fusion | flops 1344 | bytes 3584 | tf_op jit(solution)/shard_map/exp2 | solution.py:145
  0.8 0.1 copy.34
  0.9 0.0 copy-start.3
  0.9 0.0 copy-start.2
  0.9 0.0 copy-start.5
  0.9 0.1 mul.56
  1.1 0.0 copy-start.1
  1.1 0.0 copy-start.4
  1.2 0.3 copy-done
  1.4 1.3 %convolution_convert_fusion = bf16[64,896]{1,0:T(8,128)(2,1)S(1)} fusion(bf16[896,896]{1,0:T(8,128)(2,1)S(1)} %copy-done, f32[64,1,896]{2,0,1:T(8,128)S(1)} %mul.57, bf16[64,1,896]{2,0,1:T(8,128)(2,1)} %param.10, f32[896]{0:T(1024)} %param.13, f32[896]{0:T(1024)} %param.12), kind=kOutput, calls=%fused_computation | convolution fusion | flops 103448576 | bytes 2071552 | tf_op jit(solution)/shard_map/dot_general | solution.py:156
  2.7 0.7 %reshape_reshape.3 = bf16[16,4,1,896]{3,1,0,2:T(4,128)(2,1)} reshape(bf16[64,896]{1,0:T(8,128)(2,1)S(1)} %convolution_convert_fusion) | data formatting | bytes 229376 | tf_op jit(solution)/shard_map/reshape;reshape | solution.py:191
  3.4 7.4 %all-to-all-start = ((bf16[16,4,1,896]{3,1,2,0:T(4,128)(2,1)}), bf16[16,4,1,896]{3,1,2,0:T(4,128)(2,1)S(1)}, u32[]{:S(2)}, u32[]{:S(2)}) async-start(bf16[16,4,1,896]{3,1,2,0:T(4,128)(2,1)} %bitcast.3), calls=%async_computation | async-start | bytes 229376 | tf_op jit(solution)/shard_map/all_to_all | solution.py:192
  10.8 0.0 copy-done.3
  10.8 0.0 copy-done.2
  10.8 0.1 fusion.6
  10.9 1.5 %collective-permute-start = (f32[2,14]{0,1:T(8,128)S(1)}, f32[2,14]{0,1:T(8,128)S(1)}, u32[]{:S(2)}, u32[]{:S(2)}) collective-permute-start(f32[2,14]{0,1:T(8,128)S(1)} %fusion.6), channel_id=1, source_target_pairs={{0,16},{16,0},{1,17},{17,1},{2,18},{18,2},{3,19},{19,3},{4,20},{20... | collective-permute-start | bytes 344 | tf_op jit(solution)/shard_map/ppermute | solution.py:216
  12.4 0.0 copy-done.5
  12.4 0.0 copy-done.1
  12.4 0.1 copy.32
  12.5 0.7 %reshape.132.w2_ref = bf16[96,96]{1,0:T(8,128)(2,1)} reshape(bf16[3,32,3,32]{3,2,1,0:T(4,128)(2,1)S(1)} %copy.32) | data formatting | bytes 36864 | tf_op jit(solution)/shard_map/reshape | solution.py:100
  13.2 0.0 copy-done.4
  13.2 0.1 copy.31
  13.3 0.7 %copy.33.kl_ref = f32[32,1]{1,0:T(8,128)} copy(f32[32,1]{0,1:T(1,128)S(1)} %bitcast_convert_fusion) | data formatting | bytes 256 | tf_op jit(solution)/shard_map/reshape | solution.py:101
  14.0 0.6 %pad.4.w1_ref = bf16[32,16]{1,0:T(8,128)(2,1)} pad(bf16[32,9]{1,0:T(8,128)(2,1)S(1)} %copy.31, bf16[]{:T(256)} %constant.17.clone.1), padding=0_0x0_7 | pad | bytes 1602 | tf_op jit(solution)/shard_map/jit(_pad)/pad | solution.py:99
  14.6 0.6 %pad_add_fusion.bounds_ref = s32[2]{0:T(128)} fusion(s32[1]{0:T(128)} %constant.16.clone.1, s32[1]{0:T(128)} %bitcast), kind=kLoop, calls=%fused_computation.18 | loop fusion | flops 2 | bytes 16 | tf_op jit(solution)/shard_map/stack | solution.py:231
  15.2 3.3 %all-to-all-done = bf16[16,4,1,896]{3,1,2,0:T(4,128)(2,1)S(1)} async-done(((bf16[16,4,1,896]{3,1,2,0:T(4,128)(2,1)}), bf16[16,4,1,896]{3,1,2,0:T(4,128)(2,1)S(1)}, u32[]{:S(2)}, u32[]{:S(2)}) %all-to-all-start) | async-done | bytes 114720 | tf_op jit(solution)/shard_map/all_to_all | solution.py:192
  18.5 0.2 copy.39
  18.7 1.6 %collective-permute-start.1 = (bf16[4,10,896]{2,1,0:T(8,128)(2,1)S(1)}, bf16[4,10,896]{2,1,0:T(8,128)(2,1)S(1)}, u32[]{:S(2)}, u32[]{:S(2)}) collective-permute-start(bf16[4,10,896]{2,1,0:T(8,128)(2,1)S(1)} %slice_select_fusion), channel_id=1, source_target_pairs={{0,16},{16,0},{1,17},{17,1},{2,18},{18,2},{3,19},{19,3},{4,20},{20... | collective-permute-start | bytes 215048 | tf_op jit(solution)/shard_map/ppermute | solution.py:224
  20.3 0.0 collective-permute-done
  20.3 0.1 maximum_select_fusion
  20.4 0.1 copy.24
  20.5 0.7 %select_n.47.table_ref = f32[280]{0:T(512)} reshape(f32[20,14]{1,0:T(8,128)S(1)} %copy.24) | data formatting | bytes 2240 | tf_op jit(solution)/shard_map/jit(_where)/select_n | solution.py:218
  21.2 2.4 %collective-permute-done.1 = bf16[4,10,896]{2,1,0:T(8,128)(2,1)S(1)} collective-permute-done((bf16[4,10,896]{2,1,0:T(8,128)(2,1)S(1)}, bf16[4,10,896]{2,1,0:T(8,128)(2,1)S(1)}, u32[]{:S(2)}, u32[]{:S(2)}) %collective-permute-start.1) | collective-permute-done | bytes 71712 | tf_op jit(solution)/shard_map/ppermute | solution.py:224
  23.6 0.1 copy.29
  23.7 0.1 broadcast_in_dim.2
  23.8 1.8 %fusion.ext_ref = f32[4,36,1,896]{3,2,1,0:T(1,128)} fusion(pred[]{:T(512)S(6)} %eq.3, bf16[4,10,1,896]{3,2,1,0:T(2,128)(2,1)S(1)} %copy.29, bf16[4,10,1,896]{3,2,1,0:T(2,128)(2,1)S(1)} %broadcast_in_dim.2, bf16[4,16,1,896]{3,2,1,0:T(2,128)(2,1)S(1)} %bitcast.23), kind=kLoop, calls=%fused_computation.2 | loop fusion | flops 774144 | bytes 774145 | tf_op jit(solution)/shard_map/convert_element_type | solution.py:132
  25.6 10.2 %shard_map.100 = bf16[4,16,896]{2,1,0:T(8,128)(2,1)} custom-call(f32[280]{0:T(512)} %select_n.47.table_ref, s32[2]{0:T(128)} %pad_add_fusion.bounds_ref, f32[4,36,1,896]{3,2,1,0:T(1,128)} %fusion.ext_ref, bf16[32,16]{1,0:T(8,128)(2,1)} %pad.4.w1_ref, bf16[96,96]{1,0:T(8,128)(2,1)} %reshape.132.w2_ref, f32[32,1]{1,0:T(8,128)} %copy.33.kl_ref), custom_call_target="tpu_custom_call" | custom-call | tf_op jit(solution)/shard_map/pallas_call | solution.py:125
  (8 shorter events, 0.2 us)
Async XLA Ops:
  0.0 1.4 %copy-start = (bf16[896,896]{1,0:T(8,128)(2,1)S(1)}, bf16[896,896]{1,0:T(8,128)(2,1)}, u32[]{:S(2)}) copy-start(bf16[896,896]{1,0:T(8,128)(2,1)} %param.14) | copy-start | bytes 4816900
  0.9 9.9 %copy-start.3 = (s32[16,7]{0,1:T(8,128)S(1)}, s32[16,7]{0,1:T(8,128)}, u32[]{:S(2)}) copy-start(s32[16,7]{0,1:T(8,128)} %param.15) | copy-start | bytes 1348
  0.9 9.9 %copy-start.2 = (f32[16,7]{0,1:T(8,128)S(1)}, f32[16,7]{0,1:T(8,128)}, u32[]{:S(2)}) copy-start(f32[16,7]{0,1:T(8,128)} %param.16) | copy-start | bytes 1348
  0.9 11.5 %copy-start.5 = (bf16[32]{0:T(256)(128)(2,1)S(1)}, bf16[32]{0:T(256)(128)(2,1)}, u32[]{:S(2)}) copy-start(bf16[32]{0:T(256)(128)(2,1)} %param.19) | copy-start | bytes 196
  1.1 11.4 %copy-start.1 = (bf16[32,32,3,3]{1,0,3,2:T(8,128)(2,1)S(1)}, bf16[32,32,3,3]{1,0,3,2:T(8,128)(2,1)}, u32[]{:S(2)}) copy-start(bf16[32,32,3,3]{1,0,3,2:T(8,128)(2,1)} %param.18) | copy-start | bytes 55300
  1.1 12.1 %copy-start.4 = (bf16[32,3,3]{0,2,1:T(4,128)(2,1)S(1)}, bf16[32,3,3]{0,2,1:T(4,128)(2,1)}, u32[]{:S(2)}) copy-start(bf16[32,3,3]{0,2,1:T(4,128)(2,1)} %param.17) | copy-start | bytes 1732
  3.4 15.0 %all-to-all-start = ((bf16[16,4,1,896]{3,1,2,0:T(4,128)(2,1)}), bf16[16,4,1,896]{3,1,2,0:T(4,128)(2,1)S(1)}, u32[]{:S(2)}, u32[]{:S(2)}) async-start(bf16[16,4,1,896]{3,1,2,0:T(4,128)(2,1)} %bitcast.3), calls=%async_computation | async-start | bytes 229376 | tf_op jit(solution)/shard_map/all_to_all | solution.py:192
  10.9 9.4 %collective-permute-start = (f32[2,14]{0,1:T(8,128)S(1)}, f32[2,14]{0,1:T(8,128)S(1)}, u32[]{:S(2)}, u32[]{:S(2)}) collective-permute-start(f32[2,14]{0,1:T(8,128)S(1)} %fusion.6), channel_id=1, source_target_pairs={{0,16},{16,0},{1,17},{17,1},{2,18},{18,2},{3,19},{19,3},{4,20},{20... | collective-permute-start | bytes 344 | tf_op jit(solution)/shard_map/ppermute | solution.py:216
  18.7 4.9 %collective-permute-start.1 = (bf16[4,10,896]{2,1,0:T(8,128)(2,1)S(1)}, bf16[4,10,896]{2,1,0:T(8,128)(2,1)S(1)}, u32[]{:S(2)}, u32[]{:S(2)}) collective-permute-start(bf16[4,10,896]{2,1,0:T(8,128)(2,1)S(1)} %slice_select_fusion), channel_id=1, source_target_pairs={{0,16},{16,0},{1,17},{17,1},{2,18},{18,2},{3,19},{19,3},{4,20},{20... | collective-permute-start | bytes 215048 | tf_op jit(solution)/shard_map/ppermute | solution.py:224

commit v16 on v14

--- a/solution.py
+++ b/solution.py
@@ -43,8 +43,8 @@
             low = u + table_ref[entry].astype(jnp.int32) + REACH
             frac = table_ref[entry + block_count]
             cols = pl.ds(k * col_block, col_block)
-            lower = ext_ref[0, low, :, cols]
-            upper = ext_ref[0, low + 1, :, cols]
+            lower = ext_ref[0, low, :, cols].astype(jnp.float32)
+            upper = ext_ref[0, low + 1, :, cols].astype(jnp.float32)
             value = ((1.0 - frac) * lower + frac * upper).astype(jnp.bfloat16)
             sig_ref[3 * u + 1 : 3 * u + 2, cols] = value.astype(jnp.float32) * keep
         row = sig_ref[3 * u + 1 : 3 * u + 2, :]
@@ -122,7 +122,7 @@
     )(
         table.reshape(-1),
         bounds,
-        extended.astype(jnp.float32).reshape(rows, ext_views, 1, width),
+        extended.reshape(rows, ext_views, 1, width),
         w1.astype(jnp.bfloat16),
         w2.astype(jnp.bfloat16),
         kl,

time: 36.2 us -> 36.3 us (level)
    select_n x0 -> x1, other arithmetic: none -> 1.78 us  [local(): jnp.where(first, jnp.concatenate([blank_data, row_major, other_data], axi...]
    convert_element_type x1 -> x0, other arithmetic: 1.77 us -> none  [rebin_dual(): extended.astype(jnp.float32).reshape(rows, ext_views, 1, width)]
where the time goes in v16:
time: 36.3 us; the launch traced here: 36 us
  starting transfers between devices  10.5 us (29%)
  Pallas kernels  10.4 us (29%)
  waiting for transfers between devices  5.7 us (16%)
  local copies, waits for them, and re-layouts  4.62 us (13%)
  other arithmetic  3.36 us (9%)
  matrix products  1.29 us (4%)
    pallas_call x1, Pallas kernels, rebin_dual(): pl.pallas_call(kernel, out_shape=jax.ShapeDtypeStruct((rows, out_views, w...  10.4 us
    all_to_all x1, starting transfers between devices, local(): by_source = lax.all_to_all(by_dest, 'dev', 0, 0, tiled=True)  7.36 us
    all_to_all x1, waiting for transfers between devices, local(): by_source = lax.all_to_all(by_dest, 'dev', 0, 0, tiled=True)  3.28 us
    ppermute x1, waiting for transfers between devices, local(): other_data = lax.ppermute(outgoing, 'group', swap)  2.41 us
    select_n x1, other arithmetic, local(): jnp.where(first, jnp.concatenate([blank_data, row_major, other_data], axi...  1.78 us
    ppermute x1, starting transfers between devices, local(): other_data = lax.ppermute(outgoing, 'group', swap)  1.58 us
    ppermute x1, starting transfers between devices, local(): other_params = lax.ppermute(edge, 'group', swap)  1.53 us
    dot_general x1, matrix products, resample(): product = jnp.dot(flat, col_map, preferred_element_type=jnp.float32)  1.29 us
  transfers between devices with their start and end apart: 3, of which 2 were waited for; matrix products, arithmetic and copies ran while one was open for 11% of the time, Pallas kernels for 0%

profile of v16, /device:TPU:0, one launch (start us, length us, event | category | flops | bytes accessed | tf_op | source)
XLA Modules:
  0.0 36.0 jit_solution(12970536456436683953)
XLA Ops:
  0.0 0.0 copy-start
  0.0 0.8 %multiply_exponential_fusion = f32[64,1,7]{0,1,2:T(1,128)S(1)} fusion(s32[64,1,7]{0,1,2:T(1,128)} %param.11), kind=kLoop, calls=%fused_computation.16 | loop fusion | flops 1344 | bytes 3584 | tf_op jit(solution)/shard_map/exp2 | solution.py:138
  0.8 0.1 copy.34
  0.9 0.0 copy-start.3
  0.9 0.0 copy-start.2
  0.9 0.0 copy-start.5
  0.9 0.1 mul.56
  1.1 0.0 copy-start.1
  1.1 0.0 copy-start.4
  1.2 0.3 copy-done
  1.4 1.3 %convolution_convert_fusion = bf16[64,896]{1,0:T(8,128)(2,1)S(1)} fusion(bf16[896,896]{1,0:T(8,128)(2,1)S(1)} %copy-done, f32[64,1,896]{2,0,1:T(8,128)S(1)} %mul.57, bf16[64,1,896]{2,0,1:T(8,128)(2,1)} %param.10, f32[896]{0:T(1024)} %param.13, f32[896]{0:T(1024)} %param.12), kind=kOutput, calls=%fused_computation | convolution fusion | flops 103448576 | bytes 2071552 | tf_op jit(solution)/shard_map/dot_general | solution.py:149
  2.7 0.7 %reshape_reshape.3 = bf16[16,4,1,896]{3,1,0,2:T(4,128)(2,1)} reshape(bf16[64,896]{1,0:T(8,128)(2,1)S(1)} %convolution_convert_fusion) | data formatting | bytes 229376 | tf_op jit(solution)/shard_map/reshape;reshape | solution.py:184
  3.4 7.4 %all-to-all-start = ((bf16[16,4,1,896]{3,1,2,0:T(4,128)(2,1)}), bf16[16,4,1,896]{3,1,2,0:T(4,128)(2,1)S(1)}, u32[]{:S(2)}, u32[]{:S(2)}) async-start(bf16[16,4,1,896]{3,1,2,0:T(4,128)(2,1)} %bitcast.3), calls=%async_computation | async-start | bytes 229376 | tf_op jit(solution)/shard_map/all_to_all | solution.py:185
  10.8 0.0 copy-done.3
  10.8 0.0 copy-done.2
  10.8 0.1 fusion.5
  10.9 1.5 %collective-permute-start = (f32[2,14]{0,1:T(8,128)S(1)}, f32[2,14]{0,1:T(8,128)S(1)}, u32[]{:S(2)}, u32[]{:S(2)}) collective-permute-start(f32[2,14]{0,1:T(8,128)S(1)} %fusion.5), channel_id=1, source_target_pairs={{0,16},{16,0},{1,17},{17,1},{2,18},{18,2},{3,19},{19,3},{4,20},{20... | collective-permute-start | bytes 344 | tf_op jit(solution)/shard_map/ppermute | solution.py:209
  12.4 0.0 copy-done.5
  12.4 0.0 copy-done.1
  12.4 0.1 copy.32
  12.5 0.7 %reshape.129.w2_ref = bf16[96,96]{1,0:T(8,128)(2,1)} reshape(bf16[3,32,3,32]{3,2,1,0:T(4,128)(2,1)S(1)} %copy.32) | data formatting | bytes 36864 | tf_op jit(solution)/shard_map/reshape | solution.py:93
  13.2 0.0 copy-done.4
  13.2 0.1 copy.31
  13.3 0.7 %copy.33.kl_ref = f32[32,1]{1,0:T(8,128)} copy(f32[32,1]{0,1:T(1,128)S(1)} %bitcast_convert_fusion) | data formatting | bytes 256 | tf_op jit(solution)/shard_map/reshape | solution.py:94
  14.0 0.6 %pad.4.w1_ref = bf16[32,16]{1,0:T(8,128)(2,1)} pad(bf16[32,9]{1,0:T(8,128)(2,1)S(1)} %copy.31, bf16[]{:T(256)} %constant.17.clone.1), padding=0_0x0_7 | pad | bytes 1602 | tf_op jit(solution)/shard_map/jit(_pad)/pad | solution.py:92
  14.6 0.6 %pad_add_fusion.bounds_ref = s32[2]{0:T(128)} fusion(s32[1]{0:T(128)} %constant.16.clone.1, s32[1]{0:T(128)} %bitcast), kind=kLoop, calls=%fused_computation.17 | loop fusion | flops 2 | bytes 16 | tf_op jit(solution)/shard_map/stack | solution.py:224
  15.2 3.3 %all-to-all-done = bf16[16,4,1,896]{3,1,2,0:T(4,128)(2,1)S(1)} async-done(((bf16[16,4,1,896]{3,1,2,0:T(4,128)(2,1)}), bf16[16,4,1,896]{3,1,2,0:T(4,128)(2,1)S(1)}, u32[]{:S(2)}, u32[]{:S(2)}) %all-to-all-start) | async-done | bytes 114720 | tf_op jit(solution)/shard_map/all_to_all | solution.py:185
  18.5 0.2 copy.39
  18.7 1.6 %collective-permute-start.1 = (bf16[4,10,896]{2,1,0:T(8,128)(2,1)S(1)}, bf16[4,10,896]{2,1,0:T(8,128)(2,1)S(1)}, u32[]{:S(2)}, u32[]{:S(2)}) collective-permute-start(bf16[4,10,896]{2,1,0:T(8,128)(2,1)S(1)} %slice_select_fusion), channel_id=1, source_target_pairs={{0,16},{16,0},{1,17},{17,1},{2,18},{18,2},{3,19},{19,3},{4,20},{20... | collective-permute-start | bytes 215048 | tf_op jit(solution)/shard_map/ppermute | solution.py:217
  20.3 0.0 collective-permute-done
  20.3 0.1 maximum_select_fusion
  20.4 0.1 copy.24
  20.5 0.7 %select_n.47.table_ref = f32[280]{0:T(512)} reshape(f32[20,14]{1,0:T(8,128)S(1)} %copy.24) | data formatting | bytes 2240 | tf_op jit(solution)/shard_map/jit(_where)/select_n | solution.py:211
  21.2 2.4 %collective-permute-done.1 = bf16[4,10,896]{2,1,0:T(8,128)(2,1)S(1)} collective-permute-done((bf16[4,10,896]{2,1,0:T(8,128)(2,1)S(1)}, bf16[4,10,896]{2,1,0:T(8,128)(2,1)S(1)}, u32[]{:S(2)}, u32[]{:S(2)}) %collective-permute-start.1) | collective-permute-done | bytes 71712 | tf_op jit(solution)/shard_map/ppermute | solution.py:217
  23.6 0.1 copy.29
  23.7 0.1 broadcast_in_dim.2
  23.8 1.8 %broadcast_select_fusion.ext_ref = bf16[4,36,1,896]{3,2,1,0:T(2,128)(2,1)} fusion(pred[]{:T(512)S(6)} %eq.3, bf16[4,10,1,896]{3,2,1,0:T(2,128)(2,1)S(1)} %copy.29, bf16[4,10,1,896]{3,2,1,0:T(2,128)(2,1)S(1)} %broadcast_in_dim.2, bf16[4,16,1,896]{3,2,1,0:T(2,128)(2,1)S(1)} %bitcast.23), kind=kLoop, calls=%fused_computation.1 | loop fusion | flops 645120 | bytes 516097 | tf_op jit(solution)/shard_map/jit(_where)/select_n | solution.py:219
  25.6 10.4 %shard_map.100 = bf16[4,16,896]{2,1,0:T(8,128)(2,1)} custom-call(f32[280]{0:T(512)} %select_n.47.table_ref, s32[2]{0:T(128)} %pad_add_fusion.bounds_ref, bf16[4,36,1,896]{3,2,1,0:T(2,128)(2,1)} %broadcast_select_fusion.ext_ref, bf16[32,16]{1,0:T(8,128)(2,1)} %pad.4.w1_ref, bf16[96,96]{1,0:T(8,128)(2,1)} %reshape.129.w2_ref, f32[32,1]{1,0:T(8,128)} %copy.33.kl_ref), custom_call_target="tpu_custom_call" | custom-call | tf_op jit(solution)/shard_map/pallas_call | solution.py:118
  (8 shorter events, 0.2 us)
Async XLA Ops:
  0.0 1.4 %copy-start = (bf16[896,896]{1,0:T(8,128)(2,1)S(1)}, bf16[896,896]{1,0:T(8,128)(2,1)}, u32[]{:S(2)}) copy-start(bf16[896,896]{1,0:T(8,128)(2,1)} %param.14) | copy-start | bytes 4816900
  0.9 9.9 %copy-start.3 = (s32[16,7]{0,1:T(8,128)S(1)}, s32[16,7]{0,1:T(8,128)}, u32[]{:S(2)}) copy-start(s32[16,7]{0,1:T(8,128)} %param.15) | copy-start | bytes 1348
  0.9 9.9 %copy-start.2 = (f32[16,7]{0,1:T(8,128)S(1)}, f32[16,7]{0,1:T(8,128)}, u32[]{:S(2)}) copy-start(f32[16,7]{0,1:T(8,128)} %param.16) | copy-start | bytes 1348
  0.9 11.5 %copy-start.5 = (bf16[32]{0:T(256)(128)(2,1)S(1)}, bf16[32]{0:T(256)(128)(2,1)}, u32[]{:S(2)}) copy-start(bf16[32]{0:T(256)(128)(2,1)} %param.19) | copy-start | bytes 196
  1.1 11.4 %copy-start.1 = (bf16[32,32,3,3]{1,0,3,2:T(8,128)(2,1)S(1)}, bf16[32,32,3,3]{1,0,3,2:T(8,128)(2,1)}, u32[]{:S(2)}) copy-start(bf16[32,32,3,3]{1,0,3,2:T(8,128)(2,1)} %param.18) | copy-start | bytes 55300
  1.1 12.1 %copy-start.4 = (bf16[32,3,3]{0,2,1:T(4,128)(2,1)S(1)}, bf16[32,3,3]{0,2,1:T(4,128)(2,1)}, u32[]{:S(2)}) copy-start(bf16[32,3,3]{0,2,1:T(4,128)(2,1)} %param.17) | copy-start | bytes 1732
  3.4 15.0 %all-to-all-start = ((bf16[16,4,1,896]{3,1,2,0:T(4,128)(2,1)}), bf16[16,4,1,896]{3,1,2,0:T(4,128)(2,1)S(1)}, u32[]{:S(2)}, u32[]{:S(2)}) async-start(bf16[16,4,1,896]{3,1,2,0:T(4,128)(2,1)} %bitcast.3), calls=%async_computation | async-start | bytes 229376 | tf_op jit(solution)/shard_map/all_to_all | solution.py:185
  10.9 9.4 %collective-permute-start = (f32[2,14]{0,1:T(8,128)S(1)}, f32[2,14]{0,1:T(8,128)S(1)}, u32[]{:S(2)}, u32[]{:S(2)}) collective-permute-start(f32[2,14]{0,1:T(8,128)S(1)} %fusion.5), channel_id=1, source_target_pairs={{0,16},{16,0},{1,17},{17,1},{2,18},{18,2},{3,19},{19,3},{4,20},{20... | collective-permute-start | bytes 344 | tf_op jit(solution)/shard_map/ppermute | solution.py:209
  18.7 4.9 %collective-permute-start.1 = (bf16[4,10,896]{2,1,0:T(8,128)(2,1)S(1)}, bf16[4,10,896]{2,1,0:T(8,128)(2,1)S(1)}, u32[]{:S(2)}, u32[]{:S(2)}) collective-permute-start(bf16[4,10,896]{2,1,0:T(8,128)(2,1)S(1)} %slice_select_fusion), channel_id=1, source_target_pairs={{0,16},{16,0},{1,17},{17,1},{2,18},{18,2},{3,19},{19,3},{4,20},{20... | collective-permute-start | bytes 215048 | tf_op jit(solution)/shard_map/ppermute | solution.py:217
